TPU v7x, 256 devices: a whole 4x4x8 slice. The times are simulated.
256 devices in a mesh: sample: 16 (over y_hi, z), variant: 16 (over y_lo, x, core).
Axes of the slice: x: 4, y: 4 (y_hi: 2, y_lo: 2; y = y_hi * 2 + y_lo), z: 8, core: 2. Of those that a mesh axis runs over, the one named last changes fastest.
Arguments:
- dosage: bfloat16 [8192, 8192], P('sample', 'variant'), may hold values from 0 to 2
- covariates: float32 [30, 8192], P(None, 'sample'), may hold values from -6 to 6
- reach: int32 [16], replicated, may hold values from 1 to 2, as said below
Outputs:
- ld_bands: bfloat16 [4, 8192, 512], P(None, ('variant', 'sample'))
Inputs may be any that keep to these rules, and one draw needn't show every extreme that they name: `reach`: every draw has a block whose band reaches 2 blocks on each side.
All inputs are finite; a program needn't handle non-finite values.
Results may differ from a plain program's by a relative error of at most 0.015.
Values may be sent and summed in bfloat16 or wider, within the bound.
No kernel may reach another device: no remote copies, remote signals or barrier semaphores. Data moves between devices by JAX's collectives and lax.ppermute only.
A program may use at most 64 MiB of HBM per device.

v0:
```python
import math

import jax
import jax.numpy as jnp
from jax import lax
from jax.sharding import PartitionSpec as P

MAXR = 2


def passed_along(block, axis, distance):
    devices = range(lax.axis_size(axis))
    route = [((i - distance) % len(devices), i) for i in devices]
    return lax.ppermute(block, axis, route)


def step_ahead(blocks):
    return passed_along(blocks, "variant", -1)


def shards(dosage, covariates, reach):
    highest = lax.Precision.HIGHEST
    local_samples = dosage.shape[0]
    samples = local_samples * lax.axis_size("sample")
    design = jnp.concatenate([jnp.ones((1, local_samples), jnp.float32), covariates], 0)
    genotype = dosage.astype(jnp.float32)
    moment_local = jnp.dot(design, design.T, precision=highest)
    cross_local = jnp.dot(design, genotype, precision=highest)
    moment, cross = lax.psum((moment_local, cross_local), "sample")
    factor = jnp.linalg.cholesky(moment)
    coefficients = jax.scipy.linalg.cho_solve((factor, True), cross)
    residual = genotype - jnp.dot(design.T, coefficients, precision=highest)
    spread = lax.psum(jnp.sum(residual * residual, 0), "sample")
    scaled = (residual * jnp.sqrt(samples / spread)).astype(jnp.bfloat16)
    own_reach = reach[lax.axis_index("variant")]
    inverse_root = 1.0 / math.sqrt(samples)

    def band_rows(other):
        partial_tile = (
            lax.dot_general(
                scaled, other, (((0,), (0,)), ((), ())), preferred_element_type=jnp.float32
            )
            * inverse_root
        )
        return lax.psum_scatter(
            partial_tile.astype(jnp.bfloat16), "sample", scatter_dimension=0, tiled=True
        ).astype(jnp.float32)

    slots = [None] * (2 * MAXR)
    ahead = scaled
    behind = scaled
    for offset in range(1, MAXR + 1):
        ahead = step_ahead(ahead)
        slots[MAXR + offset - 1] = jnp.where(offset <= own_reach, band_rows(ahead), 0.0).astype(
            jnp.bfloat16
        )
        behind = passed_along(behind, "variant", 1)
        slots[MAXR - offset] = jnp.where(offset <= own_reach, band_rows(behind), 0.0).astype(
            jnp.bfloat16
        )
    return jnp.stack(slots)


def solution(mesh):
    placed = (P("sample", "variant"), P(None, "sample"), P())
    return jax.shard_map(
        shards,
        mesh=mesh,
        in_specs=placed,
        out_specs=P(None, ("variant", "sample"), None),
        check_vma=False,
    )
```

profile of v0, /device:TPU:6, one launch (start us, length us, event | category | flops | bytes accessed | tf_op | source)
XLA Modules:
  0.0 1017.3 jit_solution(15994381289499903516)
XLA Ops:
  6.5 1.7 fusion.7
  8.3 0.0 copy-done.1
  8.3 2.1 fusion.5
  10.4 0.0 all-reduce.4.cloned.1.call-update
  10.4 0.0 reduce-scatter.9.cloned.1.call-start
  10.5 147.8 %all-reduce.4.cloned.1.call-done = (f32[31,512]{1,0:T(8,128)}, f32[31,31]{0,1:T(8,128)}) async-done(((f32[31,512]{1,0:T(8,128)}, f32[31,31]{0,1:T(8,128)}), (f32[31,512]{1,0:T(8,128)}, f32[31,31]{0,1:T(8,128)})) %all-reduce.4.cloned.1.call-update) | async-done | bytes 67348 | tf_op jit(solution)/shard_map/psum | solution.py:29
  158.3 0.9 copy.5
  159.1 0.0 copy-done.2
  159.1 2.8 cholesky.16
  162.0 0.6 compare_reduce_fusion
  162.6 0.7 fusion.13
  163.3 2.4 custom-call.10
  165.7 0.3 fusion.16
  166.0 0.2 fusion.14
  166.2 1.1 multiply_reduce_fusion
  167.3 37.8 %psum.23 = f32[512]{0:T(512)S(1)} all-reduce(f32[512]{0:T(512)S(1)} %get-tuple-element.7), channel_id=1, replica_groups=mesh['sample'=16,'variant'=16] {'sample'}, use_global_device_ids=true, to_apply=%region_5.6 | all-reduce | flops 512 | bytes 4096 | tf_op jit(solution)/shard_map/psum | solution.py:33
  205.1 0.1 multiply_convert_fusion
  205.3 0.1 collective-permute-start.2
  205.3 6.7 collective-permute-done.2
  212.0 1.3 fusion.2
  213.3 0.0 reduce-scatter.9.cloned.1.call-update
  213.3 0.0 reduce-scatter.7.cloned.1.call-start
  213.4 1.8 collective-permute-start
  215.2 7.0 collective-permute-done
  222.2 1.3 fusion.1
  223.5 0.0 reduce-scatter.7.cloned.1.call-update
  223.5 0.0 reduce-scatter.11.cloned.1.call-start
  223.6 0.1 collective-permute-start.3
  223.7 6.7 collective-permute-done.3
  230.4 1.3 fusion.3
  231.6 0.0 reduce-scatter.11.cloned.1.call-update
  231.6 0.0 reduce-scatter.5.cloned.1.call-start
  231.7 3.9 collective-permute-start.1
  235.6 5.2 collective-permute-done.1
  240.8 1.3 fusion
  242.1 0.0 reduce-scatter.5.cloned.1.call-update
  242.1 0.0 copy-start.4
  242.2 0.6 copy-done.4
  242.8 0.6 dynamic_slice.3
  244.7 166.9 %reduce-scatter.9.cloned.1.call-done = bf16[32,512]{1,0:T(8,128)(2,1)} async-done(((bf16[512,512]{1,0:T(8,128)(2,1)}), bf16[32,512]{1,0:T(8,128)(2,1)}) %reduce-scatter.9.cloned.1.call-update) | async-done | bytes 32784 | tf_op jit(solution)/shard_map/reduce_scatter | solution.py:45
  411.6 0.8 fusion.11
  412.3 198.4 %reduce-scatter.7.cloned.1.call-done = bf16[32,512]{1,0:T(8,128)(2,1)} async-done(((bf16[512,512]{1,0:T(8,128)(2,1)}), bf16[32,512]{1,0:T(8,128)(2,1)}) %reduce-scatter.7.cloned.1.call-update) | async-done | bytes 32784 | tf_op jit(solution)/shard_map/reduce_scatter | solution.py:45
  610.7 0.8 fusion.10
  611.5 198.8 %reduce-scatter.11.cloned.1.call-done = bf16[32,512]{1,0:T(8,128)(2,1)} async-done(((bf16[512,512]{1,0:T(8,128)(2,1)}), bf16[32,512]{1,0:T(8,128)(2,1)}) %reduce-scatter.11.cloned.1.call-update) | async-done | bytes 32784 | tf_op jit(solution)/shard_map/reduce_scatter | solution.py:45
  810.3 0.8 fusion.12
  811.0 198.3 %reduce-scatter.5.cloned.1.call-done = bf16[32,512]{1,0:T(8,128)(2,1)} async-done(((bf16[512,512]{1,0:T(8,128)(2,1)}), bf16[32,512]{1,0:T(8,128)(2,1)}) %reduce-scatter.5.cloned.1.call-update) | async-done | bytes 32784 | tf_op jit(solution)/shard_map/reduce_scatter | solution.py:45
  1009.3 0.8 fusion.9
  1010.1 0.7 pad_maximum_fusion
  (10 shorter events, 0.1 us)
Async XLA Ops:
  6.5 1.7 copy-start.1
  6.5 151.7 %all-reduce.4.cloned.1.call-start = ((), (), s32[]{:S(2)}) async-start(), calls=%async_computation.8 | async-start | bytes 163840 | tf_op jit(solution)/shard_map/psum | solution.py:29
  8.3 157.9 %copy-start = (bf16[512,512]{1,0:T(8,128)(2,1)S(1)}, bf16[512,512]{1,0:T(8,128)(2,1)}, u32[]{:S(2)}) copy-start(bf16[512,512]{1,0:T(8,128)(2,1)} %param.3) | copy-start | bytes 1572868
  10.4 401.2 %reduce-scatter.9.cloned.1.call-start = ((), (), s32[]{:S(2)}) async-start(), calls=%async_computation.6 | async-start | bytes 557056 | tf_op jit(solution)/shard_map/reduce_scatter | solution.py:45
  158.3 0.9 copy-start.2
  158.3 7.4 copy-start.3
  205.3 6.8 collective-permute-start.2
  213.3 397.4 %reduce-scatter.7.cloned.1.call-start = ((), (), s32[]{:S(2)}) async-start(), calls=%async_computation.5 | async-start | bytes 557056 | tf_op jit(solution)/shard_map/reduce_scatter | solution.py:45
  213.4 8.9 collective-permute-start
  223.5 586.7 %reduce-scatter.11.cloned.1.call-start = ((), (), s32[]{:S(2)}) async-start(), calls=%async_computation.7 | async-start | bytes 557056 | tf_op jit(solution)/shard_map/reduce_scatter | solution.py:45
  223.6 6.8 collective-permute-start.3
  231.6 777.7 %reduce-scatter.5.cloned.1.call-start = ((), (), s32[]{:S(2)}) async-start(), calls=%async_computation.4 | async-start | bytes 557056 | tf_op jit(solution)/shard_map/reduce_scatter | solution.py:45
  231.7 9.1 collective-permute-start.1
  242.1 0.7 copy-start.4
Sparse Core Ops, SparseCore 0:
  10.5 147.6 all-reduce.3
  213.5 198.0 reduce-scatter.8
  415.4 195.2 reduce-scatter.6
  614.9 195.3 reduce-scatter.10
  813.9 195.3 reduce-scatter.4
where the time goes:
time: 1020 us
  waiting for transfers between devices  936 us (92%)
  blocking collectives  37.8 us (4%)
  between operations  14.5 us (1%)
  matrix products  10.5 us (1%)
  other arithmetic  10.4 us (1%)
    reduce_scatter x4, waiting for transfers between devices, band_rows(): lax.psum_scatter(partial_tile.astype(jnp.bfloat16), 'sample', scatter_dim...  762 us
    psum x1, waiting for transfers between devices, shards(): moment, cross = lax.psum((moment_local, cross_local), 'sample')  148 us
    psum x1, blocking collectives, shards(): spread = lax.psum(jnp.sum(residual * residual, 0), 'sample')  37.8 us
    ppermute x4, waiting for transfers between devices, passed_along(): return lax.ppermute(block, axis, route)  25.6 us
  transfers between devices with their start and end apart: 9, of which 9 were waited for; matrix products, arithmetic and copies ran while one was open for 1% of the time, Pallas kernels for 0%

commit v1 on v0

v1 whole, which is shorter than its diff:
```python
import math

import jax
import jax.numpy as jnp
from jax import lax
from jax.sharding import PartitionSpec as P

MAXR = 2
HIGHEST = lax.Precision.HIGHEST


def exchange(x):
    return lax.all_to_all(x, "sample", 0, 0, tiled=False)


def neighbours(block, core):
    count = lax.axis_size("variant")
    devices = range(count)
    up = lax.ppermute(block, "variant", [((i + 2) % count, i) for i in devices])
    down = lax.ppermute(block, "variant", [((i - 2) % count, i) for i in devices])
    swap = [(i, i ^ 1) for i in devices]
    mate = lax.ppermute(block, "variant", swap)
    other = lax.ppermute(jnp.where(core == 0, up, down), "variant", swap)
    after = jnp.where(core == 0, mate, other)
    before = jnp.where(core == 0, other, mate)
    return [down, before, after, up]


def shards(dosage, covariates, reach):
    local_samples, width = dosage.shape
    parts = lax.axis_size("sample")
    samples = local_samples * parts
    core = lax.axis_index("variant") % 2
    rows = covariates.shape[0] + 1
    padded = -(-rows // parts) * parts
    blank = jnp.zeros((padded - rows, local_samples), jnp.float32)
    design = jnp.concatenate([jnp.ones((1, local_samples), jnp.float32), covariates, blank], 0)

    def sums(block):
        return jnp.dot(design, block.astype(jnp.float32), precision=HIGHEST)

    moment_local = jnp.dot(design, design.T, precision=HIGHEST)
    local = jnp.concatenate([sums(dosage), moment_local], 1)
    around = neighbours(dosage, core)
    chunk = exchange(local.reshape(parts, padded // parts, -1)).sum(0)
    total = exchange(jnp.broadcast_to(chunk[None], (parts,) + chunk.shape)).reshape(padded, -1)
    cross = total[:, :width]
    moment = total[:rows, width : width + rows]
    crosses = neighbours(cross, core)
    factor = jnp.linalg.cholesky(moment)
    inverse = jax.scipy.linalg.solve_triangular(factor, jnp.eye(rows, dtype=jnp.float32), lower=True)

    def residual(block, cross):
        half = jnp.dot(inverse, cross[:rows], precision=HIGHEST)
        coefficients = jnp.dot(inverse.T, half, precision=HIGHEST)
        left = block.astype(jnp.float32) - jnp.dot(design[:rows].T, coefficients, precision=HIGHEST)
        spread = jnp.sum(left * left, 0)
        high = spread.astype(jnp.bfloat16)
        low = (spread - high.astype(jnp.float32)).astype(jnp.bfloat16)
        return left.astype(jnp.bfloat16), jnp.stack([high, low])

    own, own_spread = residual(dosage, cross)
    tiles, spreads = [], [own_spread]
    for block, cross in zip(around, crosses):
        other, spread = residual(block, cross)
        spreads.append(spread)
        tile = lax.dot_general(own, other, (((0,), (0,)), ((), ())), preferred_element_type=jnp.float32)
        tiles.append(tile.astype(jnp.bfloat16).reshape(parts, width // parts, width))
    spreads = jnp.concatenate(spreads, 0)
    spreads = jnp.pad(spreads, ((0, 6), (0, 0)))
    message = jnp.concatenate(tiles + [jnp.broadcast_to(spreads[None], (parts,) + spreads.shape)], 1)
    arrived = exchange(message)
    whole = arrived.astype(jnp.float32).sum(0)
    share = width // parts
    bands = whole[: 2 * MAXR * share].reshape(2 * MAXR, share, width)
    spread = whole[2 * MAXR * share :]
    spread = spread[0:10:2] + spread[1:10:2]
    weight = jnp.sqrt(samples / spread)
    own_weight = lax.dynamic_slice(weight[0], (lax.axis_index("sample") * share,), (share,))
    own_reach = reach[lax.axis_index("variant")]
    offsets = jnp.array([2, 1, 1, 2], jnp.int32)
    scaled = bands * own_weight[None, :, None] * weight[1:][:, None, :] * (1.0 / math.sqrt(samples))
    return jnp.where((offsets <= own_reach)[:, None, None], scaled, 0.0).astype(jnp.bfloat16)


def solution(mesh):
    placed = (P("sample", "variant"), P(None, "sample"), P())
    return jax.shard_map(
        shards,
        mesh=mesh,
        in_specs=placed,
        out_specs=P(None, ("variant", "sample"), None),
        check_vma=False,
    )
```

time: 1020 us -> 136 us (0.13)
  waiting for transfers between devices: 936 us -> 65.7 us
  blocking collectives: 37.8 us -> 21 us
  between operations: 14.5 us -> 0.44 us
  starting transfers between devices: 6.08 us -> 18.8 us
    reduce_scatter x4 -> x0, waiting for transfers between devices: 762 us -> none  [band_rows(): lax.psum_scatter(partial_tile.astype(jnp.bfloat16), 'sample', scatter_dim...]
    psum x1 -> x0, waiting for transfers between devices: 148 us -> none  [shards(): moment, cross = lax.psum((moment_local, cross_local), 'sample')]
    all_to_all x0 -> x2, waiting for transfers between devices: none -> 63.5 us  [exchange(): return lax.all_to_all(x, 'sample', 0, 0, tiled=False)]
    psum x1 -> x0, blocking collectives: 37.8 us -> none  [shards(): spread = lax.psum(jnp.sum(residual * residual, 0), 'sample')]
    ppermute x4 -> x8, waiting for transfers between devices: 25.6 us -> 2.23 us  [the longest x2 1.45 us: neighbours(): lax.ppermute(block, 'variant', [((i - 2) % count, i) for i in devices])]
    all_to_all x0 -> x1, blocking collectives: none -> 21 us  [exchange(): return lax.all_to_all(x, 'sample', 0, 0, tiled=False)]
    all_to_all x0 -> x2, starting transfers between devices: none -> 11.8 us  [exchange(): return lax.all_to_all(x, 'sample', 0, 0, tiled=False)]
  transfers between devices with their start and end apart: 9 -> 10, of which waited for: 9 -> 4; matrix products, arithmetic and copies ran while one was open for 1% -> 12% of each run, Pallas kernels for 0% -> 0%
where the time goes in v1:
time: 136 us
  waiting for transfers between devices  65.7 us (48%)
  blocking collectives  21 us (15%)
  starting transfers between devices  18.8 us (14%)
  matrix products  14.9 us (11%)
  other arithmetic  8.43 us (6%)
  local copies, waits for them, and re-layouts  6.79 us (5%)
    all_to_all x2, waiting for transfers between devices, exchange(): return lax.all_to_all(x, 'sample', 0, 0, tiled=False)  63.5 us
    all_to_all x1, blocking collectives, exchange(): return lax.all_to_all(x, 'sample', 0, 0, tiled=False)  21 us
    all_to_all x2, starting transfers between devices, exchange(): return lax.all_to_all(x, 'sample', 0, 0, tiled=False)  11.8 us
    dot_general x5, matrix products, residual(): jnp.dot(design[:rows].T, coefficients, precision=HIGHEST)  6.67 us
    unnamed x19, local copies, waits for them, and re-layouts  4.39 us
    ppermute x2, starting transfers between devices, neighbours(): lax.ppermute(block, 'variant', [((i - 2) % count, i) for i in devices])  4.15 us
    another operation x3, other arithmetic, shards(): factor = jnp.linalg.cholesky(moment)  3.5 us
    dot_general x4, matrix products, shards(): lax.dot_general(own, other, (((0,), (0,)), ((), ())), preferred_element_t...  3.06 us
  transfers between devices with their start and end apart: 10, of which 4 were waited for; matrix products, arithmetic and copies ran while one was open for 12% of the time, Pallas kernels for 0%

profile of v1, /device:TPU:6, one launch (start us, length us, event | category | flops | bytes accessed | tf_op | source)
XLA Modules:
  0.0 136.0 jit_solution(14887196308966238900)
XLA Ops:
  0.1 1.2 fusion.22
  1.3 1.5 %fusion.23 = f32[32,512]{1,0:T(8,128)S(1)} fusion(bf16[512,512]{1,0:T(8,128)(2,1)} %param.4, f32[30,512]{1,0:T(8,128)} %param.5, f32[32]{0:T(128)S(1)} %pad.10.clone, f32[32]{0:T(128)S(1)} %pad.8.clone), kind=kOutput, calls=%fused_computation.41 | convolution fusion | flops 100696064 | bytes 651520 | tf_op jit(solution)/shard_map/dot_general | solution.py:40
  2.9 21.0 %all_to_all.15 = f32[16,2,544]{2,1,0:T(2,128)S(1)} all-to-all(f32[16,2,544]{2,1,0:T(2,128)S(1)} %reshape.138), channel_id=1, replica_groups=mesh['sample'=16,'variant'=16] {'sample'}, dimensions={0} | all-to-all | bytes 139264 | tf_op jit(solution)/shard_map/all_to_all | solution.py:13
  23.9 0.7 broadcast_in_dim.38
  24.6 3.5 %all-to-all-start.1 = ((f32[16,2,544]{2,1,0:T(2,128)}), f32[16,2,544]{2,1,0:T(2,128)S(1)}, u32[]{:S(2)}, u32[]{:S(2)}) async-start(f32[16,2,544]{2,1,0:T(2,128)} %broadcast_in_dim.38), calls=%async_computation.1 | async-start | bytes 163840 | tf_op jit(solution)/shard_map/all_to_all | solution.py:13
  28.1 0.7 collective-permute-start
  28.8 1.4 %collective-permute-start.2 = (bf16[512,512]{1,0:T(8,128)(2,1)}, bf16[512,512]{1,0:T(8,128)(2,1)S(1)}, u32[]{:S(2)}, u32[]{:S(2)}) collective-permute-start(bf16[512,512]{1,0:T(8,128)(2,1)} %param.4), channel_id=1, source_target_pairs={{2,0},{3,1},{4,2},{5,3},{6,4},{7,5},{8,6},{9,7},{10,8},{11,9},{12,... | collective-permute-start | bytes 1572872 | tf_op jit(solution)/shard_map/ppermute | solution.py:19
  30.2 8.0 %all-to-all-done.1 = f32[16,2,544]{2,1,0:T(2,128)S(1)} async-done(((f32[16,2,544]{2,1,0:T(2,128)}), f32[16,2,544]{2,1,0:T(2,128)S(1)}, u32[]{:S(2)}, u32[]{:S(2)}) %all-to-all-start.1) | async-done | bytes 69664 | tf_op jit(solution)/shard_map/all_to_all | solution.py:13
  38.4 0.8 collective-permute-start.5
  39.3 2.8 %cholesky.17 = f32[31,31]{1,0:T(8,128)S(1)} custom-call(f32[31,31]{1,0:T(8,128)S(1)} %fusion.42), custom_call_target="Cholesky" | custom-call | tf_op jit(solution)/shard_map/jit(cholesky)/cholesky | solution.py:50
  42.2 0.6 compare_reduce_fusion
  42.8 0.7 fusion.39
  43.5 2.4 %custom-call.7 = f32[1,31,31]{1,2,0:T(8,128)S(1)} custom-call(f32[1,31,31]{2,1,0:T(8,128)S(1)} %fusion.39), custom_call_target="InvertDiagBlocksLowerTriangular" | custom-call | tf_op jit(solution)/shard_map/jit(_solve_triangular)/triangular_solve | solution.py:51
  45.8 0.2 fusion.40
  46.0 0.2 fusion.12
  46.3 0.3 fusion.50
  46.5 1.1 multiply_reduce_fusion.4
  47.7 3.5 %collective-permute-start.1 = (f32[32,512]{1,0:T(8,128)S(1)}, f32[32,512]{1,0:T(8,128)S(1)}, u32[]{:S(2)}, u32[]{:S(2)}) collective-permute-start(f32[32,512]{1,0:T(8,128)S(1)} %slice.73), channel_id=1, source_target_pairs={{14,0},{15,1},{0,2},{1,3},{2,4},{3,5},{4,6},{5,7},{6,8},{7,9},{8,1... | collective-permute-start | bytes 196616 | tf_op jit(solution)/shard_map/ppermute | solution.py:20
  51.2 0.2 fusion.8
  51.4 0.3 fusion.54
  51.6 1.4 %collective-permute-done.1 = f32[32,512]{1,0:T(8,128)S(1)} collective-permute-done((f32[32,512]{1,0:T(8,128)S(1)}, f32[32,512]{1,0:T(8,128)S(1)}, u32[]{:S(2)}, u32[]{:S(2)}) %collective-permute-start.1) | collective-permute-done | bytes 65568 | tf_op jit(solution)/shard_map/ppermute | solution.py:20
  53.4 0.3 fusion.51
  53.7 0.8 collective-permute-done.6
  54.4 0.2 fusion.14
  54.7 0.2 fusion.16
  54.9 0.3 fusion.52
  55.1 0.3 fusion.53
  55.4 1.0 fusion.28
  56.5 0.4 collective-permute-start.3
  56.9 1.1 multiply_reduce_fusion.3
  58.1 0.5 convolution_convert_fusion.3
  58.5 1.1 multiply_reduce_fusion
  59.7 0.9 constant_dynamic-update-slice_fusion.3
  60.6 0.5 convolution_convert_fusion
  61.1 0.8 copy-done
  61.9 2.3 %multiply_reduce_fusion.1 = (f32[512]{0:T(512)S(1)}, f32[512]{0:T(512)S(1)}, f32[512,512]{1,0:T(8,128)}) fusion(bf16[512,512]{1,0:T(8,128)(2,1)S(1)} %collective-permute-done.4, bf16[512,512]{1,0:T(8,128)(2,1)S(1)} %collective-permute-done.3, pred[]{:T(512)S(6)} %eq.4, f32[512,512]{1,0:T(8,128)S(1)} %fusion.28, f32[31,512]{1,0:T(8,128)S(1)} %fusion.53, ...), kind=kOutput, calls=%fused_computation.7 | convolution fusion | flops 100137984 | bytes 3274753 | tf_op jit(solution)/shard_map/dot_general | solution.py:56
  64.2 1.6 %convolution_convert_fusion.2 = bf16[512,512]{1,0:T(8,128)(2,1)S(1)} fusion(bf16[512,512]{1,0:T(8,128)(2,1)S(1)} %get-tuple-element.8, f32[512,512]{1,0:T(8,128)S(1)} %fusion.28, bf16[512,512]{1,0:T(8,128)(2,1)} %copy-done, bf16[512,512]{1,0:T(8,128)(2,1)S(1)} %collective-permute-done.4, pred[]{:T(512)S(6)} %eq.4), kind=kOutput, calls=%fused_computation.4 | convolution fusion | flops 269746176 | bytes 3145729 | tf_op jit(solution)/shard_map/dot_general | solution.py:67
  65.9 0.9 constant_dynamic-update-slice_fusion.2
  66.7 0.5 convolution_convert_fusion.1
  67.2 0.9 constant_dynamic-update-slice_fusion.1
  68.1 0.9 constant_dynamic-update-slice_fusion
  69.0 0.7 broadcast_dynamic-update-slice_fusion
  69.8 8.3 %all-to-all-start.2 = ((bf16[16,144,512]{2,1,0:T(8,128)(2,1)}), bf16[16,144,512]{2,1,0:T(8,128)(2,1)S(1)}, u32[]{:S(2)}, u32[]{:S(2)}) async-start(bf16[16,144,512]{2,1,0:T(8,128)(2,1)} %broadcast_dynamic-update-slice_fusion), calls=%async_computation.2 | async-start | bytes 4718592 | tf_op jit(solution)/shard_map/all_to_all | solution.py:13
  78.0 0.6 dynamic_slice.6
  78.6 0.6 broadcast_compare_fusion
  79.3 55.5 %all-to-all-done.2 = bf16[16,144,512]{2,1,0:T(8,128)(2,1)S(1)} async-done(((bf16[16,144,512]{2,1,0:T(8,128)(2,1)}), bf16[16,144,512]{2,1,0:T(8,128)(2,1)S(1)}, u32[]{:S(2)}, u32[]{:S(2)}) %all-to-all-start.2) | async-done | bytes 2359328 | tf_op jit(solution)/shard_map/all_to_all | solution.py:13
  134.7 0.3 convert_reduce_fusion
  135.3 0.8 select_convert_fusion
  (54 shorter events, 1.1 us)
Async XLA Ops:
  0.0 46.5 %copy-start.3 = (f32[30,512]{1,0:T(8,128)S(1)}, f32[30,512]{1,0:T(8,128)}, u32[]{:S(2)}) copy-start(f32[30,512]{1,0:T(8,128)} %param.5) | copy-start | bytes 184324
  0.0 46.5 %copy-start.4 = (bf16[512,512]{1,0:T(8,128)(2,1)S(1)}, bf16[512,512]{1,0:T(8,128)(2,1)}, u32[]{:S(2)}) copy-start(bf16[512,512]{1,0:T(8,128)(2,1)} %param.4) | copy-start | bytes 1572868
  24.6 13.6 %all-to-all-start.1 = ((f32[16,2,544]{2,1,0:T(2,128)}), f32[16,2,544]{2,1,0:T(2,128)S(1)}, u32[]{:S(2)}, u32[]{:S(2)}) async-start(f32[16,2,544]{2,1,0:T(2,128)} %broadcast_in_dim.38), calls=%async_computation.1 | async-start | bytes 163840 | tf_op jit(solution)/shard_map/all_to_all | solution.py:13
  28.1 28.3 %collective-permute-start = (bf16[512,512]{1,0:T(8,128)(2,1)}, bf16[512,512]{1,0:T(8,128)(2,1)S(1)}, u32[]{:S(2)}, u32[]{:S(2)}) collective-permute-start(bf16[512,512]{1,0:T(8,128)(2,1)} %param.4), channel_id=1, source_target_pairs={{14,0},{15,1},{0,2},{1,3},{2,4},{3,5},{4,6},{5,7},{6,8},{7,9},{8,1... | collective-permute-start | bytes 1572872 | tf_op jit(solution)/shard_map/ppermute | solution.py:20
  28.8 32.3 %collective-permute-start.4 = (bf16[512,512]{1,0:T(8,128)(2,1)}, bf16[512,512]{1,0:T(8,128)(2,1)S(1)}, u32[]{:S(2)}, u32[]{:S(2)}) collective-permute-start(bf16[512,512]{1,0:T(8,128)(2,1)} %param.4), channel_id=1, source_target_pairs={{0,1},{1,0},{2,3},{3,2},{4,5},{5,4},{6,7},{7,6},{8,9},{9,8},{10,11... | collective-permute-start | bytes 1572872 | tf_op jit(solution)/shard_map/ppermute | solution.py:22
  28.8 27.7 %collective-permute-start.2 = (bf16[512,512]{1,0:T(8,128)(2,1)}, bf16[512,512]{1,0:T(8,128)(2,1)S(1)}, u32[]{:S(2)}, u32[]{:S(2)}) collective-permute-start(bf16[512,512]{1,0:T(8,128)(2,1)} %param.4), channel_id=1, source_target_pairs={{2,0},{3,1},{4,2},{5,3},{6,4},{7,5},{8,6},{9,7},{10,8},{11,9},{12,... | collective-permute-start | bytes 1572872 | tf_op jit(solution)/shard_map/ppermute | solution.py:19
  38.3 15.4 %collective-permute-start.7 = (f32[32,512]{1,0:T(8,128)S(1)}, f32[32,512]{1,0:T(8,128)S(1)}, u32[]{:S(2)}, u32[]{:S(2)}) collective-permute-start(f32[32,512]{1,0:T(8,128)S(1)} %slice.73), channel_id=1, source_target_pairs={{0,1},{1,0},{2,3},{3,2},{4,5},{5,4},{6,7},{7,6},{8,9},{9,8},{10,11... | collective-permute-start | bytes 196616 | tf_op jit(solution)/shard_map/ppermute | solution.py:22
  38.4 9.3 %collective-permute-start.5 = (f32[32,512]{1,0:T(8,128)S(1)}, f32[32,512]{1,0:T(8,128)S(1)}, u32[]{:S(2)}, u32[]{:S(2)}) collective-permute-start(f32[32,512]{1,0:T(8,128)S(1)} %slice.73), channel_id=1, source_target_pairs={{2,0},{3,1},{4,2},{5,3},{6,4},{7,5},{8,6},{9,7},{10,8},{11,9},{12,... | collective-permute-start | bytes 196616 | tf_op jit(solution)/shard_map/ppermute | solution.py:19
  47.7 5.4 %collective-permute-start.1 = (f32[32,512]{1,0:T(8,128)S(1)}, f32[32,512]{1,0:T(8,128)S(1)}, u32[]{:S(2)}, u32[]{:S(2)}) collective-permute-start(f32[32,512]{1,0:T(8,128)S(1)} %slice.73), channel_id=1, source_target_pairs={{14,0},{15,1},{0,2},{1,3},{2,4},{3,5},{4,6},{5,7},{6,8},{7,9},{8,1... | collective-permute-start | bytes 196616 | tf_op jit(solution)/shard_map/ppermute | solution.py:20
  53.1 1.3 collective-permute-start.6
  56.5 4.5 %collective-permute-start.3 = (bf16[512,512]{1,0:T(8,128)(2,1)S(1)}, bf16[512,512]{1,0:T(8,128)(2,1)S(1)}, u32[]{:S(2)}, u32[]{:S(2)}) collective-permute-start(bf16[512,512]{1,0:T(8,128)(2,1)S(1)} %broadcast_select_fusion.2), channel_id=1, source_target_pairs={{0,1},{1,0},{2,3},{3,2},{4,5},{5,4},{6,7},{7,6},{8,9},{9,8},{10,11... | collective-permute-start | bytes 1572872 | tf_op jit(solution)/shard_map/ppermute | solution.py:23
  61.1 0.8 copy-start
  64.1 2.6 %copy-start.1 = (bf16[512,512]{1,0:T(8,128)(2,1)S(1)}, bf16[512,512]{1,0:T(8,128)(2,1)}, u32[]{:S(2)}) copy-start(bf16[512,512]{1,0:T(8,128)(2,1)} %copy-done) | copy-start | bytes 1572868
  64.2 2.5 %copy-start.2 = (f32[512,512]{1,0:T(8,128)S(1)}, f32[512,512]{1,0:T(8,128)}, u32[]{:S(2)}) copy-start(f32[512,512]{1,0:T(8,128)} %get-tuple-element.12) | copy-start | bytes 3145732
  69.8 8.3 %copy-start.5 = (s32[16]{0:T(128)S(1)}, s32[16]{0:T(128)}, u32[]{:S(2)}) copy-start(s32[16]{0:T(128)} %param.6) | copy-start | bytes 196
  69.8 8.9 %copy-start.6 = (s32[4]{0:T(128)S(1)}, s32[4]{0:T(128)}, u32[]{:S(2)}) copy-start(s32[4]{0:T(128)} %constant.83.clone) | copy-start | bytes 52
  69.8 65.0 %all-to-all-start.2 = ((bf16[16,144,512]{2,1,0:T(8,128)(2,1)}), bf16[16,144,512]{2,1,0:T(8,128)(2,1)S(1)}, u32[]{:S(2)}, u32[]{:S(2)}) async-start(bf16[16,144,512]{2,1,0:T(8,128)(2,1)} %broadcast_dynamic-update-slice_fusion), calls=%async_computation.2 | async-start | bytes 4718592 | tf_op jit(solution)/shard_map/all_to_all | solution.py:13

commit v2 on v1

v2 whole, which is shorter than its diff:
```python
import math

import jax
import jax.numpy as jnp
from jax import lax
from jax.experimental import pallas as pl
from jax.experimental.pallas import tpu as pltpu
from jax.sharding import PartitionSpec as P

MAXR = 2
HIGHEST = lax.Precision.HIGHEST
BF16 = jnp.bfloat16
F32 = jnp.float32
LANES = 128
STEP = 128
COLUMNS_TOGETHER = (((0,), (0,)), ((), ()))


def split(value):
    high = value.astype(BF16)
    rest = value - high.astype(F32)
    middle = rest.astype(BF16)
    low = (rest - middle.astype(F32)).astype(BF16)
    return high, middle, low


def fill_design(design_ref, covariates_ref):
    count = covariates_ref.shape[0]
    design_ref[...] = jnp.zeros_like(design_ref)
    design_ref[:count, :] = covariates_ref[...]
    design_ref[count : count + 1, :] = jnp.ones((1, design_ref.shape[1]), F32)


def sums_kernel(dosage_ref, covariates_ref, out_ref, design_ref):
    fill_design(design_ref, covariates_ref)
    width = dosage_ref.shape[1]
    padded = design_ref.shape[0]
    design = design_ref[...]
    stacked = jnp.concatenate(split(design), 0)
    parts = jnp.dot(stacked, dosage_ref[...], preferred_element_type=F32)
    out_ref[:, :width] = parts[:padded] + parts[padded : 2 * padded] + parts[2 * padded :]
    moment = lax.dot_general(
        design, design, (((1,), (1,)), ((), ())), precision=HIGHEST, preferred_element_type=F32
    )
    out_ref[:, width:] = jnp.concatenate(
        [moment, jnp.zeros((padded, out_ref.shape[1] - width - padded), F32)], 1
    )


def local_sums(dosage, covariates, padded):
    samples, width = dosage.shape
    return pl.pallas_call(
        sums_kernel,
        out_shape=jax.ShapeDtypeStruct((padded, width + LANES), F32),
        scratch_shapes=[pltpu.VMEM((padded, samples), F32)],
        name="local_sums",
    )(dosage, covariates)


def tiles_kernel(
    own0, own1, far0, far1, near0, near1, cov0, cov1, cross_own, cross_far, cross_near, inverse,
    out_ref, design, left, right,
):
    samples, width = own0.shape
    parts = out_ref.shape[0]
    share = width // parts
    fill_design(design.at[:, :samples], cov0)
    fill_design(design.at[:, samples:], cov1)
    factor = inverse[...]
    h, m, l = split(jnp.dot(factor, design[...], precision=HIGHEST, preferred_element_type=F32))
    white = jnp.concatenate([h, h, m, h, l, m], 0)

    def residual(pieces, cross, target):
        h, m, l = split(jnp.dot(factor, cross[...], precision=HIGHEST, preferred_element_type=F32))
        stacked = jnp.concatenate([h, m, h, l, h, m], 0)
        spread = jnp.zeros((1, width), F32)
        for index, piece in enumerate(pieces):
            for start in range(0, samples, STEP):
                at = index * samples + start
                fitted = lax.dot_general(
                    white[:, at : at + STEP], stacked, COLUMNS_TOGETHER, preferred_element_type=F32
                )
                rest = piece[start : start + STEP, :].astype(F32) - fitted
                spread = spread + jnp.sum(rest * rest, 0, keepdims=True)
                target[at : at + STEP, :] = rest.astype(BF16)
        high = spread.astype(BF16)
        low = (spread - high.astype(F32)).astype(BF16)
        return [high, low]

    rows = residual((own0, own1), cross_own, left)
    for slot, (pieces, cross) in enumerate((((far0, far1), cross_far), ((near0, near1), cross_near))):
        rows += residual(pieces, cross, right)
        tile = lax.dot_general(left[...], right[...], COLUMNS_TOGETHER, preferred_element_type=F32)
        tile = tile.astype(BF16)
        for part in range(parts):
            out_ref[part, slot * share : (slot + 1) * share, :] = tile[part * share : (part + 1) * share]
    rows.append(jnp.zeros((8 - len(rows), width), BF16))
    rows = jnp.concatenate(rows, 0)
    for part in range(parts):
        out_ref[part, 2 * share :, :] = rows


def tiles(pieces, designs, crosses, inverse, parts):
    samples, width = pieces[0].shape
    padded = inverse.shape[0]
    return pl.pallas_call(
        tiles_kernel,
        out_shape=jax.ShapeDtypeStruct((parts, 2 * (width // parts) + 8, width), BF16),
        scratch_shapes=[
            pltpu.VMEM((padded, 2 * samples), F32),
            pltpu.VMEM((2 * samples, width), BF16),
            pltpu.VMEM((2 * samples, width), BF16),
        ],
        compiler_params=pltpu.CompilerParams(vmem_limit_bytes=40 << 20),
        name="tiles",
    )(*pieces, *designs, *crosses, inverse)


def exchange(x):
    return lax.all_to_all(x, "sample", 0, 0, tiled=False)


def shards(dosage, covariates, reach):
    local_samples, width = dosage.shape
    parts = lax.axis_size("sample")
    blocks = lax.axis_size("variant")
    half = parts // 2
    samples = local_samples * parts
    place = lax.axis_index("sample")
    core = lax.axis_index("variant") % 2
    side = place // half
    rows = covariates.shape[0] + 1
    padded = -(-rows // parts) * parts
    both = ("sample", "variant")

    partner_route = [(i, i ^ half) for i in range(parts)]
    core_route = [(i, i ^ 1) for i in range(blocks)]
    far_route = []
    for s in range(parts):
        step = MAXR if s < half else -MAXR
        for v in range(blocks):
            far_route.append((s * blocks + (v + step) % blocks, s * blocks + v))

    def from_partner(x):
        return lax.ppermute(x, "sample", partner_route)

    def from_far(x):
        return lax.ppermute(x, both, far_route)

    def from_near(own, far):
        return lax.ppermute(jnp.where(core != side, own, far), "variant", core_route)

    own0 = dosage
    far0 = from_far(own0)
    own1 = from_partner(own0)
    covariates1 = from_partner(covariates)
    local = local_sums(dosage, covariates, padded)
    chunk = exchange(local.reshape(parts, padded // parts, -1)).sum(0)
    far1 = from_far(own1)
    near0 = from_near(own0, far0)
    total = exchange(jnp.broadcast_to(chunk[None], (parts,) + chunk.shape)).reshape(padded, -1)
    near1 = from_near(own1, far1)
    cross = total[:, :width]
    cross_far = from_far(cross)
    cross_near = from_near(cross, cross_far)
    moment = total[:rows, width : width + rows]
    factor = jnp.linalg.cholesky(moment)
    inverse = jax.scipy.linalg.solve_triangular(factor, jnp.eye(rows, dtype=F32), lower=True)
    inverse = jnp.pad(inverse, ((0, padded - rows), (0, padded - rows)))
    message = tiles(
        (own0, own1, far0, far1, near0, near1),
        (covariates, covariates1),
        (cross, cross_far, cross_near),
        inverse,
        parts,
    )
    share = width // parts
    arrived = exchange(message).reshape(2, half, 2 * share + 8, width)
    whole = arrived.astype(F32).sum(1)
    far, near = whole[:, :share], whole[:, share : 2 * share]
    bands = jnp.stack([far[1], near[1], near[0], far[0]])
    spread = whole[:, 2 * share : 2 * share + 6 : 2] + whole[:, 2 * share + 1 : 2 * share + 6 : 2]
    weight = jnp.sqrt(samples / spread)
    columns = jnp.stack([weight[1, 1], weight[1, 2], weight[0, 2], weight[0, 1]])
    own_weight = lax.dynamic_slice(weight[0, 0], (place * share,), (share,))
    own_reach = reach[lax.axis_index("variant")]
    offsets = jnp.array([2, 1, 1, 2], jnp.int32)
    scaled = bands * own_weight[None, :, None] * columns[:, None, :] * (1.0 / math.sqrt(samples))
    return jnp.where((offsets <= own_reach)[:, None, None], scaled, 0.0).astype(BF16)


def solution(mesh):
    placed = (P("sample", "variant"), P(None, "sample"), P())
    return jax.shard_map(
        shards,
        mesh=mesh,
        in_specs=placed,
        out_specs=P(None, ("variant", "sample"), None),
        check_vma=False,
    )
```

time: 136 us -> 114 us (0.84)
  matrix products: 14.9 us -> 0.19 us
  waiting for transfers between devices: 65.7 us -> 58.6 us
  Pallas kernels: 0 us -> 5.98 us
  local copies, waits for them, and re-layouts: 6.79 us -> 2.52 us
  blocking collectives: 21 us -> 18.4 us
  other arithmetic: 8.43 us -> 9.89 us
    all_to_all x2, waiting for transfers between devices: 63.5 us -> 36.1 us  [exchange(): return lax.all_to_all(x, 'sample', 0, 0, tiled=False)]
    ppermute x8, waiting for transfers between devices: 2.23 us -> 22.4 us  [the longest x3 21.7 us: from_far(): return lax.ppermute(x, both, far_route)]
    dot_general x21 -> x0, matrix products: 14.7 us -> none  [the longest x5 6.67 us: residual(): jnp.dot(design[:rows].T, coefficients, precision=HIGHEST)]
    pallas_call x0 -> x2, Pallas kernels: none -> 5.98 us  [the longest x1 4 us: tiles(): pl.pallas_call(tiles_kernel, out_shape=jax.ShapeDtypeStruct((parts, 2 * (...]
    all_to_all x2, starting transfers between devices: 11.8 us -> 7.34 us  [exchange(): return lax.all_to_all(x, 'sample', 0, 0, tiled=False)]
    unnamed x19 -> x8, local copies, waits for them, and re-layouts: 4.39 us -> 0.01 us
    ppermute x8, starting transfers between devices: 7 us -> 10.6 us  [the longest x2 7.59 us: from_partner(): return lax.ppermute(x, 'sample', partner_route)]
    all_to_all x1, blocking collectives: 21 us -> 18.4 us  [exchange(): return lax.all_to_all(x, 'sample', 0, 0, tiled=False)]
  transfers between devices with their start and end apart: 10 -> 10, of which waited for: 4 -> 5; matrix products, arithmetic and copies ran while one was open for 12% -> 10% of each run, Pallas kernels for 0% -> 2%
where the time goes in v2:
time: 114 us
  waiting for transfers between devices  58.6 us (51%)
  blocking collectives  18.4 us (16%)
  starting transfers between devices  17.9 us (16%)
  other arithmetic  9.89 us (9%)
  Pallas kernels  5.98 us (5%)
  local copies, waits for them, and re-layouts  2.52 us (2%)
    all_to_all x2, waiting for transfers between devices, exchange(): return lax.all_to_all(x, 'sample', 0, 0, tiled=False)  36.1 us
    ppermute x3, waiting for transfers between devices, from_far(): return lax.ppermute(x, both, far_route)  21.7 us
    all_to_all x1, blocking collectives, exchange(): return lax.all_to_all(x, 'sample', 0, 0, tiled=False)  18.4 us
    ppermute x2, starting transfers between devices, from_partner(): return lax.ppermute(x, 'sample', partner_route)  7.59 us
    all_to_all x2, starting transfers between devices, exchange(): return lax.all_to_all(x, 'sample', 0, 0, tiled=False)  7.34 us
    pallas_call x1, Pallas kernels, tiles(): pl.pallas_call(tiles_kernel, out_shape=jax.ShapeDtypeStruct((parts, 2 * (...  4 us
    another operation x3, other arithmetic, shards(): factor = jnp.linalg.cholesky(moment)  3.48 us
    another operation x2, other arithmetic, shards(): jax.scipy.linalg.solve_triangular(factor, jnp.eye(rows, dtype=F32), lower...  3.01 us
  transfers between devices with their start and end apart: 10, of which 5 were waited for; matrix products, arithmetic and copies ran while one was open for 10% of the time, Pallas kernels for 2%

profile of v2, /device:TPU:6, one launch (start us, length us, event | category | flops | bytes accessed | tf_op | source)
XLA Modules:
  0.0 113.6 jit_solution(15244619527828213363)
XLA Ops:
  0.0 0.0 copy-start
  0.0 0.0 copy-start.1
  0.0 3.2 %collective-permute-start = (bf16[512,512]{1,0:T(8,128)(2,1)}, bf16[512,512]{1,0:T(8,128)(2,1)S(1)}, u32[]{:S(2)}, u32[]{:S(2)}) collective-permute-start(bf16[512,512]{1,0:T(8,128)(2,1)} %own0.1), channel_id=1, source_target_pairs={{0,128},{16,144},{32,160},{48,176},{64,192},{80,208},{96,224},{112... | collective-permute-start | bytes 1572872 | tf_op jit(solution)/shard_map/ppermute | solution.py:145
  3.2 2.0 %local_sums.1 = f32[32,640]{1,0:T(8,128)} custom-call(bf16[512,512]{1,0:T(8,128)(2,1)} %own0.1, f32[30,512]{1,0:T(8,128)} %cov0.1), custom_call_target="tpu_custom_call" | custom-call | tf_op jit(solution)/shard_map/local_sums/pallas_call | solution.py:52
  5.2 0.9 reshape.25
  6.1 18.4 %all_to_all.15 = f32[16,2,640]{2,1,0:T(2,128)S(1)} all-to-all(f32[16,2,640]{2,1,0:T(2,128)S(1)} %reshape.25), channel_id=1, replica_groups=mesh['sample'=16,'variant'=16] {'sample'}, dimensions={0} | all-to-all | bytes 163840 | tf_op jit(solution)/shard_map/all_to_all | solution.py:120
  24.6 0.7 broadcast_in_dim.24
  25.2 3.5 %all-to-all-start.1 = ((f32[16,2,640]{2,1,0:T(2,128)}), f32[16,2,640]{2,1,0:T(2,128)S(1)}, u32[]{:S(2)}, u32[]{:S(2)}) async-start(f32[16,2,640]{2,1,0:T(2,128)} %broadcast_in_dim.24), calls=%async_computation.1 | async-start | bytes 163840 | tf_op jit(solution)/shard_map/all_to_all | solution.py:120
  28.7 0.0 copy-done
  28.8 0.9 collective-permute-start.1
  29.7 0.0 copy-done.1
  29.7 4.4 %collective-permute-start.5 = (f32[30,512]{1,0:T(8,128)S(1)}, f32[30,512]{1,0:T(8,128)S(1)}, u32[]{:S(2)}, u32[]{:S(2)}) collective-permute-start(f32[30,512]{1,0:T(8,128)S(1)} %copy-done.1), channel_id=1, source_target_pairs={{0,128},{16,144},{32,160},{48,176},{64,192},{80,208},{96,224},{112... | collective-permute-start | bytes 184328 | tf_op jit(solution)/shard_map/ppermute | solution.py:145
  34.1 4.7 %all-to-all-done.1 = f32[16,2,640]{2,1,0:T(2,128)S(1)} async-done(((f32[16,2,640]{2,1,0:T(2,128)}), f32[16,2,640]{2,1,0:T(2,128)S(1)}, u32[]{:S(2)}, u32[]{:S(2)}) %all-to-all-start.1) | async-done | bytes 81952 | tf_op jit(solution)/shard_map/all_to_all | solution.py:120
  38.7 0.1 reshape.26
  38.8 0.1 copy.5
  38.9 0.0 collective-permute-done.own1
  38.9 0.9 collective-permute-start.2
  39.8 2.8 %cholesky.17 = f32[31,31]{1,0:T(8,128)S(1)} custom-call(f32[31,31]{1,0:T(8,128)S(1)} %fusion.7), custom_call_target="Cholesky" | custom-call | tf_op jit(solution)/shard_map/jit(cholesky)/cholesky | solution.py:167
  42.6 0.6 collective-permute-start.6
  43.3 0.6 compare_reduce_fusion
  43.9 2.6 %collective-permute-done.1.far0 = bf16[512,512]{1,0:T(8,128)(2,1)S(1)} collective-permute-done((bf16[512,512]{1,0:T(8,128)(2,1)S(1)}, bf16[512,512]{1,0:T(8,128)(2,1)S(1)}, u32[]{:S(2)}, u32[]{:S(2)}) %collective-permute-start.1) | collective-permute-done | bytes 524320 | tf_op jit(solution)/shard_map/ppermute | solution.py:148
  46.5 0.8 broadcast_select_fusion.1
  47.4 0.0 collective-permute-start.3
  47.4 19.1 %collective-permute-done.2.far1 = bf16[512,512]{1,0:T(8,128)(2,1)S(1)} collective-permute-done((bf16[512,512]{1,0:T(8,128)(2,1)S(1)}, bf16[512,512]{1,0:T(8,128)(2,1)S(1)}, u32[]{:S(2)}, u32[]{:S(2)}) %collective-permute-start.2) | collective-permute-done | bytes 524320 | tf_op jit(solution)/shard_map/ppermute | solution.py:148
  66.5 0.9 broadcast_select_fusion
  67.3 0.0 collective-permute-start.4
  67.3 0.7 fusion.4
  68.0 2.4 %custom-call.7 = f32[1,31,31]{1,2,0:T(8,128)S(1)} custom-call(f32[1,31,31]{2,1,0:T(8,128)S(1)} %fusion.4), custom_call_target="InvertDiagBlocksLowerTriangular" | custom-call | tf_op jit(solution)/shard_map/jit(_solve_triangular)/triangular_solve | solution.py:168
  70.4 0.0 collective-permute-done.6.cross_far
  70.4 0.6 collective-permute-start.7
  71.0 0.2 fusion.5
  71.2 0.0 collective-permute-done.5.cov1
  71.2 0.7 collective-permute-done.7.cross_near
  71.9 0.0 collective-permute-done.3.near0
  71.9 0.0 collective-permute-done.4.near1
  71.9 4.0 %tiles.1 = bf16[16,72,512]{2,1,0:T(8,128)(2,1)} custom-call(bf16[512,512]{1,0:T(8,128)(2,1)S(1)} %copy-done, bf16[512,512]{1,0:T(8,128)(2,1)S(1)} %collective-permute-done.own1, bf16[512,512]{1,0:T(8,128)(2,1)S(1)} %collective-permute-done.1.far0, bf16[512,512]{1,0:T(8,128)(2,1)S(1)} %collective-permute-done.2.far1, ...), custom_call_target="tpu_custom_call" | custom-call | tf_op jit(solution)/shard_map/tiles/pallas_call | solution.py:106
  75.9 0.0 copy-start.2
  75.9 0.0 copy-start.3
  75.9 3.8 %all-to-all-start.2 = ((bf16[16,72,512]{2,1,0:T(8,128)(2,1)}), bf16[16,72,512]{2,1,0:T(8,128)(2,1)S(1)}, u32[]{:S(2)}, u32[]{:S(2)}) async-start(bf16[16,72,512]{2,1,0:T(8,128)(2,1)} %tiles.1), calls=%async_computation.2 | async-start | bytes 2359296 | tf_op jit(solution)/shard_map/all_to_all | solution.py:120
  79.7 0.0 copy-done.2
  79.7 0.6 dynamic_slice.6
  80.3 0.0 copy-done.3
  80.3 0.6 broadcast_compare_fusion
  81.0 31.4 %all-to-all-done.2 = bf16[16,72,512]{2,1,0:T(8,128)(2,1)S(1)} async-done(((bf16[16,72,512]{2,1,0:T(8,128)(2,1)}), bf16[16,72,512]{2,1,0:T(8,128)(2,1)S(1)}, u32[]{:S(2)}, u32[]{:S(2)}) %all-to-all-start.2) | async-done | bytes 1179680 | tf_op jit(solution)/shard_map/all_to_all | solution.py:120
  112.4 0.2 convert_reduce_fusion
  112.7 0.1 dynamic-slice_bitcast_fusion
  112.8 0.8 fusion.3
  (13 shorter events, 0.2 us)
Async XLA Ops:
  0.0 28.8 %copy-start = (bf16[512,512]{1,0:T(8,128)(2,1)S(1)}, bf16[512,512]{1,0:T(8,128)(2,1)}, u32[]{:S(2)}) copy-start(bf16[512,512]{1,0:T(8,128)(2,1)} %own0.1) | copy-start | bytes 1572868
  0.0 29.7 %copy-start.1 = (f32[30,512]{1,0:T(8,128)S(1)}, f32[30,512]{1,0:T(8,128)}, u32[]{:S(2)}) copy-start(f32[30,512]{1,0:T(8,128)} %cov0.1) | copy-start | bytes 184324
  0.0 38.9 %collective-permute-start = (bf16[512,512]{1,0:T(8,128)(2,1)}, bf16[512,512]{1,0:T(8,128)(2,1)S(1)}, u32[]{:S(2)}, u32[]{:S(2)}) collective-permute-start(bf16[512,512]{1,0:T(8,128)(2,1)} %own0.1), channel_id=1, source_target_pairs={{0,128},{16,144},{32,160},{48,176},{64,192},{80,208},{96,224},{112... | collective-permute-start | bytes 1572872 | tf_op jit(solution)/shard_map/ppermute | solution.py:145
  25.2 13.5 %all-to-all-start.1 = ((f32[16,2,640]{2,1,0:T(2,128)}), f32[16,2,640]{2,1,0:T(2,128)S(1)}, u32[]{:S(2)}, u32[]{:S(2)}) async-start(f32[16,2,640]{2,1,0:T(2,128)} %broadcast_in_dim.24), calls=%async_computation.1 | async-start | bytes 163840 | tf_op jit(solution)/shard_map/all_to_all | solution.py:120
  28.8 17.8 %collective-permute-start.1 = (bf16[512,512]{1,0:T(8,128)(2,1)S(1)}, bf16[512,512]{1,0:T(8,128)(2,1)S(1)}, u32[]{:S(2)}, u32[]{:S(2)}) collective-permute-start(bf16[512,512]{1,0:T(8,128)(2,1)S(1)} %copy-done), channel_id=1, source_target_pairs={{2,0},{3,1},{4,2},{5,3},{6,4},{7,5},{8,6},{9,7},{10,8},{11,9},{12,... | collective-permute-start | bytes 1572872 | tf_op jit(solution)/shard_map/ppermute | solution.py:148
  29.7 41.5 %collective-permute-start.5 = (f32[30,512]{1,0:T(8,128)S(1)}, f32[30,512]{1,0:T(8,128)S(1)}, u32[]{:S(2)}, u32[]{:S(2)}) collective-permute-start(f32[30,512]{1,0:T(8,128)S(1)} %copy-done.1), channel_id=1, source_target_pairs={{0,128},{16,144},{32,160},{48,176},{64,192},{80,208},{96,224},{112... | collective-permute-start | bytes 184328 | tf_op jit(solution)/shard_map/ppermute | solution.py:145
  38.9 27.6 %collective-permute-start.2 = (bf16[512,512]{1,0:T(8,128)(2,1)S(1)}, bf16[512,512]{1,0:T(8,128)(2,1)S(1)}, u32[]{:S(2)}, u32[]{:S(2)}) collective-permute-start(bf16[512,512]{1,0:T(8,128)(2,1)S(1)} %collective-permute-done.own1), channel_id=1, source_target_pairs={{2,0},{3,1},{4,2},{5,3},{6,4},{7,5},{8,6},{9,7},{10,8},{11,9},{12,... | collective-permute-start | bytes 1572872 | tf_op jit(solution)/shard_map/ppermute | solution.py:148
  42.6 27.7 %collective-permute-start.6 = (f32[32,512]{1,0:T(8,128)S(1)}, f32[32,512]{1,0:T(8,128)S(1)}, u32[]{:S(2)}, u32[]{:S(2)}) collective-permute-start(f32[32,512]{1,0:T(8,128)S(1)} %slice.70.cross_own), channel_id=1, source_target_pairs={{2,0},{3,1},{4,2},{5,3},{6,4},{7,5},{8,6},{9,7},{10,8},{11,9},{12,... | collective-permute-start | bytes 196616 | tf_op jit(solution)/shard_map/ppermute | solution.py:148
  47.4 24.5 %collective-permute-start.3 = (bf16[512,512]{1,0:T(8,128)(2,1)}, bf16[512,512]{1,0:T(8,128)(2,1)S(1)}, u32[]{:S(2)}, u32[]{:S(2)}) collective-permute-start(bf16[512,512]{1,0:T(8,128)(2,1)} %broadcast_select_fusion.1), channel_id=1, source_target_pairs={{0,1},{1,0},{2,3},{3,2},{4,5},{5,4},{6,7},{7,6},{8,9},{9,8},{10,11... | collective-permute-start | bytes 1572872 | tf_op jit(solution)/shard_map/ppermute | solution.py:151
  67.3 4.6 %collective-permute-start.4 = (bf16[512,512]{1,0:T(8,128)(2,1)}, bf16[512,512]{1,0:T(8,128)(2,1)S(1)}, u32[]{:S(2)}, u32[]{:S(2)}) collective-permute-start(bf16[512,512]{1,0:T(8,128)(2,1)} %broadcast_select_fusion), channel_id=1, source_target_pairs={{0,1},{1,0},{2,3},{3,2},{4,5},{5,4},{6,7},{7,6},{8,9},{9,8},{10,11... | collective-permute-start | bytes 1572872 | tf_op jit(solution)/shard_map/ppermute | solution.py:151
  70.4 1.5 %collective-permute-start.7 = (f32[32,512]{1,0:T(8,128)S(1)}, f32[32,512]{1,0:T(8,128)S(1)}, u32[]{:S(2)}, u32[]{:S(2)}) collective-permute-start(f32[32,512]{1,0:T(8,128)S(1)} %broadcast_select_fusion.2), channel_id=1, source_target_pairs={{0,1},{1,0},{2,3},{3,2},{4,5},{5,4},{6,7},{7,6},{8,9},{9,8},{10,11... | collective-permute-start | bytes 196616 | tf_op jit(solution)/shard_map/ppermute | solution.py:151
  75.9 3.8 %copy-start.2 = (s32[16]{0:T(128)S(1)}, s32[16]{0:T(128)}, u32[]{:S(2)}) copy-start(s32[16]{0:T(128)} %param.6) | copy-start | bytes 196
  75.9 4.4 %copy-start.3 = (s32[4]{0:T(128)S(1)}, s32[4]{0:T(128)}, u32[]{:S(2)}) copy-start(s32[4]{0:T(128)} %constant.93.clone) | copy-start | bytes 52
  75.9 36.5 %all-to-all-start.2 = ((bf16[16,72,512]{2,1,0:T(8,128)(2,1)}), bf16[16,72,512]{2,1,0:T(8,128)(2,1)S(1)}, u32[]{:S(2)}, u32[]{:S(2)}) async-start(bf16[16,72,512]{2,1,0:T(8,128)(2,1)} %tiles.1), calls=%async_computation.2 | async-start | bytes 2359296 | tf_op jit(solution)/shard_map/all_to_all | solution.py:120

commit v3 on v2

--- a/solution.py
+++ b/solution.py
@@ -128,16 +128,16 @@
     samples = local_samples * parts
     place = lax.axis_index("sample")
     core = lax.axis_index("variant") % 2
-    side = place // half
+    side = place % 2
     rows = covariates.shape[0] + 1
     padded = -(-rows // parts) * parts
     both = ("sample", "variant")
 
-    partner_route = [(i, i ^ half) for i in range(parts)]
+    partner_route = [(i, i ^ 1) for i in range(parts)]
     core_route = [(i, i ^ 1) for i in range(blocks)]
     far_route = []
     for s in range(parts):
-        step = MAXR if s < half else -MAXR
+        step = MAXR if s % 2 == 0 else -MAXR
         for v in range(blocks):
             far_route.append((s * blocks + (v + step) % blocks, s * blocks + v))
 
@@ -147,22 +147,31 @@
     def from_far(x):
         return lax.ppermute(x, both, far_route)
 
-    def from_near(own, far):
-        return lax.ppermute(jnp.where(core != side, own, far), "variant", core_route)
+    def for_mate(own, far):
+        return jnp.where(core != side, own, far)
+
+    def swap(x):
+        return lax.ppermute(x, "variant", core_route)
+
+    def after(x, *earlier):
+        return lax.optimization_barrier((x,) + earlier)[0]
 
     own0 = dosage
-    far0 = from_far(own0)
-    own1 = from_partner(own0)
     covariates1 = from_partner(covariates)
-    local = local_sums(dosage, covariates, padded)
-    chunk = exchange(local.reshape(parts, padded // parts, -1)).sum(0)
-    far1 = from_far(own1)
-    near0 = from_near(own0, far0)
-    total = exchange(jnp.broadcast_to(chunk[None], (parts,) + chunk.shape)).reshape(padded, -1)
-    near1 = from_near(own1, far1)
+    message = local_sums(dosage, covariates, padded).reshape(parts, padded // parts, -1)
+    sent = own0
+    own1 = from_partner(sent)
+    far0 = from_far(sent)
+    chunk = exchange(message).sum(0)
+    message = jnp.broadcast_to(chunk[None], (parts,) + chunk.shape)
+    far1 = from_far(after(own1, message))
+    message = after(message, own1, far0)
+    total = exchange(message).reshape(padded, -1)
+    give0, give1 = for_mate(own0, far0), for_mate(own1, far1)
+    near0, near1 = swap(give0), swap(give1)
     cross = total[:, :width]
     cross_far = from_far(cross)
-    cross_near = from_near(cross, cross_far)
+    cross_near = swap(for_mate(cross, cross_far))
     moment = total[:rows, width : width + rows]
     factor = jnp.linalg.cholesky(moment)
     inverse = jax.scipy.linalg.solve_triangular(factor, jnp.eye(rows, dtype=F32), lower=True)
@@ -175,8 +184,8 @@
         parts,
     )
     share = width // parts
-    arrived = exchange(message).reshape(2, half, 2 * share + 8, width)
-    whole = arrived.astype(F32).sum(1)
+    arrived = exchange(message).reshape(half, 2, 2 * share + 8, width)
+    whole = arrived.astype(F32).sum(0)
     far, near = whole[:, :share], whole[:, share : 2 * share]
     bands = jnp.stack([far[1], near[1], near[0], far[0]])
     spread = whole[:, 2 * share : 2 * share + 6 : 2] + whole[:, 2 * share + 1 : 2 * share + 6 : 2]

time: 114 us -> 98.5 us (0.86)
  blocking collectives: 18.4 us -> 0 us
  starting transfers between devices: 17.9 us -> 29.2 us
  waiting for transfers between devices: 58.6 us -> 49.6 us
    ppermute x3, waiting for transfers between devices: 21.7 us -> 1.28 us  [from_far(): return lax.ppermute(x, both, far_route)]
    all_to_all x1 -> x0, blocking collectives: 18.4 us -> none  [exchange(): return lax.all_to_all(x, 'sample', 0, 0, tiled=False)]
    all_to_all x2 -> x3, starting transfers between devices: 7.34 us -> 22.2 us  [exchange(): return lax.all_to_all(x, 'sample', 0, 0, tiled=False)]
    all_to_all x2 -> x3, waiting for transfers between devices: 36.1 us -> 47.3 us  [exchange(): return lax.all_to_all(x, 'sample', 0, 0, tiled=False)]
    ppermute x2, starting transfers between devices: 7.59 us -> 4.51 us  [from_partner(): return lax.ppermute(x, 'sample', partner_route)]
  transfers between devices with their start and end apart: 10 -> 11, of which waited for: 5 -> 5; matrix products, arithmetic and copies ran while one was open for 10% -> 12% of each run, Pallas kernels for 2% -> 2%
where the time goes in v3:
time: 98.5 us; the launch traced here: 98.1 us
  waiting for transfers between devices  49.6 us (50%)
  starting transfers between devices  29.2 us (30%)
  other arithmetic  9.88 us (10%)
  Pallas kernels  6 us (6%)
  local copies, waits for them, and re-layouts  3.15 us (3%)
    all_to_all x3, waiting for transfers between devices, exchange(): return lax.all_to_all(x, 'sample', 0, 0, tiled=False)  47.3 us
    all_to_all x3, starting transfers between devices, exchange(): return lax.all_to_all(x, 'sample', 0, 0, tiled=False)  22.2 us
    ppermute x2, starting transfers between devices, from_partner(): return lax.ppermute(x, 'sample', partner_route)  4.51 us
    pallas_call x1, Pallas kernels, tiles(): pl.pallas_call(tiles_kernel, out_shape=jax.ShapeDtypeStruct((parts, 2 * (...  4.01 us
    another operation x3, other arithmetic, shards(): factor = jnp.linalg.cholesky(moment)  3.48 us
    another operation x2, other arithmetic, shards(): jax.scipy.linalg.solve_triangular(factor, jnp.eye(rows, dtype=F32), lower...  3.01 us
    ppermute x3, starting transfers between devices, from_far(): return lax.ppermute(x, both, far_route)  2.34 us
    pallas_call x1, Pallas kernels, local_sums(): pl.pallas_call(sums_kernel, out_shape=jax.ShapeDtypeStruct((padded, width...  1.99 us
  transfers between devices with their start and end apart: 11, of which 5 were waited for; matrix products, arithmetic and copies ran while one was open for 12% of the time, Pallas kernels for 2%

profile of v3, /device:TPU:6, one launch (start us, length us, event | category | flops | bytes accessed | tf_op | source)
XLA Modules:
  0.0 98.1 jit_solution(909475798429686898)
XLA Ops:
  0.0 0.0 copy-start
  0.0 0.8 collective-permute-start.1
  0.8 2.6 %collective-permute-start = (bf16[512,512]{1,0:T(8,128)(2,1)}, bf16[512,512]{1,0:T(8,128)(2,1)S(1)}, u32[]{:S(2)}, u32[]{:S(2)}) collective-permute-start(bf16[512,512]{1,0:T(8,128)(2,1)} %own0.1), channel_id=1, source_target_pairs={{0,16},{16,0},{32,48},{48,32},{64,80},{80,64},{96,112},{112,96},{1... | collective-permute-start | bytes 1572872 | tf_op jit(solution)/shard_map/ppermute | solution.py:145
  3.4 2.0 %local_sums.1 = f32[32,640]{1,0:T(8,128)} custom-call(bf16[512,512]{1,0:T(8,128)(2,1)} %own0.1, f32[30,512]{1,0:T(8,128)} %cov0.1), custom_call_target="tpu_custom_call" | custom-call | tf_op jit(solution)/shard_map/local_sums/pallas_call | solution.py:52
  5.4 1.6 %reshape.25 = f32[16,2,640]{2,1,0:T(2,128)} reshape(f32[32,640]{1,0:T(8,128)} %local_sums.1) | data formatting | bytes 163840 | tf_op jit(solution)/shard_map/reshape | solution.py:161
  7.0 10.0 %all-to-all-start = ((f32[16,2,640]{2,1,0:T(2,128)}), f32[16,2,640]{2,1,0:T(2,128)S(1)}, u32[]{:S(2)}, u32[]{:S(2)}) async-start(f32[16,2,640]{2,1,0:T(2,128)} %reshape.25), calls=%async_computation | async-start | bytes 163840 | tf_op jit(solution)/shard_map/all_to_all | solution.py:120
  17.0 1.9 %collective-permute-start.5 = (f32[30,512]{1,0:T(8,128)}, f32[30,512]{1,0:T(8,128)S(1)}, u32[]{:S(2)}, u32[]{:S(2)}) collective-permute-start(f32[30,512]{1,0:T(8,128)} %cov0.1), channel_id=1, source_target_pairs={{0,16},{16,0},{32,48},{48,32},{64,80},{80,64},{96,112},{112,96},{1... | collective-permute-start | bytes 184328 | tf_op jit(solution)/shard_map/ppermute | solution.py:145
  18.9 8.1 %all-to-all-done = f32[16,2,640]{2,1,0:T(2,128)S(1)} async-done(((f32[16,2,640]{2,1,0:T(2,128)}), f32[16,2,640]{2,1,0:T(2,128)S(1)}, u32[]{:S(2)}, u32[]{:S(2)}) %all-to-all-start) | async-done | bytes 81952 | tf_op jit(solution)/shard_map/all_to_all | solution.py:120
  27.1 0.0 collective-permute-done.1.far0
  27.1 0.0 collective-permute-done.own1
  27.1 0.7 broadcast_in_dim.24
  27.7 3.5 %all-to-all-start.1 = ((f32[16,2,640]{2,1,0:T(2,128)}), f32[16,2,640]{2,1,0:T(2,128)S(1)}, u32[]{:S(2)}, u32[]{:S(2)}) async-start(f32[16,2,640]{2,1,0:T(2,128)} %broadcast_in_dim.24), calls=%async_computation.1 | async-start | bytes 163840 | tf_op jit(solution)/shard_map/all_to_all | solution.py:120
  31.2 0.9 collective-permute-start.2
  32.2 0.0 copy-done
  32.2 0.9 broadcast_select_fusion.1
  33.0 0.0 copy-start.1
  33.0 0.0 collective-permute-start.3
  33.0 8.5 %all-to-all-done.1 = f32[16,2,640]{2,1,0:T(2,128)S(1)} async-done(((f32[16,2,640]{2,1,0:T(2,128)}), f32[16,2,640]{2,1,0:T(2,128)S(1)}, u32[]{:S(2)}, u32[]{:S(2)}) %all-to-all-start.1) | async-done | bytes 81952 | tf_op jit(solution)/shard_map/all_to_all | solution.py:120
  41.5 0.1 reshape.26
  41.6 0.1 copy.5
  41.7 2.8 %cholesky.17 = f32[31,31]{1,0:T(8,128)S(1)} custom-call(f32[31,31]{1,0:T(8,128)S(1)} %fusion.7), custom_call_target="Cholesky" | custom-call | tf_op jit(solution)/shard_map/jit(cholesky)/cholesky | solution.py:176
  44.5 0.6 collective-permute-start.6
  45.2 0.6 compare_reduce_fusion
  45.8 0.0 collective-permute-done.2.far1
  45.8 0.9 broadcast_select_fusion
  46.7 0.0 collective-permute-start.4
  46.7 0.7 fusion.4
  47.3 2.4 %custom-call.7 = f32[1,31,31]{1,2,0:T(8,128)S(1)} custom-call(f32[1,31,31]{2,1,0:T(8,128)S(1)} %fusion.4), custom_call_target="InvertDiagBlocksLowerTriangular" | custom-call | tf_op jit(solution)/shard_map/jit(_solve_triangular)/triangular_solve | solution.py:177
  49.7 1.3 %collective-permute-done.6.cross_far = f32[32,512]{1,0:T(8,128)S(1)} collective-permute-done((f32[32,512]{1,0:T(8,128)S(1)}, f32[32,512]{1,0:T(8,128)S(1)}, u32[]{:S(2)}, u32[]{:S(2)}) %collective-permute-start.6) | collective-permute-done | bytes 65568 | tf_op jit(solution)/shard_map/ppermute | solution.py:148
  51.0 0.1 collective-permute-start.7
  51.1 0.2 fusion.5
  51.3 0.0 collective-permute-done.5.cov1
  51.3 1.0 %collective-permute-done.7.cross_near = f32[32,512]{1,0:T(8,128)S(1)} collective-permute-done((f32[32,512]{1,0:T(8,128)S(1)}, f32[32,512]{1,0:T(8,128)S(1)}, u32[]{:S(2)}, u32[]{:S(2)}) %collective-permute-start.7) | collective-permute-done | bytes 65568 | tf_op jit(solution)/shard_map/ppermute | solution.py:154
  52.3 0.0 collective-permute-done.3.near0
  52.3 0.0 collective-permute-done.4.near1
  52.3 0.0 copy-done.1
  52.3 4.0 %tiles.1 = bf16[16,72,512]{2,1,0:T(8,128)(2,1)} custom-call(bf16[512,512]{1,0:T(8,128)(2,1)S(1)} %copy-done, bf16[512,512]{1,0:T(8,128)(2,1)S(1)} %collective-permute-done.own1, bf16[512,512]{1,0:T(8,128)(2,1)S(1)} %collective-permute-done.1.far0, bf16[512,512]{1,0:T(8,128)(2,1)S(1)} %collective-permute-done.2.far1, ...), custom_call_target="tpu_custom_call" | custom-call | tf_op jit(solution)/shard_map/tiles/pallas_call | solution.py:106
  56.3 0.0 copy-start.2
  56.3 0.0 copy-start.3
  56.3 8.7 %all-to-all-start.2 = ((bf16[16,72,512]{2,1,0:T(8,128)(2,1)}), bf16[16,72,512]{2,1,0:T(8,128)(2,1)S(1)}, u32[]{:S(2)}, u32[]{:S(2)}) async-start(bf16[16,72,512]{2,1,0:T(8,128)(2,1)} %tiles.1), calls=%async_computation.2 | async-start | bytes 2359296 | tf_op jit(solution)/shard_map/all_to_all | solution.py:120
  65.1 0.0 copy-done.2
  65.1 0.6 dynamic_slice.6
  65.7 0.0 copy-done.3
  65.7 0.6 broadcast_compare_fusion
  66.3 30.7 %all-to-all-done.2 = bf16[16,72,512]{2,1,0:T(8,128)(2,1)S(1)} async-done(((bf16[16,72,512]{2,1,0:T(8,128)(2,1)}), bf16[16,72,512]{2,1,0:T(8,128)(2,1)S(1)}, u32[]{:S(2)}, u32[]{:S(2)}) %all-to-all-start.2) | async-done | bytes 1179680 | tf_op jit(solution)/shard_map/all_to_all | solution.py:120
  97.0 0.2 convert_reduce_fusion
  97.3 0.1 dynamic-slice_bitcast_fusion
  97.4 0.8 fusion.3
  (13 shorter events, 0.2 us)
Async XLA Ops:
  0.0 32.2 %copy-start = (bf16[512,512]{1,0:T(8,128)(2,1)S(1)}, bf16[512,512]{1,0:T(8,128)(2,1)}, u32[]{:S(2)}) copy-start(bf16[512,512]{1,0:T(8,128)(2,1)} %own0.1) | copy-start | bytes 1572868
  0.0 27.1 %collective-permute-start.1 = (bf16[512,512]{1,0:T(8,128)(2,1)}, bf16[512,512]{1,0:T(8,128)(2,1)S(1)}, u32[]{:S(2)}, u32[]{:S(2)}) collective-permute-start(bf16[512,512]{1,0:T(8,128)(2,1)} %own0.1), channel_id=1, source_target_pairs={{2,0},{3,1},{4,2},{5,3},{6,4},{7,5},{8,6},{9,7},{10,8},{11,9},{12,... | collective-permute-start | bytes 1572872 | tf_op jit(solution)/shard_map/ppermute | solution.py:148
  0.8 26.2 %collective-permute-start = (bf16[512,512]{1,0:T(8,128)(2,1)}, bf16[512,512]{1,0:T(8,128)(2,1)S(1)}, u32[]{:S(2)}, u32[]{:S(2)}) collective-permute-start(bf16[512,512]{1,0:T(8,128)(2,1)} %own0.1), channel_id=1, source_target_pairs={{0,16},{16,0},{32,48},{48,32},{64,80},{80,64},{96,112},{112,96},{1... | collective-permute-start | bytes 1572872 | tf_op jit(solution)/shard_map/ppermute | solution.py:145
  7.0 20.0 %all-to-all-start = ((f32[16,2,640]{2,1,0:T(2,128)}), f32[16,2,640]{2,1,0:T(2,128)S(1)}, u32[]{:S(2)}, u32[]{:S(2)}) async-start(f32[16,2,640]{2,1,0:T(2,128)} %reshape.25), calls=%async_computation | async-start | bytes 163840 | tf_op jit(solution)/shard_map/all_to_all | solution.py:120
  17.0 34.3 %collective-permute-start.5 = (f32[30,512]{1,0:T(8,128)}, f32[30,512]{1,0:T(8,128)S(1)}, u32[]{:S(2)}, u32[]{:S(2)}) collective-permute-start(f32[30,512]{1,0:T(8,128)} %cov0.1), channel_id=1, source_target_pairs={{0,16},{16,0},{32,48},{48,32},{64,80},{80,64},{96,112},{112,96},{1... | collective-permute-start | bytes 184328 | tf_op jit(solution)/shard_map/ppermute | solution.py:145
  27.7 13.8 %all-to-all-start.1 = ((f32[16,2,640]{2,1,0:T(2,128)}), f32[16,2,640]{2,1,0:T(2,128)S(1)}, u32[]{:S(2)}, u32[]{:S(2)}) async-start(f32[16,2,640]{2,1,0:T(2,128)} %broadcast_in_dim.24), calls=%async_computation.1 | async-start | bytes 163840 | tf_op jit(solution)/shard_map/all_to_all | solution.py:120
  31.2 14.6 %collective-permute-start.2 = (bf16[512,512]{1,0:T(8,128)(2,1)S(1)}, bf16[512,512]{1,0:T(8,128)(2,1)S(1)}, u32[]{:S(2)}, u32[]{:S(2)}) collective-permute-start(bf16[512,512]{1,0:T(8,128)(2,1)S(1)} %collective-permute-done.own1), channel_id=1, source_target_pairs={{2,0},{3,1},{4,2},{5,3},{6,4},{7,5},{8,6},{9,7},{10,8},{11,9},{12,... | collective-permute-start | bytes 1572872 | tf_op jit(solution)/shard_map/ppermute | solution.py:148
  33.0 19.3 %copy-start.1 = (f32[30,512]{1,0:T(8,128)S(1)}, f32[30,512]{1,0:T(8,128)}, u32[]{:S(2)}) copy-start(f32[30,512]{1,0:T(8,128)} %cov0.1) | copy-start | bytes 184324
  33.0 19.3 %collective-permute-start.3 = (bf16[512,512]{1,0:T(8,128)(2,1)}, bf16[512,512]{1,0:T(8,128)(2,1)S(1)}, u32[]{:S(2)}, u32[]{:S(2)}) collective-permute-start(bf16[512,512]{1,0:T(8,128)(2,1)} %broadcast_select_fusion.1), channel_id=1, source_target_pairs={{0,1},{1,0},{2,3},{3,2},{4,5},{5,4},{6,7},{7,6},{8,9},{9,8},{10,11... | collective-permute-start | bytes 1572872 | tf_op jit(solution)/shard_map/ppermute | solution.py:154
  44.5 6.4 %collective-permute-start.6 = (f32[32,512]{1,0:T(8,128)S(1)}, f32[32,512]{1,0:T(8,128)S(1)}, u32[]{:S(2)}, u32[]{:S(2)}) collective-permute-start(f32[32,512]{1,0:T(8,128)S(1)} %slice.70.cross_own), channel_id=1, source_target_pairs={{2,0},{3,1},{4,2},{5,3},{6,4},{7,5},{8,6},{9,7},{10,8},{11,9},{12,... | collective-permute-start | bytes 196616 | tf_op jit(solution)/shard_map/ppermute | solution.py:148
  46.7 5.7 %collective-permute-start.4 = (bf16[512,512]{1,0:T(8,128)(2,1)}, bf16[512,512]{1,0:T(8,128)(2,1)S(1)}, u32[]{:S(2)}, u32[]{:S(2)}) collective-permute-start(bf16[512,512]{1,0:T(8,128)(2,1)} %broadcast_select_fusion), channel_id=1, source_target_pairs={{0,1},{1,0},{2,3},{3,2},{4,5},{5,4},{6,7},{7,6},{8,9},{9,8},{10,11... | collective-permute-start | bytes 1572872 | tf_op jit(solution)/shard_map/ppermute | solution.py:154
  51.0 1.3 %collective-permute-start.7 = (f32[32,512]{1,0:T(8,128)S(1)}, f32[32,512]{1,0:T(8,128)S(1)}, u32[]{:S(2)}, u32[]{:S(2)}) collective-permute-start(f32[32,512]{1,0:T(8,128)S(1)} %broadcast_select_fusion.2), channel_id=1, source_target_pairs={{0,1},{1,0},{2,3},{3,2},{4,5},{5,4},{6,7},{7,6},{8,9},{9,8},{10,11... | collective-permute-start | bytes 196616 | tf_op jit(solution)/shard_map/ppermute | solution.py:154
  56.3 8.7 %copy-start.2 = (s32[16]{0:T(128)S(1)}, s32[16]{0:T(128)}, u32[]{:S(2)}) copy-start(s32[16]{0:T(128)} %param.6) | copy-start | bytes 196
  56.3 9.3 %copy-start.3 = (s32[4]{0:T(128)S(1)}, s32[4]{0:T(128)}, u32[]{:S(2)}) copy-start(s32[4]{0:T(128)} %constant.83.clone) | copy-start | bytes 52
  56.3 40.6 %all-to-all-start.2 = ((bf16[16,72,512]{2,1,0:T(8,128)(2,1)}), bf16[16,72,512]{2,1,0:T(8,128)(2,1)S(1)}, u32[]{:S(2)}, u32[]{:S(2)}) async-start(bf16[16,72,512]{2,1,0:T(8,128)(2,1)} %tiles.1), calls=%async_computation.2 | async-start | bytes 2359296 | tf_op jit(solution)/shard_map/all_to_all | solution.py:120

commit v4 on v3

v4 whole, which is shorter than its diff:
```python
import functools
import math

import jax
import jax.numpy as jnp
from jax import lax
from jax.experimental import pallas as pl
from jax.experimental.pallas import tpu as pltpu
from jax.sharding import PartitionSpec as P

MAXR = 2
HIGHEST = lax.Precision.HIGHEST
BF16 = jnp.bfloat16
F32 = jnp.float32
LANES = 128
STEP = 128
COLUMNS_TOGETHER = (((0,), (0,)), ((), ()))


def split(value):
    high = value.astype(BF16)
    rest = value - high.astype(F32)
    middle = rest.astype(BF16)
    low = (rest - middle.astype(F32)).astype(BF16)
    return high, middle, low


def fill_design(design_ref, covariates_ref):
    count = covariates_ref.shape[0]
    design_ref[...] = jnp.zeros_like(design_ref)
    design_ref[:count, :] = covariates_ref[...]
    design_ref[count : count + 1, :] = jnp.ones((1, design_ref.shape[1]), F32)


def sums_kernel(dosage_ref, covariates_ref, out_ref, design_ref):
    fill_design(design_ref, covariates_ref)
    width = dosage_ref.shape[1]
    padded = design_ref.shape[0]
    design = design_ref[...]
    stacked = jnp.concatenate(split(design), 0)
    parts = jnp.dot(stacked, dosage_ref[...], preferred_element_type=F32)
    cross = parts[:padded] + parts[padded : 2 * padded] + parts[2 * padded :]
    moment = lax.dot_general(
        design, design, (((1,), (1,)), ((), ())), precision=HIGHEST, preferred_element_type=F32
    )
    left = jnp.zeros((padded, LANES // 2), F32)
    right = jnp.zeros((padded, LANES - LANES // 2 - padded), F32)
    moment = jnp.concatenate([left, moment, right], 1)
    each = out_ref.shape[1]
    for part in range(out_ref.shape[0]):
        out_ref[part, :, :width] = cross[part * each : (part + 1) * each]
        out_ref[part, :, width:] = moment[part * each : (part + 1) * each]


def local_sums(dosage, covariates, padded, parts):
    samples, width = dosage.shape
    return pl.pallas_call(
        sums_kernel,
        out_shape=jax.ShapeDtypeStruct((parts, padded // parts, width + LANES), F32),
        scratch_shapes=[pltpu.VMEM((padded, samples), F32)],
        name="local_sums",
    )(dosage, covariates)


def factor(total, count):
    padded, width = total.shape[0], total.shape[1] - LANES
    row = lax.broadcasted_iota(jnp.int32, (padded, LANES), 0)
    lane = lax.broadcasted_iota(jnp.int32, (padded, LANES), 1)
    first = LANES // 2
    spare = (row >= count) & (lane == row + first)
    work = total[:, width:] + jnp.where((lane == row) | spare, 1.0, 0.0)
    for step in range(count - 1):
        pivot_row = work[step : step + 1, :]
        pivot_row = pivot_row / pivot_row[:, first + step : first + step + 1]
        column = jnp.broadcast_to(work[:, first + step : first + step + 1], work.shape)
        work = work - jnp.where(row > step, column, 0.0) * pivot_row
    diagonal = jnp.sum(jnp.where(lane == row + first, work, 0.0), 1, keepdims=True)
    return work[:, :padded], work[:, :padded] / diagonal


def residual(pieces, cross, solved, white, target):
    h, m, l = split(jnp.dot(solved, cross, precision=HIGHEST, preferred_element_type=F32))
    stacked = jnp.concatenate([h, m, h, l, h, m], 0)
    spread = jnp.zeros((1, stacked.shape[1]), F32)
    at = 0
    for piece in pieces:
        for start in range(0, piece.shape[0], STEP):
            fitted = lax.dot_general(
                white[:, at : at + STEP], stacked, COLUMNS_TOGETHER, preferred_element_type=F32
            )
            rest = piece[start : start + STEP, :].astype(F32) - fitted
            spread = spread + jnp.sum(rest * rest, 0, keepdims=True)
            target[at : at + STEP, :] = rest.astype(BF16)
            at += STEP
    high = spread.astype(BF16)
    low = (spread - high.astype(F32)).astype(BF16)
    return [high, low]


def tile_of(left, right):
    tile = lax.dot_general(left[...], right[...], COLUMNS_TOGETHER, preferred_element_type=F32)
    return tile.astype(BF16)


def own_kernel(count, own0, own1, cov0, cov1, total, solved_ref, white_ref, left, rows_ref, design):
    samples, width = own0.shape
    fill_design(design.at[:, :samples], cov0)
    fill_design(design.at[:, samples:], cov1)
    unit, solved = factor(total[...], count)
    h, m, l = split(jnp.dot(unit, design[...], precision=HIGHEST, preferred_element_type=F32))
    white = jnp.concatenate([h, h, m, h, l, m], 0)
    white_ref[...] = white
    solved_ref[...] = solved
    rows = residual((own0, own1), total[:, :width], solved, white, left)
    rows_ref[...] = jnp.concatenate(rows, 0)


def far_kernel(far0, far1, cross_far, solved, white, left, own_rows, tile_ref, rows_ref, right):
    rows = residual((far0, far1), cross_far[...], solved[...], white[...], right)
    tile_ref[...] = tile_of(left, right)
    rows_ref[...] = jnp.concatenate([own_rows[...]] + rows, 0)


def near_kernel(
    near0, near1, cross_near, solved, far_tile_ref, left, white, rows_ref, out_ref, right
):
    width = near0.shape[1]
    share = width // out_ref.shape[0]
    rows = [rows_ref[...]] + residual((near0, near1), cross_near[...], solved[...], white[...], right)
    tile = tile_of(left, right)
    extra = out_ref.shape[1] - 2 * share
    rows = jnp.concatenate(rows + [jnp.zeros((extra - 6, width), BF16)], 0)
    for part in range(out_ref.shape[0]):
        at = slice(part * share, (part + 1) * share)
        out_ref[part, :share, :] = far_tile_ref[at, :]
        out_ref[part, share : 2 * share, :] = tile[at]
        out_ref[part, 2 * share :, :] = rows


def own_residual(own, covariates, total):
    samples, width = own[0].shape
    padded = total.shape[0]
    return pl.pallas_call(
        functools.partial(own_kernel, covariates[0].shape[0] + 1),
        out_shape=(
            jax.ShapeDtypeStruct((padded, padded), F32),
            jax.ShapeDtypeStruct((6 * padded, 2 * samples), BF16),
            jax.ShapeDtypeStruct((2 * samples, width), BF16),
            jax.ShapeDtypeStruct((2, width), BF16),
        ),
        scratch_shapes=[pltpu.VMEM((padded, 2 * samples), F32)],
        compiler_params=pltpu.CompilerParams(vmem_limit_bytes=12 << 20),
        cost_estimate=pl.CostEstimate(flops=4_000_000_000, bytes_accessed=15_000_000, transcendentals=0),
        name="own_residual",
    )(*own, *covariates, total)


def far_tile(far, cross_far, solved, white, left, own_rows):
    samples, width = far[0].shape
    return pl.pallas_call(
        far_kernel,
        out_shape=(
            jax.ShapeDtypeStruct((width, width), BF16),
            jax.ShapeDtypeStruct((4, width), BF16),
        ),
        scratch_shapes=[pltpu.VMEM((2 * samples, width), BF16)],
        compiler_params=pltpu.CompilerParams(vmem_limit_bytes=12 << 20),
        cost_estimate=pl.CostEstimate(flops=1_000_000_000, bytes_accessed=6_000_000, transcendentals=0),
        name="far_tile",
    )(*far, cross_far, solved, white, left, own_rows)


def messages(near, cross_near, solved, far, left, white, rows, parts):
    samples, width = near[0].shape
    return pl.pallas_call(
        near_kernel,
        out_shape=jax.ShapeDtypeStruct((parts, 2 * (width // parts) + 8, width), BF16),
        scratch_shapes=[pltpu.VMEM((2 * samples, width), BF16)],
        compiler_params=pltpu.CompilerParams(vmem_limit_bytes=16 << 20),
        name="messages",
    )(*near, cross_near, solved, far, left, white, rows)


def bands_kernel(samples, where_ref, reach_ref, arrived_ref, out_ref):
    parts = arrived_ref.shape[0]
    share, width = out_ref.shape[1:]
    place = where_ref[0]
    reached = reach_ref[where_ref[1]]
    far, near, weights = [], [], []
    for side in range(2):
        whole = sum(arrived_ref[part].astype(F32) for part in range(side, parts, 2))
        far.append(whole[:share])
        near.append(whole[share : 2 * share])
        spread = [whole[at : at + 1] + whole[at + 1 : at + 2] for at in range(2 * share, 2 * share + 6, 2)]
        weights.append([jnp.sqrt(samples / value) for value in spread])
    row = lax.broadcasted_iota(jnp.int32, (share, width), 0)
    lane = lax.broadcasted_iota(jnp.int32, (share, width), 1)
    mine = lane == row + place * share
    own = jnp.sum(jnp.where(mine, weights[0][0], 0.0), 1, keepdims=True) * (1.0 / math.sqrt(samples))
    slots = [
        (far[1], weights[1][1], 2),
        (near[1], weights[1][2], 1),
        (near[0], weights[0][2], 1),
        (far[0], weights[0][1], 2),
    ]
    for slot, (total, weight, offset) in enumerate(slots):
        live = jnp.full((share, width), reached, jnp.int32) >= offset
        out_ref[slot] = jnp.where(live, total * own * weight, 0.0).astype(BF16)


def bands(where, reach, arrived, samples):
    parts, _, width = arrived.shape
    share = width // parts
    smem = pl.BlockSpec(memory_space=pltpu.SMEM)
    vmem = pl.BlockSpec(memory_space=pltpu.VMEM)
    return pl.pallas_call(
        functools.partial(bands_kernel, samples),
        out_shape=jax.ShapeDtypeStruct((2 * MAXR, share, width), BF16),
        in_specs=[smem, smem, vmem],
        out_specs=vmem,
        compiler_params=pltpu.CompilerParams(vmem_limit_bytes=8 << 20),
        name="bands",
    )(where, reach, arrived)


def exchange(x):
    return lax.all_to_all(x, "sample", 0, 0, tiled=False)


def shards(dosage, covariates, reach):
    local_samples, width = dosage.shape
    parts = lax.axis_size("sample")
    blocks = lax.axis_size("variant")
    half = parts // 2
    samples = local_samples * parts
    place = lax.axis_index("sample")
    core = lax.axis_index("variant") % 2
    side = place % 2
    padded = -(-(covariates.shape[0] + 1) // parts) * parts
    both = ("sample", "variant")

    partner_route = [(i, i ^ 1) for i in range(parts)]
    core_route = [(i, i ^ 1) for i in range(blocks)]
    far_route = []
    for s in range(parts):
        step = MAXR if s % 2 == 0 else -MAXR
        for v in range(blocks):
            far_route.append((s * blocks + (v + step) % blocks, s * blocks + v))

    def from_partner(x):
        return lax.ppermute(x, "sample", partner_route)

    def from_far(x):
        return lax.ppermute(x, both, far_route)

    def for_mate(own, far):
        return jnp.where(core != side, own, far)

    def swap(x):
        return lax.ppermute(x, "variant", core_route)

    def after(x, *earlier):
        return lax.optimization_barrier((x,) + earlier)[0]

    own0 = dosage
    covariates1 = from_partner(covariates)
    message = local_sums(dosage, covariates, padded, parts)
    sent = own0
    own1 = from_partner(sent)
    far0 = from_far(sent)
    chunk = exchange(message).sum(0)
    message = jnp.broadcast_to(chunk[None], (parts,) + chunk.shape)
    message = after(message, own1, far0)
    give0 = for_mate(after(own0, message), far0)
    far1 = from_far(after(own1, give0))
    total = exchange(message).reshape(padded, -1)
    near0, near1 = swap(give0), swap(for_mate(own1, far1))
    cross = total[:, :width]
    cross_far = from_far(cross)
    solved, white, left, own_rows = own_residual((own0, own1), (covariates, covariates1), total)
    cross_near = swap(for_mate(after(cross, left), cross_far))
    tile, spreads = far_tile((far0, far1), cross_far, solved, white, left, own_rows)
    message = messages((near0, near1), cross_near, solved, tile, left, white, spreads, parts)
    where = jnp.stack([place, lax.axis_index("variant")])
    return bands(where, reach, exchange(message), samples)


def solution(mesh):
    placed = (P("sample", "variant"), P(None, "sample"), P())
    return jax.shard_map(
        shards,
        mesh=mesh,
        in_specs=placed,
        out_specs=P(None, ("variant", "sample"), None),
        check_vma=False,
    )
```

time: 98.5 us -> 91.9 us (0.933); the launches traced: 98.1 us -> 90.5 us
  other arithmetic: 9.88 us -> 0.24 us
  Pallas kernels: 6 us -> 10.3 us
  waiting for transfers between devices: 49.6 us -> 52.4 us
  starting transfers between devices: 29.2 us -> 26.7 us
  local copies, waits for them, and re-layouts: 3.15 us -> 0.73 us
    another operation x6 -> x1, other arithmetic: 6.51 us -> 0.08 us  [shards(): where = jnp.stack([place, lax.axis_index('variant')])]
    pallas_call x2 -> x5, Pallas kernels: 6 us -> 10.3 us  [the longest x1 3.27 us: own_residual(): pl.pallas_call(functools.partial(own_kernel, covariates[0].shape[0] + 1),...]
    all_to_all x3, waiting for transfers between devices: 47.3 us -> 49.5 us  [exchange(): return lax.all_to_all(x, 'sample', 0, 0, tiled=False)]
    ppermute x3, waiting for transfers between devices: 1.28 us -> 2.9 us  [from_far(): return lax.ppermute(x, both, far_route)]
    select_n x3, other arithmetic: 1.72 us -> 0.12 us  [for_mate(): return jnp.where(core != side, own, far)]
    reshape x1 -> x0, local copies, waits for them, and re-layouts: 1.56 us -> none  [shards(): local_sums(dosage, covariates, padded).reshape(parts, padded // parts, -1)]
    all_to_all x3, starting transfers between devices: 22.2 us -> 20.8 us  [exchange(): return lax.all_to_all(x, 'sample', 0, 0, tiled=False)]
    ppermute x3, waiting for transfers between devices: 1.02 us -> 0.01 us  [swap(): return lax.ppermute(x, 'variant', core_route)]
  transfers between devices with their start and end apart: 11 -> 11, of which waited for: 5 -> 4; matrix products, arithmetic and copies ran while one was open for 12% -> 0% of each run, Pallas kernels for 2% -> 7%
where the time goes in v4:
time: 91.9 us; the launch traced here: 90.5 us
  waiting for transfers between devices  52.4 us (57%)
  starting transfers between devices  26.7 us (29%)
  Pallas kernels  10.3 us (11%)
    all_to_all x3, waiting for transfers between devices, exchange(): return lax.all_to_all(x, 'sample', 0, 0, tiled=False)  49.5 us
    all_to_all x3, starting transfers between devices, exchange(): return lax.all_to_all(x, 'sample', 0, 0, tiled=False)  20.8 us
    ppermute x2, starting transfers between devices, from_partner(): return lax.ppermute(x, 'sample', partner_route)  3.93 us
    pallas_call x1, Pallas kernels, own_residual(): pl.pallas_call(functools.partial(own_kernel, covariates[0].shape[0] + 1),...  3.27 us
    ppermute x3, waiting for transfers between devices, from_far(): return lax.ppermute(x, both, far_route)  2.9 us
    pallas_call x1, Pallas kernels, messages(): pl.pallas_call(near_kernel, out_shape=jax.ShapeDtypeStruct((parts, 2 * (w...  2.27 us
    pallas_call x1, Pallas kernels, local_sums(): pl.pallas_call(sums_kernel, out_shape=jax.ShapeDtypeStruct((parts, padded...  2.06 us
  transfers between devices with their start and end apart: 11, of which 4 were waited for; matrix products, arithmetic and copies ran while one was open for 0% of the time, Pallas kernels for 7%

profile of v4, /device:TPU:6, one launch (start us, length us, event | category | flops | bytes accessed | tf_op | source)
XLA Modules:
  0.0 90.5 jit_solution(9266007979571994971)
XLA Ops:
  0.0 0.0 copy-start
  0.0 1.9 %collective-permute-start = (bf16[512,512]{1,0:T(8,128)(2,1)}, bf16[512,512]{1,0:T(8,128)(2,1)S(1)}, u32[]{:S(2)}, u32[]{:S(2)}) collective-permute-start(bf16[512,512]{1,0:T(8,128)(2,1)} %own0.1), channel_id=1, source_target_pairs={{0,16},{16,0},{32,48},{48,32},{64,80},{80,64},{96,112},{112,96},{1... | collective-permute-start | bytes 1572872 | tf_op jit(solution)/shard_map/ppermute | solution.py:251
  1.9 0.8 collective-permute-start.1
  2.7 2.1 %local_sums.1 = f32[16,2,640]{2,1,0:T(2,128)} custom-call(bf16[512,512]{1,0:T(8,128)(2,1)} %own0.1, f32[30,512]{1,0:T(8,128)} %cov0.1), custom_call_target="tpu_custom_call" | custom-call | tf_op jit(solution)/shard_map/local_sums/pallas_call | solution.py:57
  4.8 0.0 copy-start.1
  4.8 10.4 %all-to-all-start = ((f32[16,2,640]{2,1,0:T(2,128)}), f32[16,2,640]{2,1,0:T(2,128)S(1)}, u32[]{:S(2)}, u32[]{:S(2)}) async-start(f32[16,2,640]{2,1,0:T(2,128)} %local_sums.1), calls=%async_computation | async-start | bytes 163840 | tf_op jit(solution)/shard_map/all_to_all | solution.py:227
  15.3 10.0 %all-to-all-done = f32[16,2,640]{2,1,0:T(2,128)S(1)} async-done(((f32[16,2,640]{2,1,0:T(2,128)}), f32[16,2,640]{2,1,0:T(2,128)S(1)}, u32[]{:S(2)}, u32[]{:S(2)}) %all-to-all-start) | async-done | bytes 81952 | tf_op jit(solution)/shard_map/all_to_all | solution.py:227
  25.3 0.0 collective-permute-done.own1
  25.3 0.0 collective-permute-done.1.far0
  25.3 0.7 broadcast_in_dim.2
  26.0 0.0 copy-done
  26.0 0.1 broadcast_select_fusion.1
  26.1 0.8 collective-permute-start.3
  26.9 5.3 %all-to-all-start.1 = ((f32[16,2,640]{2,1,0:T(2,128)}), f32[16,2,640]{2,1,0:T(2,128)S(1)}, u32[]{:S(2)}, u32[]{:S(2)}) async-start(f32[16,2,640]{2,1,0:T(2,128)} %broadcast_in_dim.2), calls=%async_computation.1 | async-start | bytes 163840 | tf_op jit(solution)/shard_map/all_to_all | solution.py:227
  32.2 0.0 copy-done.1
  32.2 2.0 %collective-permute-start.5 = (f32[30,512]{1,0:T(8,128)S(1)}, f32[30,512]{1,0:T(8,128)S(1)}, u32[]{:S(2)}, u32[]{:S(2)}) collective-permute-start(f32[30,512]{1,0:T(8,128)S(1)} %copy-done.1), channel_id=1, source_target_pairs={{0,16},{16,0},{32,48},{48,32},{64,80},{80,64},{96,112},{112,96},{1... | collective-permute-start | bytes 184328 | tf_op jit(solution)/shard_map/ppermute | solution.py:251
  34.2 0.0 collective-permute-start.2
  34.2 8.0 %all-to-all-done.1 = f32[16,2,640]{2,1,0:T(2,128)S(1)} async-done(((f32[16,2,640]{2,1,0:T(2,128)}), f32[16,2,640]{2,1,0:T(2,128)S(1)}, u32[]{:S(2)}, u32[]{:S(2)}) %all-to-all-start.1) | async-done | bytes 81952 | tf_op jit(solution)/shard_map/all_to_all | solution.py:227
  42.3 0.1 reshape.4.total
  42.4 0.1 collective-permute-start.6
  42.5 0.0 collective-permute-done.3.far1
  42.5 0.1 broadcast_select_fusion
  42.5 0.1 collective-permute-start.4
  42.6 0.0 collective-permute-done.5.cov1
  42.6 3.3 %own_residual.1 = (f32[32,32]{1,0:T(8,128)S(1)}, bf16[192,1024]{1,0:T(8,128)(2,1)S(1)}, bf16[1024,512]{1,0:T(8,128)(2,1)S(1)}, bf16[2,512]{1,0:T(2,128)(2,1)S(1)}) custom-call(bf16[512,512]{1,0:T(8,128)(2,1)S(1)} %copy-done, bf16[512,512]{1,0:T(8,128)(2,1)S(1)} %collective-permute-done.own1, f32[30,512]{1,0:T(8,128)S(1)} %copy-done.1, ...), custom_call_target="tpu_custom_call" | custom-call | flops 4000000000 | bytes 15000000 | tf_op jit(solution)/shard_map/own_residual/pallas_call | solution.py:143
  45.9 2.9 %collective-permute-done.6.cross_far = f32[32,512]{1,0:T(8,128)S(1)} collective-permute-done((f32[32,512]{1,0:T(8,128)S(1)}, f32[32,512]{1,0:T(8,128)S(1)}, u32[]{:S(2)}, u32[]{:S(2)}) %collective-permute-start.6) | collective-permute-done | bytes 65568 | tf_op jit(solution)/shard_map/ppermute | solution.py:254
  48.8 0.1 collective-permute-start.7
  48.9 1.2 %far_tile.1 = (bf16[512,512]{1,0:T(8,128)(2,1)S(1)}, bf16[4,512]{1,0:T(4,128)(2,1)S(1)}) custom-call(bf16[512,512]{1,0:T(8,128)(2,1)S(1)} %collective-permute-done.1.far0, bf16[512,512]{1,0:T(8,128)(2,1)S(1)} %collective-permute-done.3.far1, f32[32,512]{1,0:T(8,128)S(1)} %collective-permute-done.6.cross_far, f32[32,32]{1,0:T(8,128)S(1)} %get-tuple-element.20.solved, ...), custom_call_target="tpu_custom_call" | custom-call | flops 1000000000 | bytes 6000000 | tf_op jit(solution)/shard_map/far_tile/pallas_call | solution.py:160
  50.2 0.0 collective-permute-done.7.cross_near
  50.2 0.0 collective-permute-done.2.near0
  50.2 0.0 collective-permute-done.4.near1
  50.2 2.3 %messages.1 = bf16[16,72,512]{2,1,0:T(8,128)(2,1)} custom-call(bf16[512,512]{1,0:T(8,128)(2,1)S(1)} %collective-permute-done.2.near0, bf16[512,512]{1,0:T(8,128)(2,1)S(1)} %collective-permute-done.4.near1, f32[32,512]{1,0:T(8,128)S(1)} %collective-permute-done.7.cross_near, f32[32,32]{1,0:T(8,128)S(1)} %get-tuple-element.20.solved, ...), custom_call_target="tpu_custom_call" | custom-call | tf_op jit(solution)/shard_map/messages/pallas_call | solution.py:175
  52.5 0.0 copy-start.2
  52.5 5.1 %all-to-all-start.2 = ((bf16[16,72,512]{2,1,0:T(8,128)(2,1)}), bf16[16,72,512]{2,1,0:T(8,128)(2,1)S(1)}, u32[]{:S(2)}, u32[]{:S(2)}) async-start(bf16[16,72,512]{2,1,0:T(8,128)(2,1)} %messages.1), calls=%async_computation.2 | async-start | bytes 2359296 | tf_op jit(solution)/shard_map/all_to_all | solution.py:227
  57.5 0.1 pad_add_fusion.where_ref
  57.6 31.4 %all-to-all-done.2.arrived_ref = bf16[16,72,512]{2,1,0:T(8,128)(2,1)S(1)} async-done(((bf16[16,72,512]{2,1,0:T(8,128)(2,1)}), bf16[16,72,512]{2,1,0:T(8,128)(2,1)S(1)}, u32[]{:S(2)}, u32[]{:S(2)}) %all-to-all-start.2) | async-done | bytes 1179680 | tf_op jit(solution)/shard_map/all_to_all | solution.py:227
  89.1 0.0 copy-done.2
  89.1 1.4 %bands.1 = bf16[4,32,512]{2,1,0:T(8,128)(2,1)} custom-call(s32[2]{0:T(128)S(1)} %pad_add_fusion.where_ref, s32[16]{0:T(128)S(1)} %copy-done.2, bf16[16,72,512]{2,1,0:T(8,128)(2,1)S(1)} %all-to-all-done.2.arrived_ref), custom_call_target="tpu_custom_call" | custom-call | tf_op jit(solution)/shard_map/bands/pallas_call | solution.py:216
  (3 shorter events, 0.1 us)
Async XLA Ops:
  0.0 26.0 %copy-start = (bf16[512,512]{1,0:T(8,128)(2,1)S(1)}, bf16[512,512]{1,0:T(8,128)(2,1)}, u32[]{:S(2)}) copy-start(bf16[512,512]{1,0:T(8,128)(2,1)} %own0.1) | copy-start | bytes 1572868
  0.0 25.3 %collective-permute-start = (bf16[512,512]{1,0:T(8,128)(2,1)}, bf16[512,512]{1,0:T(8,128)(2,1)S(1)}, u32[]{:S(2)}, u32[]{:S(2)}) collective-permute-start(bf16[512,512]{1,0:T(8,128)(2,1)} %own0.1), channel_id=1, source_target_pairs={{0,16},{16,0},{32,48},{48,32},{64,80},{80,64},{96,112},{112,96},{1... | collective-permute-start | bytes 1572872 | tf_op jit(solution)/shard_map/ppermute | solution.py:251
  1.9 23.4 %collective-permute-start.1 = (bf16[512,512]{1,0:T(8,128)(2,1)}, bf16[512,512]{1,0:T(8,128)(2,1)S(1)}, u32[]{:S(2)}, u32[]{:S(2)}) collective-permute-start(bf16[512,512]{1,0:T(8,128)(2,1)} %own0.1), channel_id=1, source_target_pairs={{2,0},{3,1},{4,2},{5,3},{6,4},{7,5},{8,6},{9,7},{10,8},{11,9},{12,... | collective-permute-start | bytes 1572872 | tf_op jit(solution)/shard_map/ppermute | solution.py:254
  4.8 27.4 %copy-start.1 = (f32[30,512]{1,0:T(8,128)S(1)}, f32[30,512]{1,0:T(8,128)}, u32[]{:S(2)}) copy-start(f32[30,512]{1,0:T(8,128)} %cov0.1) | copy-start | bytes 184324
  4.8 20.5 %all-to-all-start = ((f32[16,2,640]{2,1,0:T(2,128)}), f32[16,2,640]{2,1,0:T(2,128)S(1)}, u32[]{:S(2)}, u32[]{:S(2)}) async-start(f32[16,2,640]{2,1,0:T(2,128)} %local_sums.1), calls=%async_computation | async-start | bytes 163840 | tf_op jit(solution)/shard_map/all_to_all | solution.py:227
  26.1 16.4 %collective-permute-start.3 = (bf16[512,512]{1,0:T(8,128)(2,1)S(1)}, bf16[512,512]{1,0:T(8,128)(2,1)S(1)}, u32[]{:S(2)}, u32[]{:S(2)}) collective-permute-start(bf16[512,512]{1,0:T(8,128)(2,1)S(1)} %collective-permute-done.own1), channel_id=1, source_target_pairs={{2,0},{3,1},{4,2},{5,3},{6,4},{7,5},{8,6},{9,7},{10,8},{11,9},{12,... | collective-permute-start | bytes 1572872 | tf_op jit(solution)/shard_map/ppermute | solution.py:254
  26.9 15.4 %all-to-all-start.1 = ((f32[16,2,640]{2,1,0:T(2,128)}), f32[16,2,640]{2,1,0:T(2,128)S(1)}, u32[]{:S(2)}, u32[]{:S(2)}) async-start(f32[16,2,640]{2,1,0:T(2,128)} %broadcast_in_dim.2), calls=%async_computation.1 | async-start | bytes 163840 | tf_op jit(solution)/shard_map/all_to_all | solution.py:227
  32.2 10.4 %collective-permute-start.5 = (f32[30,512]{1,0:T(8,128)S(1)}, f32[30,512]{1,0:T(8,128)S(1)}, u32[]{:S(2)}, u32[]{:S(2)}) collective-permute-start(f32[30,512]{1,0:T(8,128)S(1)} %copy-done.1), channel_id=1, source_target_pairs={{0,16},{16,0},{32,48},{48,32},{64,80},{80,64},{96,112},{112,96},{1... | collective-permute-start | bytes 184328 | tf_op jit(solution)/shard_map/ppermute | solution.py:251
  34.2 15.9 %collective-permute-start.2 = (bf16[512,512]{1,0:T(8,128)(2,1)S(1)}, bf16[512,512]{1,0:T(8,128)(2,1)S(1)}, u32[]{:S(2)}, u32[]{:S(2)}) collective-permute-start(bf16[512,512]{1,0:T(8,128)(2,1)S(1)} %broadcast_select_fusion.1), channel_id=1, source_target_pairs={{0,1},{1,0},{2,3},{3,2},{4,5},{5,4},{6,7},{7,6},{8,9},{9,8},{10,11... | collective-permute-start | bytes 1572872 | tf_op jit(solution)/shard_map/ppermute | solution.py:260
  42.4 6.5 %collective-permute-start.6 = (f32[32,512]{1,0:T(8,128)S(1)}, f32[32,512]{1,0:T(8,128)S(1)}, u32[]{:S(2)}, u32[]{:S(2)}) collective-permute-start(f32[32,512]{1,0:T(8,128)S(1)} %slice.4), channel_id=1, source_target_pairs={{2,0},{3,1},{4,2},{5,3},{6,4},{7,5},{8,6},{9,7},{10,8},{11,9},{12,... | collective-permute-start | bytes 196616 | tf_op jit(solution)/shard_map/ppermute | solution.py:254
  42.5 7.7 %collective-permute-start.4 = (bf16[512,512]{1,0:T(8,128)(2,1)S(1)}, bf16[512,512]{1,0:T(8,128)(2,1)S(1)}, u32[]{:S(2)}, u32[]{:S(2)}) collective-permute-start(bf16[512,512]{1,0:T(8,128)(2,1)S(1)} %broadcast_select_fusion), channel_id=1, source_target_pairs={{0,1},{1,0},{2,3},{3,2},{4,5},{5,4},{6,7},{7,6},{8,9},{9,8},{10,11... | collective-permute-start | bytes 1572872 | tf_op jit(solution)/shard_map/ppermute | solution.py:260
  48.8 1.3 %collective-permute-start.7 = (f32[32,512]{1,0:T(8,128)S(1)}, f32[32,512]{1,0:T(8,128)S(1)}, u32[]{:S(2)}, u32[]{:S(2)}) collective-permute-start(f32[32,512]{1,0:T(8,128)S(1)} %broadcast_select_fusion.2), channel_id=1, source_target_pairs={{0,1},{1,0},{2,3},{3,2},{4,5},{5,4},{6,7},{7,6},{8,9},{9,8},{10,11... | collective-permute-start | bytes 196616 | tf_op jit(solution)/shard_map/ppermute | solution.py:260
  52.5 36.6 %copy-start.2 = (s32[16]{0:T(128)S(1)}, s32[16]{0:T(128)}, u32[]{:S(2)}) copy-start(s32[16]{0:T(128)} %reach_ref.1) | copy-start | bytes 196
  52.5 36.6 %all-to-all-start.2 = ((bf16[16,72,512]{2,1,0:T(8,128)(2,1)}), bf16[16,72,512]{2,1,0:T(8,128)(2,1)S(1)}, u32[]{:S(2)}, u32[]{:S(2)}) async-start(bf16[16,72,512]{2,1,0:T(8,128)(2,1)} %messages.1), calls=%async_computation.2 | async-start | bytes 2359296 | tf_op jit(solution)/shard_map/all_to_all | solution.py:227

commit v5 on v4

v5 whole, which is shorter than its diff:
```python
import functools
import math

import jax
import jax.numpy as jnp
from jax import lax
from jax.experimental import pallas as pl
from jax.experimental.pallas import tpu as pltpu
from jax.sharding import PartitionSpec as P

MAXR = 2
HIGHEST = lax.Precision.HIGHEST
BF16 = jnp.bfloat16
F32 = jnp.float32
LANES = 128
STEP = 128
COLUMNS_TOGETHER = (((0,), (0,)), ((), ()))


def split(value):
    high = value.astype(BF16)
    rest = value - high.astype(F32)
    middle = rest.astype(BF16)
    low = (rest - middle.astype(F32)).astype(BF16)
    return high, middle, low


def fill_design(design_ref, covariates_ref):
    count = covariates_ref.shape[0]
    design_ref[...] = jnp.zeros_like(design_ref)
    design_ref[:count, :] = covariates_ref[...]
    design_ref[count : count + 1, :] = jnp.ones((1, design_ref.shape[1]), F32)


def sums_kernel(dosage_ref, covariates_ref, out_ref, design_ref):
    fill_design(design_ref, covariates_ref)
    width = dosage_ref.shape[1]
    padded = design_ref.shape[0]
    design = design_ref[...]
    stacked = jnp.concatenate(split(design), 0)
    parts = jnp.dot(stacked, dosage_ref[...], preferred_element_type=F32)
    cross = parts[:padded] + parts[padded : 2 * padded] + parts[2 * padded :]
    moment = lax.dot_general(
        design, design, (((1,), (1,)), ((), ())), precision=HIGHEST, preferred_element_type=F32
    )
    packed = jnp.concatenate([moment[at : at + 8] for at in range(0, padded, 8)], 1)
    each = out_ref.shape[1]
    for part in range(out_ref.shape[0]):
        out_ref[part, :, :width] = cross[part * each : (part + 1) * each]
        for at in range(0, 8, each):
            first = width + at // each * LANES
            out_ref[part, :, first : first + LANES] = packed[at : at + each]


def local_sums(dosage, covariates, padded, parts):
    samples, width = dosage.shape
    return pl.pallas_call(
        sums_kernel,
        out_shape=jax.ShapeDtypeStruct((parts, padded // parts, width + 8 * LANES // (padded // parts)), F32),
        scratch_shapes=[pltpu.VMEM((padded, samples), F32)],
        name="local_sums",
    )(dosage, covariates)


def factor_kernel(count, sums_ref, cov0, cov1, solved_ref, white_ref, design):
    samples = cov0.shape[1]
    padded = solved_ref.shape[0]
    parts, each, total_width = sums_ref.shape
    width = total_width - 8 * LANES // each
    whole = sums_ref[0, :, width:]
    for part in range(1, parts):
        whole = whole + sums_ref[part, :, width:]
    packed = jnp.concatenate([whole[:, at : at + LANES] for at in range(0, whole.shape[1], LANES)], 0)
    first = LANES // 2
    moment = jnp.concatenate(
        [pltpu.roll(packed, (first - group * padded) % LANES, 1) for group in range(padded // 8)], 0
    )
    row = lax.broadcasted_iota(jnp.int32, (padded, LANES), 0)
    lane = lax.broadcasted_iota(jnp.int32, (padded, LANES), 1)
    spare = (row >= count) & (lane == row + first)
    inside = (lane >= first) & (lane < first + padded)
    work = jnp.where(inside, moment, 0.0) + jnp.where((lane == row) | spare, 1.0, 0.0)
    for step in range(count - 1):
        pivot_row = work[step : step + 1, :]
        pivot_row = pivot_row / pivot_row[:, first + step : first + step + 1]
        column = jnp.broadcast_to(work[:, first + step : first + step + 1], work.shape)
        work = work - jnp.where(row > step, column, 0.0) * pivot_row
    diagonal = jnp.sum(jnp.where(lane == row + first, work, 0.0), 1, keepdims=True)
    unit = work[:, :padded]
    solved_ref[...] = unit / diagonal
    fill_design(design.at[:, :samples], cov0)
    fill_design(design.at[:, samples:], cov1)
    h, m, l = split(jnp.dot(unit, design[...], precision=HIGHEST, preferred_element_type=F32))
    white_ref[...] = jnp.concatenate([h, h, m, h, l, m], 0)


def residual(pieces, cross, solved, white, target):
    h, m, l = split(jnp.dot(solved, cross, precision=HIGHEST, preferred_element_type=F32))
    stacked = jnp.concatenate([h, m, h, l, h, m], 0)
    spread = jnp.zeros((1, stacked.shape[1]), F32)
    at = 0
    for piece in pieces:
        for start in range(0, piece.shape[0], STEP):
            fitted = lax.dot_general(
                white[:, at : at + STEP], stacked, COLUMNS_TOGETHER, preferred_element_type=F32
            )
            rest = piece[start : start + STEP, :].astype(F32) - fitted
            spread = spread + jnp.sum(rest * rest, 0, keepdims=True)
            target[at : at + STEP, :] = rest.astype(BF16)
            at += STEP
    return [spread.astype(BF16)]


def tile_of(left, right):
    tile = lax.dot_general(left[...], right[...], COLUMNS_TOGETHER, preferred_element_type=F32)
    return tile.astype(BF16)


def own_kernel(own0, own1, cross, solved, white, left, rows_ref):
    rows = residual((own0, own1), cross[...], solved[...], white[...], left)
    rows_ref[...] = rows[0]


def tiles_kernel(
    far0, far1, near, cross_far, cross_near, solved, white, left, own_rows,
    out_ref, right, far_part, near_part, sems,
):
    width = far0.shape[1]
    parts = out_ref.shape[0]
    share = width // parts
    groups = range(0, width, LANES)
    tall = share * len(groups)

    def sent(buffer, first, count, row, sem):
        return pltpu.make_async_copy(
            buffer.at[first : first + count],
            out_ref.at[first : first + count, row : row + buffer.shape[1], :],
            sems.at[sem],
        )

    def place(tile, index, buffer, part):
        for group, lane in enumerate(groups):
            buffer[part, group * share : (group + 1) * share, :] = tile[
                index * share : (index + 1) * share, lane : lane + LANES
            ]

    rows = [own_rows[...]] + residual((far0, far1), cross_far[...], solved[...], white[...], right)
    tile = tile_of(left, right)
    for part in range(parts):
        place(tile, part, far_part, part)
    copies = [sent(far_part, 0, parts, 0, 0)]
    copies[0].start()
    rows += residual((near.at[0], near.at[1]), cross_near[...], solved[...], white[...], right)
    rows = jnp.concatenate(rows + [jnp.zeros((1, width), BF16)], 0)
    rows = jnp.concatenate([rows[:, lane : lane + LANES] for lane in groups], 0)
    half = parts // 2
    for group in range(2):
        tile = tile_of(left.at[:, group * half * share : (group + 1) * half * share], right)
        for index in range(half):
            part = group * half + index
            place(tile, index, near_part, part)
            near_part[part, tall:, :] = rows
        copies.append(sent(near_part, group * half, half, tall, 1 + group))
        copies[-1].start()
    for copy in copies:
        copy.wait()


def factored(sums, covariates, padded):
    count, samples = covariates[0].shape
    return pl.pallas_call(
        functools.partial(factor_kernel, count + 1),
        out_shape=(
            jax.ShapeDtypeStruct((padded, padded), F32),
            jax.ShapeDtypeStruct((6 * padded, 2 * samples), BF16),
        ),
        scratch_shapes=[pltpu.VMEM((padded, 2 * samples), F32)],
        compiler_params=pltpu.CompilerParams(vmem_limit_bytes=4 << 20),
        cost_estimate=pl.CostEstimate(flops=3_000_000_000, bytes_accessed=10_000_000, transcendentals=0),
        name="factored",
    )(sums, *covariates)


def own_residual(own, cross, solved, white):
    samples, width = own[0].shape
    return pl.pallas_call(
        own_kernel,
        out_shape=(
            jax.ShapeDtypeStruct((2 * samples, width), BF16),
            jax.ShapeDtypeStruct((1, width), BF16),
        ),
        compiler_params=pltpu.CompilerParams(vmem_limit_bytes=8 << 20),
        cost_estimate=pl.CostEstimate(flops=800_000_000, bytes_accessed=4_000_000, transcendentals=0),
        name="own_residual",
    )(*own, cross, solved, white)


def tiles(far, near, cross_far, cross_near, solved, white, left, own_rows, parts):
    samples, width = far[0].shape
    share = width // parts
    tall = share * width // LANES
    extra = 4 * width // LANES
    return pl.pallas_call(
        tiles_kernel,
        out_shape=jax.ShapeDtypeStruct((parts, 2 * tall + extra, LANES), BF16),
        out_specs=pl.BlockSpec(memory_space=pl.ANY),
        scratch_shapes=[
            pltpu.VMEM((2 * samples, width), BF16),
            pltpu.VMEM((parts, tall, LANES), BF16),
            pltpu.VMEM((parts, tall + extra, LANES), BF16),
            pltpu.SemaphoreType.DMA((3,)),
        ],
        compiler_params=pltpu.CompilerParams(vmem_limit_bytes=16 << 20),
        cost_estimate=pl.CostEstimate(flops=2_000_000_000, bytes_accessed=6_000_000, transcendentals=0),
        name="tiles",
    )(*far, near, cross_far, cross_near, solved, white, left, own_rows)


def bands_kernel(samples, where_ref, reach_ref, arrived_ref, out_ref):
    parts = arrived_ref.shape[0]
    share, width = out_ref.shape[1:]
    place = where_ref[0]
    reached = reach_ref[where_ref[1]]
    groups = width // LANES
    tall = share * groups

    def wide(rows, height):
        return jnp.concatenate([rows[g * height : (g + 1) * height] for g in range(groups)], 1)

    far, near, weights = [], [], []
    for side in range(2):
        whole = sum(arrived_ref[part].astype(F32) for part in range(side, parts, 2))
        far.append(wide(whole[:tall], share))
        near.append(wide(whole[tall : 2 * tall], share))
        spread = wide(whole[2 * tall :], 4)
        weights.append([jnp.sqrt(samples / spread[at : at + 1]) for at in range(3)])
    row = lax.broadcasted_iota(jnp.int32, (share, width), 0)
    lane = lax.broadcasted_iota(jnp.int32, (share, width), 1)
    mine = lane == row + place * share
    own = jnp.sum(jnp.where(mine, weights[0][0], 0.0), 1, keepdims=True) * (1.0 / math.sqrt(samples))
    slots = [
        (far[1], weights[1][1], 2),
        (near[1], weights[1][2], 1),
        (near[0], weights[0][2], 1),
        (far[0], weights[0][1], 2),
    ]
    for slot, (total, weight, offset) in enumerate(slots):
        live = jnp.full((share, width), reached, jnp.int32) >= offset
        out_ref[slot] = jnp.where(live, total * own * weight, 0.0).astype(BF16)


def bands(where, reach, arrived, samples, width):
    share = width // arrived.shape[0]
    smem = pl.BlockSpec(memory_space=pltpu.SMEM)
    vmem = pl.BlockSpec(memory_space=pltpu.VMEM)
    return pl.pallas_call(
        functools.partial(bands_kernel, samples),
        out_shape=jax.ShapeDtypeStruct((2 * MAXR, share, width), BF16),
        in_specs=[smem, smem, vmem],
        out_specs=vmem,
        compiler_params=pltpu.CompilerParams(vmem_limit_bytes=8 << 20),
        name="bands",
    )(where, reach, arrived)


def exchange(x):
    return lax.all_to_all(x, "sample", 0, 0, tiled=False)


def shards(dosage, covariates, reach):
    local_samples, width = dosage.shape
    parts = lax.axis_size("sample")
    blocks = lax.axis_size("variant")
    half = parts // 2
    samples = local_samples * parts
    place = lax.axis_index("sample")
    core = lax.axis_index("variant") % 2
    side = place % 2
    padded = -(-(covariates.shape[0] + 1) // parts) * parts
    both = ("sample", "variant")

    partner_route = [(i, i ^ 1) for i in range(parts)]
    core_route = [(i, i ^ 1) for i in range(blocks)]
    far_route = []
    near_route = []
    for s in range(parts):
        step = MAXR if s % 2 == 0 else -MAXR
        for v in range(blocks):
            far_route.append((s * blocks + (v + step) % blocks, s * blocks + v))
            near_route.append((s * blocks + (v + step // MAXR) % blocks, s * blocks + v))

    def from_partner(x):
        return lax.ppermute(x, "sample", partner_route)

    def from_far(x):
        return lax.ppermute(x, both, far_route)

    def for_mate(own, far):
        return jnp.where(core != side, own, far)

    def swap(x):
        return lax.ppermute(x, "variant", core_route)

    def after(x, *earlier):
        return lax.optimization_barrier((x,) + earlier)[0]

    own0 = dosage
    covariates1 = from_partner(covariates)
    message = local_sums(dosage, covariates, padded, parts)
    sent = own0
    own1 = from_partner(sent)
    far0 = from_far(sent)
    sums = exchange(message)
    chunk = sums[:, :, :width].sum(0)
    message = jnp.broadcast_to(chunk[None], (parts,) + chunk.shape)
    message = after(message, own1, far0, covariates1)
    far1 = from_far(after(own1, message))
    cross = exchange(message).reshape(padded, width)
    solved, white = factored(after(sums, message), (covariates, covariates1), padded)
    cross_far = from_far(cross)
    left, own_rows = own_residual((own0, own1), cross, solved, white)
    cross_near = lax.ppermute(cross, both, near_route)
    near = swap(after(for_mate(jnp.stack([own0, own1]), jnp.stack([far0, far1])), left))
    message = tiles(
        (far0, far1), near, cross_far, cross_near, solved, white, left, own_rows, parts
    )
    where = jnp.stack([place, lax.axis_index("variant")])
    return bands(where, reach, exchange(message), samples, width)


def solution(mesh):
    placed = (P("sample", "variant"), P(None, "sample"), P())
    return jax.shard_map(
        shards,
        mesh=mesh,
        in_specs=placed,
        out_specs=P(None, ("variant", "sample"), None),
        check_vma=False,
    )
```

time: 91.9 us -> 89.5 us (0.974); the launches traced: 90.5 us -> 89.1 us
  waiting for transfers between devices: 52.4 us -> 50.6 us
    all_to_all x3, waiting for transfers between devices: 49.5 us -> 44.5 us  [exchange(): return lax.all_to_all(x, 'sample', 0, 0, tiled=False)]
    ppermute x3, waiting for transfers between devices: 2.9 us -> 4.68 us  [from_far(): return lax.ppermute(x, both, far_route)]
    ppermute x0 -> x1, waiting for transfers between devices: none -> 1.39 us  [shards(): cross_near = lax.ppermute(cross, both, near_route)]
    ppermute x3, starting transfers between devices: 1.73 us -> 2.83 us  [from_far(): return lax.ppermute(x, both, far_route)]
  transfers between devices with their start and end apart: 11 -> 10, of which waited for: 4 -> 5; matrix products, arithmetic and copies ran while one was open for 0% -> 0% of each run, Pallas kernels for 7% -> 6%
where the time goes in v5:
time: 89.5 us; the launch traced here: 89.1 us
  waiting for transfers between devices  50.6 us (57%)
  starting transfers between devices  27.2 us (30%)
  Pallas kernels  10.2 us (11%)
    all_to_all x3, waiting for transfers between devices, exchange(): return lax.all_to_all(x, 'sample', 0, 0, tiled=False)  44.5 us
    all_to_all x3, starting transfers between devices, exchange(): return lax.all_to_all(x, 'sample', 0, 0, tiled=False)  20.4 us
    ppermute x3, waiting for transfers between devices, from_far(): return lax.ppermute(x, both, far_route)  4.68 us
    ppermute x2, starting transfers between devices, from_partner(): return lax.ppermute(x, 'sample', partner_route)  3.84 us
    pallas_call x1, Pallas kernels, tiles(): pl.pallas_call(tiles_kernel, out_shape=jax.ShapeDtypeStruct((parts, 2 * t...  3.16 us
    ppermute x3, starting transfers between devices, from_far(): return lax.ppermute(x, both, far_route)  2.83 us
    pallas_call x1, Pallas kernels, factored(): pl.pallas_call(functools.partial(factor_kernel, count + 1), out_shape=(ja...  2.76 us
    pallas_call x1, Pallas kernels, local_sums(): pl.pallas_call(sums_kernel, out_shape=jax.ShapeDtypeStruct((parts, padded...  2.09 us
  transfers between devices with their start and end apart: 10, of which 5 were waited for; matrix products, arithmetic and copies ran while one was open for 0% of the time, Pallas kernels for 6%

profile of v5, /device:TPU:6, one launch (start us, length us, event | category | flops | bytes accessed | tf_op | source)
XLA Modules:
  0.0 89.1 jit_solution(15007409091150087927)
XLA Ops:
  0.0 0.0 copy-start.1
  0.0 1.9 %collective-permute-start.1 = (bf16[512,512]{1,0:T(8,128)(2,1)}, bf16[512,512]{1,0:T(8,128)(2,1)S(1)}, u32[]{:S(2)}, u32[]{:S(2)}) collective-permute-start(bf16[512,512]{1,0:T(8,128)(2,1)} %own0.1), channel_id=1, source_target_pairs={{0,16},{16,0},{32,48},{48,32},{64,80},{80,64},{96,112},{112,96},{1... | collective-permute-start | bytes 1572872 | tf_op jit(solution)/shard_map/ppermute | solution.py:293
  1.9 0.8 collective-permute-start
  2.7 2.1 %local_sums.1 = f32[16,2,1024]{2,1,0:T(2,128)} custom-call(bf16[512,512]{1,0:T(8,128)(2,1)} %own0.1, f32[30,512]{1,0:T(8,128)} %cov0.1), custom_call_target="tpu_custom_call" | custom-call | tf_op jit(solution)/shard_map/local_sums/pallas_call | solution.py:57
  4.8 10.3 %all-to-all-start = ((f32[16,2,1024]{2,1,0:T(2,128)}), f32[16,2,1024]{2,1,0:T(2,128)S(1)}, u32[]{:S(2)}, u32[]{:S(2)}) async-start(f32[16,2,1024]{2,1,0:T(2,128)} %local_sums.1), calls=%async_computation | async-start | bytes 262144 | tf_op jit(solution)/shard_map/all_to_all | solution.py:267
  15.1 1.9 %collective-permute-start.2 = (f32[30,512]{1,0:T(8,128)}, f32[30,512]{1,0:T(8,128)S(1)}, u32[]{:S(2)}, u32[]{:S(2)}) collective-permute-start(f32[30,512]{1,0:T(8,128)} %cov0.1), channel_id=1, source_target_pairs={{0,16},{16,0},{32,48},{48,32},{64,80},{80,64},{96,112},{112,96},{1... | collective-permute-start | bytes 184328 | tf_op jit(solution)/shard_map/ppermute | solution.py:293
  17.1 8.4 %all-to-all-done.sums_ref = f32[16,2,1024]{2,1,0:T(2,128)S(1)} async-done(((f32[16,2,1024]{2,1,0:T(2,128)}), f32[16,2,1024]{2,1,0:T(2,128)S(1)}, u32[]{:S(2)}, u32[]{:S(2)}) %all-to-all-start) | async-done | bytes 131104 | tf_op jit(solution)/shard_map/all_to_all | solution.py:267
  25.5 0.0 collective-permute-done.2.cov1
  25.5 0.0 collective-permute-done.1.own1
  25.5 0.0 collective-permute-done.far0
  25.5 0.6 broadcast_in_dim.2
  26.2 0.7 collective-permute-start.3
  26.9 6.4 %all-to-all-start.1 = ((f32[16,2,512]{2,1,0:T(2,128)}), f32[16,2,512]{2,1,0:T(2,128)S(1)}, u32[]{:S(2)}, u32[]{:S(2)}) async-start(f32[16,2,512]{2,1,0:T(2,128)} %broadcast_in_dim.2), calls=%async_computation.1 | async-start | bytes 131072 | tf_op jit(solution)/shard_map/all_to_all | solution.py:267
  33.3 0.0 copy-done.1
  33.3 0.0 copy-start
  33.3 2.8 %factored.1 = (f32[32,32]{1,0:T(8,128)S(1)}, bf16[192,1024]{1,0:T(8,128)(2,1)S(1)}) custom-call(f32[16,2,1024]{2,1,0:T(2,128)S(1)} %all-to-all-done.sums_ref, f32[30,512]{1,0:T(8,128)S(1)} %copy-done.1, f32[30,512]{1,0:T(8,128)S(1)} %collective-permute-done.2.cov1), custom_call_target="tpu_custom_call" | custom-call | flops 3000000000 | bytes 10000000 | tf_op jit(solution)/shard_map/factored/pallas_call | solution.py:171
  36.1 7.2 %all-to-all-done.1 = f32[16,2,512]{2,1,0:T(2,128)S(1)} async-done(((f32[16,2,512]{2,1,0:T(2,128)}), f32[16,2,512]{2,1,0:T(2,128)S(1)}, u32[]{:S(2)}, u32[]{:S(2)}) %all-to-all-start.1) | async-done | bytes 65568 | tf_op jit(solution)/shard_map/all_to_all | solution.py:267
  43.4 0.0 copy-done
  43.4 0.7 own_residual.1
  44.1 0.0 collective-permute-done.3.far1
  44.1 0.2 maximum_select_fusion
  44.3 0.1 collective-permute-start.4
  44.4 0.1 collective-permute-start.6
  44.5 1.3 %collective-permute-start.5 = (f32[32,512]{1,0:T(8,128)S(1)}, f32[32,512]{1,0:T(8,128)S(1)}, u32[]{:S(2)}, u32[]{:S(2)}) collective-permute-start(f32[32,512]{1,0:T(8,128)S(1)} %reshape.4.cross), channel_id=1, source_target_pairs={{2,0},{3,1},{4,2},{5,3},{6,4},{7,5},{8,6},{9,7},{10,8},{11,9},{12,... | collective-permute-start | bytes 196616 | tf_op jit(solution)/shard_map/ppermute | solution.py:296
  45.7 1.4 %collective-permute-done.6.cross_near = f32[32,512]{1,0:T(8,128)S(1)} collective-permute-done((f32[32,512]{1,0:T(8,128)S(1)}, f32[32,512]{1,0:T(8,128)S(1)}, u32[]{:S(2)}, u32[]{:S(2)}) %collective-permute-start.6) | collective-permute-done | bytes 65568 | tf_op jit(solution)/shard_map/ppermute | solution.py:322
  47.1 4.7 %collective-permute-done.5.cross_far = f32[32,512]{1,0:T(8,128)S(1)} collective-permute-done((f32[32,512]{1,0:T(8,128)S(1)}, f32[32,512]{1,0:T(8,128)S(1)}, u32[]{:S(2)}, u32[]{:S(2)}) %collective-permute-start.5) | collective-permute-done | bytes 65568 | tf_op jit(solution)/shard_map/ppermute | solution.py:296
  51.8 0.0 collective-permute-done.4.near
  51.8 3.2 %tiles.1 = bf16[16,272,128]{2,1,0:T(8,128)(2,1)} custom-call(bf16[512,512]{1,0:T(8,128)(2,1)S(1)} %collective-permute-done.far0, bf16[512,512]{1,0:T(8,128)(2,1)S(1)} %collective-permute-done.3.far1, bf16[2,512,512]{2,1,0:T(8,128)(2,1)S(1)} %collective-permute-done.4.near, f32[32,512]{1,0:T(8,128)S(1)} %collective-permute-done.5.cross_far, ...), custom_call_target="tpu_custom_call" | custom-call | flops 2000000000 | bytes 6000000 | tf_op jit(solution)/shard_map/tiles/pallas_call | solution.py:203
  55.0 0.0 copy-start.2
  55.0 3.7 %all-to-all-start.2 = ((bf16[16,272,128]{2,1,0:T(8,128)(2,1)}), bf16[16,272,128]{2,1,0:T(8,128)(2,1)S(1)}, u32[]{:S(2)}, u32[]{:S(2)}) async-start(bf16[16,272,128]{2,1,0:T(8,128)(2,1)} %tiles.1), calls=%async_computation.2 | async-start | bytes 2228224 | tf_op jit(solution)/shard_map/all_to_all | solution.py:267
  58.7 0.1 pad_add_fusion.where_ref
  58.8 28.9 %all-to-all-done.2.arrived_ref = bf16[16,272,128]{2,1,0:T(8,128)(2,1)S(1)} async-done(((bf16[16,272,128]{2,1,0:T(8,128)(2,1)}), bf16[16,272,128]{2,1,0:T(8,128)(2,1)S(1)}, u32[]{:S(2)}, u32[]{:S(2)}) %all-to-all-start.2) | async-done | bytes 1114144 | tf_op jit(solution)/shard_map/all_to_all | solution.py:267
  87.7 0.0 copy-done.2
  87.7 1.4 %bands.1 = bf16[4,32,512]{2,1,0:T(8,128)(2,1)} custom-call(s32[2]{0:T(128)S(1)} %pad_add_fusion.where_ref, s32[16]{0:T(128)S(1)} %copy-done.2, bf16[16,272,128]{2,1,0:T(8,128)(2,1)S(1)} %all-to-all-done.2.arrived_ref), custom_call_target="tpu_custom_call" | custom-call | tf_op jit(solution)/shard_map/bands/pallas_call | solution.py:256
  (2 shorter events, 0.1 us)
Async XLA Ops:
  0.0 33.3 %copy-start.1 = (f32[30,512]{1,0:T(8,128)S(1)}, f32[30,512]{1,0:T(8,128)}, u32[]{:S(2)}) copy-start(f32[30,512]{1,0:T(8,128)} %cov0.1) | copy-start | bytes 184324
  0.0 25.5 %collective-permute-start.1 = (bf16[512,512]{1,0:T(8,128)(2,1)}, bf16[512,512]{1,0:T(8,128)(2,1)S(1)}, u32[]{:S(2)}, u32[]{:S(2)}) collective-permute-start(bf16[512,512]{1,0:T(8,128)(2,1)} %own0.1), channel_id=1, source_target_pairs={{0,16},{16,0},{32,48},{48,32},{64,80},{80,64},{96,112},{112,96},{1... | collective-permute-start | bytes 1572872 | tf_op jit(solution)/shard_map/ppermute | solution.py:293
  1.9 23.6 %collective-permute-start = (bf16[512,512]{1,0:T(8,128)(2,1)}, bf16[512,512]{1,0:T(8,128)(2,1)S(1)}, u32[]{:S(2)}, u32[]{:S(2)}) collective-permute-start(bf16[512,512]{1,0:T(8,128)(2,1)} %own0.1), channel_id=1, source_target_pairs={{2,0},{3,1},{4,2},{5,3},{6,4},{7,5},{8,6},{9,7},{10,8},{11,9},{12,... | collective-permute-start | bytes 1572872 | tf_op jit(solution)/shard_map/ppermute | solution.py:296
  4.8 20.6 %all-to-all-start = ((f32[16,2,1024]{2,1,0:T(2,128)}), f32[16,2,1024]{2,1,0:T(2,128)S(1)}, u32[]{:S(2)}, u32[]{:S(2)}) async-start(f32[16,2,1024]{2,1,0:T(2,128)} %local_sums.1), calls=%async_computation | async-start | bytes 262144 | tf_op jit(solution)/shard_map/all_to_all | solution.py:267
  15.1 10.3 %collective-permute-start.2 = (f32[30,512]{1,0:T(8,128)}, f32[30,512]{1,0:T(8,128)S(1)}, u32[]{:S(2)}, u32[]{:S(2)}) collective-permute-start(f32[30,512]{1,0:T(8,128)} %cov0.1), channel_id=1, source_target_pairs={{0,16},{16,0},{32,48},{48,32},{64,80},{80,64},{96,112},{112,96},{1... | collective-permute-start | bytes 184328 | tf_op jit(solution)/shard_map/ppermute | solution.py:293
  26.2 17.9 %collective-permute-start.3 = (bf16[512,512]{1,0:T(8,128)(2,1)S(1)}, bf16[512,512]{1,0:T(8,128)(2,1)S(1)}, u32[]{:S(2)}, u32[]{:S(2)}) collective-permute-start(bf16[512,512]{1,0:T(8,128)(2,1)S(1)} %collective-permute-done.1.own1), channel_id=1, source_target_pairs={{2,0},{3,1},{4,2},{5,3},{6,4},{7,5},{8,6},{9,7},{10,8},{11,9},{12,... | collective-permute-start | bytes 1572872 | tf_op jit(solution)/shard_map/ppermute | solution.py:296
  26.9 16.4 %all-to-all-start.1 = ((f32[16,2,512]{2,1,0:T(2,128)}), f32[16,2,512]{2,1,0:T(2,128)S(1)}, u32[]{:S(2)}, u32[]{:S(2)}) async-start(f32[16,2,512]{2,1,0:T(2,128)} %broadcast_in_dim.2), calls=%async_computation.1 | async-start | bytes 131072 | tf_op jit(solution)/shard_map/all_to_all | solution.py:267
  33.3 10.1 %copy-start = (bf16[512,512]{1,0:T(8,128)(2,1)S(1)}, bf16[512,512]{1,0:T(8,128)(2,1)}, u32[]{:S(2)}) copy-start(bf16[512,512]{1,0:T(8,128)(2,1)} %own0.1) | copy-start | bytes 1572868
  44.3 7.5 %collective-permute-start.4 = (bf16[2,512,512]{2,1,0:T(8,128)(2,1)S(1)}, bf16[2,512,512]{2,1,0:T(8,128)(2,1)S(1)}, u32[]{:S(2)}, u32[]{:S(2)}) collective-permute-start(bf16[2,512,512]{2,1,0:T(8,128)(2,1)S(1)} %maximum_select_fusion), channel_id=1, source_target_pairs={{0,1},{1,0},{2,3},{3,2},{4,5},{5,4},{6,7},{7,6},{8,9},{9,8},{10,11... | collective-permute-start | bytes 3145736 | tf_op jit(solution)/shard_map/ppermute | solution.py:302
  44.4 2.7 %collective-permute-start.6 = (f32[32,512]{1,0:T(8,128)S(1)}, f32[32,512]{1,0:T(8,128)S(1)}, u32[]{:S(2)}, u32[]{:S(2)}) collective-permute-start(f32[32,512]{1,0:T(8,128)S(1)} %reshape.4.cross), channel_id=1, source_target_pairs={{1,0},{2,1},{3,2},{4,3},{5,4},{6,5},{7,6},{8,7},{9,8},{10,9},{11,1... | collective-permute-start | bytes 196616 | tf_op jit(solution)/shard_map/ppermute | solution.py:322
  44.5 7.3 %collective-permute-start.5 = (f32[32,512]{1,0:T(8,128)S(1)}, f32[32,512]{1,0:T(8,128)S(1)}, u32[]{:S(2)}, u32[]{:S(2)}) collective-permute-start(f32[32,512]{1,0:T(8,128)S(1)} %reshape.4.cross), channel_id=1, source_target_pairs={{2,0},{3,1},{4,2},{5,3},{6,4},{7,5},{8,6},{9,7},{10,8},{11,9},{12,... | collective-permute-start | bytes 196616 | tf_op jit(solution)/shard_map/ppermute | solution.py:296
  55.0 32.7 %copy-start.2 = (s32[16]{0:T(128)S(1)}, s32[16]{0:T(128)}, u32[]{:S(2)}) copy-start(s32[16]{0:T(128)} %reach_ref.1) | copy-start | bytes 196
  55.0 32.7 %all-to-all-start.2 = ((bf16[16,272,128]{2,1,0:T(8,128)(2,1)}), bf16[16,272,128]{2,1,0:T(8,128)(2,1)S(1)}, u32[]{:S(2)}, u32[]{:S(2)}) async-start(bf16[16,272,128]{2,1,0:T(8,128)(2,1)} %tiles.1), calls=%async_computation.2 | async-start | bytes 2228224 | tf_op jit(solution)/shard_map/all_to_all | solution.py:267

commit v6 on v5

--- a/solution.py
+++ b/solution.py
@@ -13,7 +13,7 @@
 BF16 = jnp.bfloat16
 F32 = jnp.float32
 LANES = 128
-STEP = 128
+STEP = 256
 COLUMNS_TOGETHER = (((0,), (0,)), ((), ()))
 
 
@@ -216,11 +216,9 @@
     )(*far, near, cross_far, cross_near, solved, white, left, own_rows)
 
 
-def bands_kernel(samples, where_ref, reach_ref, arrived_ref, out_ref):
+def bands_kernel(samples, marks_ref, arrived_ref, out_ref):
     parts = arrived_ref.shape[0]
     share, width = out_ref.shape[1:]
-    place = where_ref[0]
-    reached = reach_ref[where_ref[1]]
     groups = width // LANES
     tall = share * groups
 
@@ -235,8 +233,8 @@
         spread = wide(whole[2 * tall :], 4)
         weights.append([jnp.sqrt(samples / spread[at : at + 1]) for at in range(3)])
     row = lax.broadcasted_iota(jnp.int32, (share, width), 0)
-    lane = lax.broadcasted_iota(jnp.int32, (share, width), 1)
-    mine = lane == row + place * share
+    mine = row == marks_ref[0:1, :]
+    reached = marks_ref[1:2, :]
     own = jnp.sum(jnp.where(mine, weights[0][0], 0.0), 1, keepdims=True) * (1.0 / math.sqrt(samples))
     slots = [
         (far[1], weights[1][1], 2),
@@ -245,22 +243,21 @@
         (far[0], weights[0][1], 2),
     ]
     for slot, (total, weight, offset) in enumerate(slots):
-        live = jnp.full((share, width), reached, jnp.int32) >= offset
+        live = reached >= offset
         out_ref[slot] = jnp.where(live, total * own * weight, 0.0).astype(BF16)
 
 
-def bands(where, reach, arrived, samples, width):
+def bands(marks, arrived, samples, width):
     share = width // arrived.shape[0]
-    smem = pl.BlockSpec(memory_space=pltpu.SMEM)
     vmem = pl.BlockSpec(memory_space=pltpu.VMEM)
     return pl.pallas_call(
         functools.partial(bands_kernel, samples),
         out_shape=jax.ShapeDtypeStruct((2 * MAXR, share, width), BF16),
-        in_specs=[smem, smem, vmem],
+        in_specs=[vmem, vmem],
         out_specs=vmem,
         compiler_params=pltpu.CompilerParams(vmem_limit_bytes=8 << 20),
         name="bands",
-    )(where, reach, arrived)
+    )(marks, arrived)
 
 
 def exchange(x):
@@ -306,6 +303,9 @@
 
     own0 = dosage
     covariates1 = from_partner(covariates)
+    reached = reach[lax.axis_index("variant")]
+    lanes = jnp.arange(width, dtype=jnp.int32) - place * (width // parts)
+    marks = jnp.stack([lanes, jnp.full((width,), reached, jnp.int32)])
     message = local_sums(dosage, covariates, padded, parts)
     sent = own0
     own1 = from_partner(sent)
@@ -313,19 +313,18 @@
     sums = exchange(message)
     chunk = sums[:, :, :width].sum(0)
     message = jnp.broadcast_to(chunk[None], (parts,) + chunk.shape)
-    message = after(message, own1, far0, covariates1)
+    message = after(message, own1, far0, covariates1, marks)
     far1 = from_far(after(own1, message))
     cross = exchange(message).reshape(padded, width)
     solved, white = factored(after(sums, message), (covariates, covariates1), padded)
     cross_far = from_far(cross)
-    left, own_rows = own_residual((own0, own1), cross, solved, white)
+    left, own_rows = own_residual((own0, after(own1, far1)), cross, solved, white)
     cross_near = lax.ppermute(cross, both, near_route)
     near = swap(after(for_mate(jnp.stack([own0, own1]), jnp.stack([far0, far1])), left))
     message = tiles(
         (far0, far1), near, cross_far, cross_near, solved, white, left, own_rows, parts
     )
-    where = jnp.stack([place, lax.axis_index("variant")])
-    return bands(where, reach, exchange(message), samples, width)
+    return bands(marks, exchange(message), samples, width)
 
 
 def solution(mesh):

time: 89.5 us -> 90.3 us (level)
  blocking collectives: 0 us -> 34 us
  waiting for transfers between devices: 50.6 us -> 19.8 us
  starting transfers between devices: 27.2 us -> 23.5 us
  local copies, waits for them, and re-layouts: 0.71 us -> 2.6 us
  Pallas kernels: 10.2 us -> 9.18 us
    all_to_all x0 -> x1, blocking collectives: none -> 34 us  [exchange(): return lax.all_to_all(x, 'sample', 0, 0, tiled=False)]
    all_to_all x3 -> x2, waiting for transfers between devices: 44.5 us -> 13.7 us  [exchange(): return lax.all_to_all(x, 'sample', 0, 0, tiled=False)]
    all_to_all x3 -> x2, starting transfers between devices: 20.4 us -> 16.7 us  [exchange(): return lax.all_to_all(x, 'sample', 0, 0, tiled=False)]
    dynamic_slice x0 -> x1, local copies, waits for them, and re-layouts: none -> 1.26 us  [shards(): reached = reach[lax.axis_index('variant')]]
  transfers between devices with their start and end apart: 10 -> 9, of which waited for: 5 -> 4; matrix products, arithmetic and copies ran while one was open for 0% -> 2% of each run, Pallas kernels for 6% -> 5%
where the time goes in v6:
time: 90.3 us; the launch traced here: 89.5 us
  blocking collectives  34 us (38%)
  starting transfers between devices  23.5 us (26%)
  waiting for transfers between devices  19.8 us (22%)
  Pallas kernels  9.18 us (10%)
  local copies, waits for them, and re-layouts  2.6 us (3%)
    all_to_all x1, blocking collectives, exchange(): return lax.all_to_all(x, 'sample', 0, 0, tiled=False)  34 us
    all_to_all x2, starting transfers between devices, exchange(): return lax.all_to_all(x, 'sample', 0, 0, tiled=False)  16.7 us
    all_to_all x2, waiting for transfers between devices, exchange(): return lax.all_to_all(x, 'sample', 0, 0, tiled=False)  13.7 us
    ppermute x3, waiting for transfers between devices, from_far(): return lax.ppermute(x, both, far_route)  4.68 us
    ppermute x2, starting transfers between devices, from_partner(): return lax.ppermute(x, 'sample', partner_route)  3.84 us
    ppermute x3, starting transfers between devices, from_far(): return lax.ppermute(x, both, far_route)  2.83 us
    pallas_call x1, Pallas kernels, factored(): pl.pallas_call(functools.partial(factor_kernel, count + 1), out_shape=(ja...  2.76 us
    pallas_call x1, Pallas kernels, tiles(): pl.pallas_call(tiles_kernel, out_shape=jax.ShapeDtypeStruct((parts, 2 * t...  2.75 us
  transfers between devices with their start and end apart: 9, of which 4 were waited for; matrix products, arithmetic and copies ran while one was open for 2% of the time, Pallas kernels for 5%

profile of v6, /device:TPU:6, one launch (start us, length us, event | category | flops | bytes accessed | tf_op | source)
XLA Modules:
  0.0 89.5 jit_solution(16357911514173658027)
XLA Ops:
  0.0 0.0 copy-start.1
  0.0 1.9 %collective-permute-start.1 = (bf16[512,512]{1,0:T(8,128)(2,1)}, bf16[512,512]{1,0:T(8,128)(2,1)S(1)}, u32[]{:S(2)}, u32[]{:S(2)}) collective-permute-start(bf16[512,512]{1,0:T(8,128)(2,1)} %own0.1), channel_id=1, source_target_pairs={{0,16},{16,0},{32,48},{48,32},{64,80},{80,64},{96,112},{112,96},{1... | collective-permute-start | bytes 1572872 | tf_op jit(solution)/shard_map/ppermute | solution.py:290
  1.9 0.8 collective-permute-start
  2.7 2.1 %local_sums.1 = f32[16,2,1024]{2,1,0:T(2,128)} custom-call(bf16[512,512]{1,0:T(8,128)(2,1)} %own0.1, f32[30,512]{1,0:T(8,128)} %cov0.1), custom_call_target="tpu_custom_call" | custom-call | tf_op jit(solution)/shard_map/local_sums/pallas_call | solution.py:57
  4.8 10.3 %all-to-all-start = ((f32[16,2,1024]{2,1,0:T(2,128)}), f32[16,2,1024]{2,1,0:T(2,128)S(1)}, u32[]{:S(2)}, u32[]{:S(2)}) async-start(f32[16,2,1024]{2,1,0:T(2,128)} %local_sums.1), calls=%async_computation | async-start | bytes 262144 | tf_op jit(solution)/shard_map/all_to_all | solution.py:264
  15.1 1.9 %collective-permute-start.2 = (f32[30,512]{1,0:T(8,128)}, f32[30,512]{1,0:T(8,128)S(1)}, u32[]{:S(2)}, u32[]{:S(2)}) collective-permute-start(f32[30,512]{1,0:T(8,128)} %cov0.1), channel_id=1, source_target_pairs={{0,16},{16,0},{32,48},{48,32},{64,80},{80,64},{96,112},{112,96},{1... | collective-permute-start | bytes 184328 | tf_op jit(solution)/shard_map/ppermute | solution.py:290
  17.1 1.3 %dynamic_slice.3 = s32[1]{0:T(128)} dynamic-slice(s32[16]{0:T(128)} %param.5, s32[]{:T(128)S(6)} %select_n.22), dynamic_slice_sizes={1} | dynamic-slice | bytes 12 | tf_op jit(solution)/shard_map/dynamic_slice | solution.py:306
  18.3 0.6 stack.22.marks_ref
  19.0 6.5 %all-to-all-done.sums_ref = f32[16,2,1024]{2,1,0:T(2,128)S(1)} async-done(((f32[16,2,1024]{2,1,0:T(2,128)}), f32[16,2,1024]{2,1,0:T(2,128)S(1)}, u32[]{:S(2)}, u32[]{:S(2)}) %all-to-all-start) | async-done | bytes 131104 | tf_op jit(solution)/shard_map/all_to_all | solution.py:264
  25.5 0.0 collective-permute-done.2.cov1
  25.5 0.0 collective-permute-done.1.own1
  25.5 0.0 collective-permute-done.far0
  25.5 0.6 broadcast_in_dim.2
  26.2 0.7 collective-permute-start.3
  26.9 6.4 %all-to-all-start.1 = ((f32[16,2,512]{2,1,0:T(2,128)}), f32[16,2,512]{2,1,0:T(2,128)S(1)}, u32[]{:S(2)}, u32[]{:S(2)}) async-start(f32[16,2,512]{2,1,0:T(2,128)} %broadcast_in_dim.2), calls=%async_computation.1 | async-start | bytes 131072 | tf_op jit(solution)/shard_map/all_to_all | solution.py:264
  33.3 0.0 copy-done.1
  33.3 0.0 copy-start
  33.3 2.8 %factored.1 = (f32[32,32]{1,0:T(8,128)S(1)}, bf16[192,1024]{1,0:T(8,128)(2,1)S(1)}) custom-call(f32[16,2,1024]{2,1,0:T(2,128)S(1)} %all-to-all-done.sums_ref, f32[30,512]{1,0:T(8,128)S(1)} %copy-done.1, f32[30,512]{1,0:T(8,128)S(1)} %collective-permute-done.2.cov1), custom_call_target="tpu_custom_call" | custom-call | flops 3000000000 | bytes 10000000 | tf_op jit(solution)/shard_map/factored/pallas_call | solution.py:171
  36.1 7.2 %all-to-all-done.1 = f32[16,2,512]{2,1,0:T(2,128)S(1)} async-done(((f32[16,2,512]{2,1,0:T(2,128)}), f32[16,2,512]{2,1,0:T(2,128)S(1)}, u32[]{:S(2)}, u32[]{:S(2)}) %all-to-all-start.1) | async-done | bytes 65568 | tf_op jit(solution)/shard_map/all_to_all | solution.py:264
  43.4 0.0 collective-permute-done.3.far1
  43.4 0.0 copy-done
  43.4 0.7 own_residual.1
  44.1 0.2 maximum_select_fusion
  44.3 0.1 collective-permute-start.4
  44.4 0.1 collective-permute-start.6
  44.5 1.3 %collective-permute-start.5 = (f32[32,512]{1,0:T(8,128)S(1)}, f32[32,512]{1,0:T(8,128)S(1)}, u32[]{:S(2)}, u32[]{:S(2)}) collective-permute-start(f32[32,512]{1,0:T(8,128)S(1)} %reshape.11.cross), channel_id=1, source_target_pairs={{2,0},{3,1},{4,2},{5,3},{6,4},{7,5},{8,6},{9,7},{10,8},{11,9},{12,... | collective-permute-start | bytes 196616 | tf_op jit(solution)/shard_map/ppermute | solution.py:293
  45.7 1.4 %collective-permute-done.6.cross_near = f32[32,512]{1,0:T(8,128)S(1)} collective-permute-done((f32[32,512]{1,0:T(8,128)S(1)}, f32[32,512]{1,0:T(8,128)S(1)}, u32[]{:S(2)}, u32[]{:S(2)}) %collective-permute-start.6) | collective-permute-done | bytes 65568 | tf_op jit(solution)/shard_map/ppermute | solution.py:322
  47.1 4.7 %collective-permute-done.5.cross_far = f32[32,512]{1,0:T(8,128)S(1)} collective-permute-done((f32[32,512]{1,0:T(8,128)S(1)}, f32[32,512]{1,0:T(8,128)S(1)}, u32[]{:S(2)}, u32[]{:S(2)}) %collective-permute-start.5) | collective-permute-done | bytes 65568 | tf_op jit(solution)/shard_map/ppermute | solution.py:293
  51.8 0.0 collective-permute-done.4.near
  51.8 2.8 %tiles.1 = bf16[16,272,128]{2,1,0:T(8,128)(2,1)S(1)} custom-call(bf16[512,512]{1,0:T(8,128)(2,1)S(1)} %collective-permute-done.far0, bf16[512,512]{1,0:T(8,128)(2,1)S(1)} %collective-permute-done.3.far1, bf16[2,512,512]{2,1,0:T(8,128)(2,1)S(1)} %collective-permute-done.4.near, f32[32,512]{1,0:T(8,128)S(1)} %collective-permute-done.5.cross_far, ...), custom_call_target="tpu_custom_call" | custom-call | flops 2000000000 | bytes 6000000 | tf_op jit(solution)/shard_map/tiles/pallas_call | solution.py:203
  54.5 34.0 %all_to_all.15.arrived_ref = bf16[16,272,128]{2,1,0:T(8,128)(2,1)S(1)} all-to-all(bf16[16,272,128]{2,1,0:T(8,128)(2,1)S(1)} %tiles.1), channel_id=1, replica_groups=mesh['sample'=16,'variant'=16] {'sample'}, dimensions={0} | all-to-all | bytes 2228224 | tf_op jit(solution)/shard_map/all_to_all | solution.py:264
  88.6 0.9 bands.1
  (3 shorter events, 0.1 us)
Async XLA Ops:
  0.0 33.3 %copy-start.1 = (f32[30,512]{1,0:T(8,128)S(1)}, f32[30,512]{1,0:T(8,128)}, u32[]{:S(2)}) copy-start(f32[30,512]{1,0:T(8,128)} %cov0.1) | copy-start | bytes 184324
  0.0 25.5 %collective-permute-start.1 = (bf16[512,512]{1,0:T(8,128)(2,1)}, bf16[512,512]{1,0:T(8,128)(2,1)S(1)}, u32[]{:S(2)}, u32[]{:S(2)}) collective-permute-start(bf16[512,512]{1,0:T(8,128)(2,1)} %own0.1), channel_id=1, source_target_pairs={{0,16},{16,0},{32,48},{48,32},{64,80},{80,64},{96,112},{112,96},{1... | collective-permute-start | bytes 1572872 | tf_op jit(solution)/shard_map/ppermute | solution.py:290
  1.9 23.6 %collective-permute-start = (bf16[512,512]{1,0:T(8,128)(2,1)}, bf16[512,512]{1,0:T(8,128)(2,1)S(1)}, u32[]{:S(2)}, u32[]{:S(2)}) collective-permute-start(bf16[512,512]{1,0:T(8,128)(2,1)} %own0.1), channel_id=1, source_target_pairs={{2,0},{3,1},{4,2},{5,3},{6,4},{7,5},{8,6},{9,7},{10,8},{11,9},{12,... | collective-permute-start | bytes 1572872 | tf_op jit(solution)/shard_map/ppermute | solution.py:293
  4.8 20.6 %all-to-all-start = ((f32[16,2,1024]{2,1,0:T(2,128)}), f32[16,2,1024]{2,1,0:T(2,128)S(1)}, u32[]{:S(2)}, u32[]{:S(2)}) async-start(f32[16,2,1024]{2,1,0:T(2,128)} %local_sums.1), calls=%async_computation | async-start | bytes 262144 | tf_op jit(solution)/shard_map/all_to_all | solution.py:264
  15.1 10.3 %collective-permute-start.2 = (f32[30,512]{1,0:T(8,128)}, f32[30,512]{1,0:T(8,128)S(1)}, u32[]{:S(2)}, u32[]{:S(2)}) collective-permute-start(f32[30,512]{1,0:T(8,128)} %cov0.1), channel_id=1, source_target_pairs={{0,16},{16,0},{32,48},{48,32},{64,80},{80,64},{96,112},{112,96},{1... | collective-permute-start | bytes 184328 | tf_op jit(solution)/shard_map/ppermute | solution.py:290
  26.2 17.2 %collective-permute-start.3 = (bf16[512,512]{1,0:T(8,128)(2,1)S(1)}, bf16[512,512]{1,0:T(8,128)(2,1)S(1)}, u32[]{:S(2)}, u32[]{:S(2)}) collective-permute-start(bf16[512,512]{1,0:T(8,128)(2,1)S(1)} %collective-permute-done.1.own1), channel_id=1, source_target_pairs={{2,0},{3,1},{4,2},{5,3},{6,4},{7,5},{8,6},{9,7},{10,8},{11,9},{12,... | collective-permute-start | bytes 1572872 | tf_op jit(solution)/shard_map/ppermute | solution.py:293
  26.9 16.4 %all-to-all-start.1 = ((f32[16,2,512]{2,1,0:T(2,128)}), f32[16,2,512]{2,1,0:T(2,128)S(1)}, u32[]{:S(2)}, u32[]{:S(2)}) async-start(f32[16,2,512]{2,1,0:T(2,128)} %broadcast_in_dim.2), calls=%async_computation.1 | async-start | bytes 131072 | tf_op jit(solution)/shard_map/all_to_all | solution.py:264
  33.3 10.1 %copy-start = (bf16[512,512]{1,0:T(8,128)(2,1)S(1)}, bf16[512,512]{1,0:T(8,128)(2,1)}, u32[]{:S(2)}) copy-start(bf16[512,512]{1,0:T(8,128)(2,1)} %own0.1) | copy-start | bytes 1572868
  44.3 7.5 %collective-permute-start.4 = (bf16[2,512,512]{2,1,0:T(8,128)(2,1)S(1)}, bf16[2,512,512]{2,1,0:T(8,128)(2,1)S(1)}, u32[]{:S(2)}, u32[]{:S(2)}) collective-permute-start(bf16[2,512,512]{2,1,0:T(8,128)(2,1)S(1)} %maximum_select_fusion), channel_id=1, source_target_pairs={{0,1},{1,0},{2,3},{3,2},{4,5},{5,4},{6,7},{7,6},{8,9},{9,8},{10,11... | collective-permute-start | bytes 3145736 | tf_op jit(solution)/shard_map/ppermute | solution.py:299
  44.4 2.7 %collective-permute-start.6 = (f32[32,512]{1,0:T(8,128)S(1)}, f32[32,512]{1,0:T(8,128)S(1)}, u32[]{:S(2)}, u32[]{:S(2)}) collective-permute-start(f32[32,512]{1,0:T(8,128)S(1)} %reshape.11.cross), channel_id=1, source_target_pairs={{1,0},{2,1},{3,2},{4,3},{5,4},{6,5},{7,6},{8,7},{9,8},{10,9},{11,1... | collective-permute-start | bytes 196616 | tf_op jit(solution)/shard_map/ppermute | solution.py:322
  44.5 7.3 %collective-permute-start.5 = (f32[32,512]{1,0:T(8,128)S(1)}, f32[32,512]{1,0:T(8,128)S(1)}, u32[]{:S(2)}, u32[]{:S(2)}) collective-permute-start(f32[32,512]{1,0:T(8,128)S(1)} %reshape.11.cross), channel_id=1, source_target_pairs={{2,0},{3,1},{4,2},{5,3},{6,4},{7,5},{8,6},{9,7},{10,8},{11,9},{12,... | collective-permute-start | bytes 196616 | tf_op jit(solution)/shard_map/ppermute | solution.py:293

commit v7 on v5

--- a/solution.py
+++ b/solution.py
@@ -32,17 +32,23 @@
     design_ref[count : count + 1, :] = jnp.ones((1, design_ref.shape[1]), F32)
 
 
-def sums_kernel(dosage_ref, covariates_ref, out_ref, design_ref):
+def sums_kernel(dosage_hbm, covariates_hbm, out_ref, design_ref, dosage_ref, covariates_ref, sems):
+    dosage_copy = pltpu.make_async_copy(dosage_hbm, dosage_ref, sems.at[0])
+    covariates_copy = pltpu.make_async_copy(covariates_hbm, covariates_ref, sems.at[1])
+    dosage_copy.start()
+    covariates_copy.start()
+    covariates_copy.wait()
     fill_design(design_ref, covariates_ref)
     width = dosage_ref.shape[1]
     padded = design_ref.shape[0]
     design = design_ref[...]
     stacked = jnp.concatenate(split(design), 0)
-    parts = jnp.dot(stacked, dosage_ref[...], preferred_element_type=F32)
-    cross = parts[:padded] + parts[padded : 2 * padded] + parts[2 * padded :]
     moment = lax.dot_general(
         design, design, (((1,), (1,)), ((), ())), precision=HIGHEST, preferred_element_type=F32
     )
+    dosage_copy.wait()
+    parts = jnp.dot(stacked, dosage_ref[...], preferred_element_type=F32)
+    cross = parts[:padded] + parts[padded : 2 * padded] + parts[2 * padded :]
     packed = jnp.concatenate([moment[at : at + 8] for at in range(0, padded, 8)], 1)
     each = out_ref.shape[1]
     for part in range(out_ref.shape[0]):
@@ -57,7 +63,13 @@
     return pl.pallas_call(
         sums_kernel,
         out_shape=jax.ShapeDtypeStruct((parts, padded // parts, width + 8 * LANES // (padded // parts)), F32),
-        scratch_shapes=[pltpu.VMEM((padded, samples), F32)],
+        in_specs=[pl.BlockSpec(memory_space=pl.ANY)] * 2,
+        scratch_shapes=[
+            pltpu.VMEM((padded, samples), F32),
+            pltpu.VMEM(dosage.shape, BF16),
+            pltpu.VMEM(covariates.shape, F32),
+            pltpu.SemaphoreType.DMA((2,)),
+        ],
         name="local_sums",
     )(dosage, covariates)
 

time: 89.5 us -> 89.5 us (level)
  no operation moved by 1% of the time
where the time goes in v7:
time: 89.5 us; the launch traced here: 89.2 us
  waiting for transfers between devices  50.6 us (57%)
  starting transfers between devices  27.2 us (30%)
  Pallas kernels  10.2 us (11%)
    all_to_all x3, waiting for transfers between devices, exchange(): return lax.all_to_all(x, 'sample', 0, 0, tiled=False)  44.5 us
    all_to_all x3, starting transfers between devices, exchange(): return lax.all_to_all(x, 'sample', 0, 0, tiled=False)  20.4 us
    ppermute x3, waiting for transfers between devices, from_far(): return lax.ppermute(x, both, far_route)  4.68 us
    ppermute x2, starting transfers between devices, from_partner(): return lax.ppermute(x, 'sample', partner_route)  3.84 us
    pallas_call x1, Pallas kernels, tiles(): pl.pallas_call(tiles_kernel, out_shape=jax.ShapeDtypeStruct((parts, 2 * t...  3.15 us
    ppermute x3, starting transfers between devices, from_far(): return lax.ppermute(x, both, far_route)  2.83 us
    pallas_call x1, Pallas kernels, factored(): pl.pallas_call(functools.partial(factor_kernel, count + 1), out_shape=(ja...  2.78 us
    pallas_call x1, Pallas kernels, local_sums(): pl.pallas_call(sums_kernel, out_shape=jax.ShapeDtypeStruct((parts, padded...  2.17 us
  transfers between devices with their start and end apart: 10, of which 5 were waited for; matrix products, arithmetic and copies ran while one was open for 0% of the time, Pallas kernels for 6%

profile of v7, /device:TPU:6, one launch (start us, length us, event | category | flops | bytes accessed | tf_op | source)
XLA Modules:
  0.0 89.2 jit_solution(3608417221670698673)
XLA Ops:
  0.0 0.0 copy-start.1
  0.0 1.9 %collective-permute-start.1 = (bf16[512,512]{1,0:T(8,128)(2,1)}, bf16[512,512]{1,0:T(8,128)(2,1)S(1)}, u32[]{:S(2)}, u32[]{:S(2)}) collective-permute-start(bf16[512,512]{1,0:T(8,128)(2,1)} %own0.1), channel_id=1, source_target_pairs={{0,16},{16,0},{32,48},{48,32},{64,80},{80,64},{96,112},{112,96},{1... | collective-permute-start | bytes 1572872 | tf_op jit(solution)/shard_map/ppermute | solution.py:305
  1.9 0.8 collective-permute-start
  2.7 2.2 %local_sums.1 = f32[16,2,1024]{2,1,0:T(2,128)} custom-call(bf16[512,512]{1,0:T(8,128)(2,1)} %own0.1, f32[30,512]{1,0:T(8,128)} %cov0.1), custom_call_target="tpu_custom_call" | custom-call | tf_op jit(solution)/shard_map/local_sums/pallas_call | solution.py:63
  4.9 10.3 %all-to-all-start = ((f32[16,2,1024]{2,1,0:T(2,128)}), f32[16,2,1024]{2,1,0:T(2,128)S(1)}, u32[]{:S(2)}, u32[]{:S(2)}) async-start(f32[16,2,1024]{2,1,0:T(2,128)} %local_sums.1), calls=%async_computation | async-start | bytes 262144 | tf_op jit(solution)/shard_map/all_to_all | solution.py:279
  15.2 1.9 %collective-permute-start.2 = (f32[30,512]{1,0:T(8,128)}, f32[30,512]{1,0:T(8,128)S(1)}, u32[]{:S(2)}, u32[]{:S(2)}) collective-permute-start(f32[30,512]{1,0:T(8,128)} %cov0.1), channel_id=1, source_target_pairs={{0,16},{16,0},{32,48},{48,32},{64,80},{80,64},{96,112},{112,96},{1... | collective-permute-start | bytes 184328 | tf_op jit(solution)/shard_map/ppermute | solution.py:305
  17.2 8.4 %all-to-all-done.sums_ref = f32[16,2,1024]{2,1,0:T(2,128)S(1)} async-done(((f32[16,2,1024]{2,1,0:T(2,128)}), f32[16,2,1024]{2,1,0:T(2,128)S(1)}, u32[]{:S(2)}, u32[]{:S(2)}) %all-to-all-start) | async-done | bytes 131104 | tf_op jit(solution)/shard_map/all_to_all | solution.py:279
  25.6 0.0 collective-permute-done.2.cov1
  25.6 0.0 collective-permute-done.1.own1
  25.6 0.0 collective-permute-done.far0
  25.6 0.6 broadcast_in_dim.2
  26.3 0.7 collective-permute-start.3
  27.0 6.4 %all-to-all-start.1 = ((f32[16,2,512]{2,1,0:T(2,128)}), f32[16,2,512]{2,1,0:T(2,128)S(1)}, u32[]{:S(2)}, u32[]{:S(2)}) async-start(f32[16,2,512]{2,1,0:T(2,128)} %broadcast_in_dim.2), calls=%async_computation.1 | async-start | bytes 131072 | tf_op jit(solution)/shard_map/all_to_all | solution.py:279
  33.4 0.0 copy-done.1
  33.4 0.0 copy-start
  33.4 2.8 %factored.1 = (f32[32,32]{1,0:T(8,128)S(1)}, bf16[192,1024]{1,0:T(8,128)(2,1)S(1)}) custom-call(f32[16,2,1024]{2,1,0:T(2,128)S(1)} %all-to-all-done.sums_ref, f32[30,512]{1,0:T(8,128)S(1)} %copy-done.1, f32[30,512]{1,0:T(8,128)S(1)} %collective-permute-done.2.cov1), custom_call_target="tpu_custom_call" | custom-call | flops 3000000000 | bytes 10000000 | tf_op jit(solution)/shard_map/factored/pallas_call | solution.py:183
  36.2 7.2 %all-to-all-done.1 = f32[16,2,512]{2,1,0:T(2,128)S(1)} async-done(((f32[16,2,512]{2,1,0:T(2,128)}), f32[16,2,512]{2,1,0:T(2,128)S(1)}, u32[]{:S(2)}, u32[]{:S(2)}) %all-to-all-start.1) | async-done | bytes 65568 | tf_op jit(solution)/shard_map/all_to_all | solution.py:279
  43.5 0.0 copy-done
  43.5 0.7 own_residual.1
  44.2 0.0 collective-permute-done.3.far1
  44.2 0.2 maximum_select_fusion
  44.4 0.1 collective-permute-start.4
  44.5 0.1 collective-permute-start.6
  44.6 1.3 %collective-permute-start.5 = (f32[32,512]{1,0:T(8,128)S(1)}, f32[32,512]{1,0:T(8,128)S(1)}, u32[]{:S(2)}, u32[]{:S(2)}) collective-permute-start(f32[32,512]{1,0:T(8,128)S(1)} %reshape.4.cross), channel_id=1, source_target_pairs={{2,0},{3,1},{4,2},{5,3},{6,4},{7,5},{8,6},{9,7},{10,8},{11,9},{12,... | collective-permute-start | bytes 196616 | tf_op jit(solution)/shard_map/ppermute | solution.py:308
  45.8 1.4 %collective-permute-done.6.cross_near = f32[32,512]{1,0:T(8,128)S(1)} collective-permute-done((f32[32,512]{1,0:T(8,128)S(1)}, f32[32,512]{1,0:T(8,128)S(1)}, u32[]{:S(2)}, u32[]{:S(2)}) %collective-permute-start.6) | collective-permute-done | bytes 65568 | tf_op jit(solution)/shard_map/ppermute | solution.py:334
  47.2 4.7 %collective-permute-done.5.cross_far = f32[32,512]{1,0:T(8,128)S(1)} collective-permute-done((f32[32,512]{1,0:T(8,128)S(1)}, f32[32,512]{1,0:T(8,128)S(1)}, u32[]{:S(2)}, u32[]{:S(2)}) %collective-permute-start.5) | collective-permute-done | bytes 65568 | tf_op jit(solution)/shard_map/ppermute | solution.py:308
  51.9 0.0 collective-permute-done.4.near
  51.9 3.2 %tiles.1 = bf16[16,272,128]{2,1,0:T(8,128)(2,1)} custom-call(bf16[512,512]{1,0:T(8,128)(2,1)S(1)} %collective-permute-done.far0, bf16[512,512]{1,0:T(8,128)(2,1)S(1)} %collective-permute-done.3.far1, bf16[2,512,512]{2,1,0:T(8,128)(2,1)S(1)} %collective-permute-done.4.near, f32[32,512]{1,0:T(8,128)S(1)} %collective-permute-done.5.cross_far, ...), custom_call_target="tpu_custom_call" | custom-call | flops 2000000000 | bytes 6000000 | tf_op jit(solution)/shard_map/tiles/pallas_call | solution.py:215
  55.1 0.0 copy-start.2
  55.1 3.7 %all-to-all-start.2 = ((bf16[16,272,128]{2,1,0:T(8,128)(2,1)}), bf16[16,272,128]{2,1,0:T(8,128)(2,1)S(1)}, u32[]{:S(2)}, u32[]{:S(2)}) async-start(bf16[16,272,128]{2,1,0:T(8,128)(2,1)} %tiles.1), calls=%async_computation.2 | async-start | bytes 2228224 | tf_op jit(solution)/shard_map/all_to_all | solution.py:279
  58.8 0.1 pad_add_fusion.where_ref
  58.9 28.9 %all-to-all-done.2.arrived_ref = bf16[16,272,128]{2,1,0:T(8,128)(2,1)S(1)} async-done(((bf16[16,272,128]{2,1,0:T(8,128)(2,1)}), bf16[16,272,128]{2,1,0:T(8,128)(2,1)S(1)}, u32[]{:S(2)}, u32[]{:S(2)}) %all-to-all-start.2) | async-done | bytes 1114144 | tf_op jit(solution)/shard_map/all_to_all | solution.py:279
  87.8 0.0 copy-done.2
  87.8 1.4 %bands.1 = bf16[4,32,512]{2,1,0:T(8,128)(2,1)} custom-call(s32[2]{0:T(128)S(1)} %pad_add_fusion.where_ref, s32[16]{0:T(128)S(1)} %copy-done.2, bf16[16,272,128]{2,1,0:T(8,128)(2,1)S(1)} %all-to-all-done.2.arrived_ref), custom_call_target="tpu_custom_call" | custom-call | tf_op jit(solution)/shard_map/bands/pallas_call | solution.py:268
  (2 shorter events, 0.1 us)
Async XLA Ops:
  0.0 33.4 %copy-start.1 = (f32[30,512]{1,0:T(8,128)S(1)}, f32[30,512]{1,0:T(8,128)}, u32[]{:S(2)}) copy-start(f32[30,512]{1,0:T(8,128)} %cov0.1) | copy-start | bytes 184324
  0.0 25.6 %collective-permute-start.1 = (bf16[512,512]{1,0:T(8,128)(2,1)}, bf16[512,512]{1,0:T(8,128)(2,1)S(1)}, u32[]{:S(2)}, u32[]{:S(2)}) collective-permute-start(bf16[512,512]{1,0:T(8,128)(2,1)} %own0.1), channel_id=1, source_target_pairs={{0,16},{16,0},{32,48},{48,32},{64,80},{80,64},{96,112},{112,96},{1... | collective-permute-start | bytes 1572872 | tf_op jit(solution)/shard_map/ppermute | solution.py:305
  1.9 23.7 %collective-permute-start = (bf16[512,512]{1,0:T(8,128)(2,1)}, bf16[512,512]{1,0:T(8,128)(2,1)S(1)}, u32[]{:S(2)}, u32[]{:S(2)}) collective-permute-start(bf16[512,512]{1,0:T(8,128)(2,1)} %own0.1), channel_id=1, source_target_pairs={{2,0},{3,1},{4,2},{5,3},{6,4},{7,5},{8,6},{9,7},{10,8},{11,9},{12,... | collective-permute-start | bytes 1572872 | tf_op jit(solution)/shard_map/ppermute | solution.py:308
  4.9 20.6 %all-to-all-start = ((f32[16,2,1024]{2,1,0:T(2,128)}), f32[16,2,1024]{2,1,0:T(2,128)S(1)}, u32[]{:S(2)}, u32[]{:S(2)}) async-start(f32[16,2,1024]{2,1,0:T(2,128)} %local_sums.1), calls=%async_computation | async-start | bytes 262144 | tf_op jit(solution)/shard_map/all_to_all | solution.py:279
  15.2 10.3 %collective-permute-start.2 = (f32[30,512]{1,0:T(8,128)}, f32[30,512]{1,0:T(8,128)S(1)}, u32[]{:S(2)}, u32[]{:S(2)}) collective-permute-start(f32[30,512]{1,0:T(8,128)} %cov0.1), channel_id=1, source_target_pairs={{0,16},{16,0},{32,48},{48,32},{64,80},{80,64},{96,112},{112,96},{1... | collective-permute-start | bytes 184328 | tf_op jit(solution)/shard_map/ppermute | solution.py:305
  26.3 17.9 %collective-permute-start.3 = (bf16[512,512]{1,0:T(8,128)(2,1)S(1)}, bf16[512,512]{1,0:T(8,128)(2,1)S(1)}, u32[]{:S(2)}, u32[]{:S(2)}) collective-permute-start(bf16[512,512]{1,0:T(8,128)(2,1)S(1)} %collective-permute-done.1.own1), channel_id=1, source_target_pairs={{2,0},{3,1},{4,2},{5,3},{6,4},{7,5},{8,6},{9,7},{10,8},{11,9},{12,... | collective-permute-start | bytes 1572872 | tf_op jit(solution)/shard_map/ppermute | solution.py:308
  27.0 16.4 %all-to-all-start.1 = ((f32[16,2,512]{2,1,0:T(2,128)}), f32[16,2,512]{2,1,0:T(2,128)S(1)}, u32[]{:S(2)}, u32[]{:S(2)}) async-start(f32[16,2,512]{2,1,0:T(2,128)} %broadcast_in_dim.2), calls=%async_computation.1 | async-start | bytes 131072 | tf_op jit(solution)/shard_map/all_to_all | solution.py:279
  33.4 10.1 %copy-start = (bf16[512,512]{1,0:T(8,128)(2,1)S(1)}, bf16[512,512]{1,0:T(8,128)(2,1)}, u32[]{:S(2)}) copy-start(bf16[512,512]{1,0:T(8,128)(2,1)} %own0.1) | copy-start | bytes 1572868
  44.4 7.5 %collective-permute-start.4 = (bf16[2,512,512]{2,1,0:T(8,128)(2,1)S(1)}, bf16[2,512,512]{2,1,0:T(8,128)(2,1)S(1)}, u32[]{:S(2)}, u32[]{:S(2)}) collective-permute-start(bf16[2,512,512]{2,1,0:T(8,128)(2,1)S(1)} %maximum_select_fusion), channel_id=1, source_target_pairs={{0,1},{1,0},{2,3},{3,2},{4,5},{5,4},{6,7},{7,6},{8,9},{9,8},{10,11... | collective-permute-start | bytes 3145736 | tf_op jit(solution)/shard_map/ppermute | solution.py:314
  44.5 2.7 %collective-permute-start.6 = (f32[32,512]{1,0:T(8,128)S(1)}, f32[32,512]{1,0:T(8,128)S(1)}, u32[]{:S(2)}, u32[]{:S(2)}) collective-permute-start(f32[32,512]{1,0:T(8,128)S(1)} %reshape.4.cross), channel_id=1, source_target_pairs={{1,0},{2,1},{3,2},{4,3},{5,4},{6,5},{7,6},{8,7},{9,8},{10,9},{11,1... | collective-permute-start | bytes 196616 | tf_op jit(solution)/shard_map/ppermute | solution.py:334
  44.6 7.3 %collective-permute-start.5 = (f32[32,512]{1,0:T(8,128)S(1)}, f32[32,512]{1,0:T(8,128)S(1)}, u32[]{:S(2)}, u32[]{:S(2)}) collective-permute-start(f32[32,512]{1,0:T(8,128)S(1)} %reshape.4.cross), channel_id=1, source_target_pairs={{2,0},{3,1},{4,2},{5,3},{6,4},{7,5},{8,6},{9,7},{10,8},{11,9},{12,... | collective-permute-start | bytes 196616 | tf_op jit(solution)/shard_map/ppermute | solution.py:308
  55.1 32.7 %copy-start.2 = (s32[16]{0:T(128)S(1)}, s32[16]{0:T(128)}, u32[]{:S(2)}) copy-start(s32[16]{0:T(128)} %reach_ref.1) | copy-start | bytes 196
  55.1 32.7 %all-to-all-start.2 = ((bf16[16,272,128]{2,1,0:T(8,128)(2,1)}), bf16[16,272,128]{2,1,0:T(8,128)(2,1)S(1)}, u32[]{:S(2)}, u32[]{:S(2)}) async-start(bf16[16,272,128]{2,1,0:T(8,128)(2,1)} %tiles.1), calls=%async_computation.2 | async-start | bytes 2228224 | tf_op jit(solution)/shard_map/all_to_all | solution.py:279

commit v8 on v6

--- a/solution.py
+++ b/solution.py
@@ -13,7 +13,7 @@
 BF16 = jnp.bfloat16
 F32 = jnp.float32
 LANES = 128
-STEP = 256
+STEP = 128
 COLUMNS_TOGETHER = (((0,), (0,)), ((), ()))
 
 
@@ -247,9 +247,11 @@
         out_ref[slot] = jnp.where(live, total * own * weight, 0.0).astype(BF16)
 
 
-def bands(marks, arrived, samples, width):
+def bands(place, reached, arrived, samples, width):
     share = width // arrived.shape[0]
     vmem = pl.BlockSpec(memory_space=pltpu.VMEM)
+    lanes = jnp.arange(width, dtype=jnp.int32) - place * share
+    marks = jnp.stack([lanes, jnp.full((width,), reached, jnp.int32)])
     return pl.pallas_call(
         functools.partial(bands_kernel, samples),
         out_shape=jax.ShapeDtypeStruct((2 * MAXR, share, width), BF16),
@@ -303,9 +305,6 @@
 
     own0 = dosage
     covariates1 = from_partner(covariates)
-    reached = reach[lax.axis_index("variant")]
-    lanes = jnp.arange(width, dtype=jnp.int32) - place * (width // parts)
-    marks = jnp.stack([lanes, jnp.full((width,), reached, jnp.int32)])
     message = local_sums(dosage, covariates, padded, parts)
     sent = own0
     own1 = from_partner(sent)
@@ -313,18 +312,19 @@
     sums = exchange(message)
     chunk = sums[:, :, :width].sum(0)
     message = jnp.broadcast_to(chunk[None], (parts,) + chunk.shape)
-    message = after(message, own1, far0, covariates1, marks)
+    message = after(message, own1, far0, covariates1)
     far1 = from_far(after(own1, message))
     cross = exchange(message).reshape(padded, width)
     solved, white = factored(after(sums, message), (covariates, covariates1), padded)
     cross_far = from_far(cross)
-    left, own_rows = own_residual((own0, after(own1, far1)), cross, solved, white)
+    left, own_rows = own_residual((own0, own1), cross, solved, white)
     cross_near = lax.ppermute(cross, both, near_route)
     near = swap(after(for_mate(jnp.stack([own0, own1]), jnp.stack([far0, far1])), left))
     message = tiles(
         (far0, far1), near, cross_far, cross_near, solved, white, left, own_rows, parts
     )
-    return bands(marks, exchange(message), samples, width)
+    reached = reach[lax.axis_index("variant")]
+    return bands(place, reached, exchange(message), samples, width)
 
 
 def solution(mesh):

time: 90.3 us -> 90.2 us (level)
  blocking collectives: 34 us -> 0 us
  waiting for transfers between devices: 19.8 us -> 51 us
  starting transfers between devices: 23.5 us -> 27 us
    all_to_all x1 -> x0, blocking collectives: 34 us -> none  [exchange(): return lax.all_to_all(x, 'sample', 0, 0, tiled=False)]
    all_to_all x2 -> x3, waiting for transfers between devices: 13.7 us -> 45.4 us  [exchange(): return lax.all_to_all(x, 'sample', 0, 0, tiled=False)]
    all_to_all x2 -> x3, starting transfers between devices: 16.7 us -> 20.4 us  [exchange(): return lax.all_to_all(x, 'sample', 0, 0, tiled=False)]
    ppermute x1, waiting for transfers between devices: 1.39 us -> 0.01 us  [shards(): cross_near = lax.ppermute(cross, both, near_route)]
    ppermute x3, starting transfers between devices: 2.83 us -> 1.65 us  [from_far(): return lax.ppermute(x, both, far_route)]
    ppermute x1, starting transfers between devices: 0.08 us -> 1 us  [shards(): cross_near = lax.ppermute(cross, both, near_route)]
  transfers between devices with their start and end apart: 9 -> 10, of which waited for: 4 -> 4; matrix products, arithmetic and copies ran while one was open for 2% -> 1% of each run, Pallas kernels for 5% -> 6%
where the time goes in v8:
time: 90.2 us; the launch traced here: 89.9 us
  waiting for transfers between devices  51 us (57%)
  starting transfers between devices  27 us (30%)
  Pallas kernels  9.6 us (11%)
  local copies, waits for them, and re-layouts  1.95 us (2%)
    all_to_all x3, waiting for transfers between devices, exchange(): return lax.all_to_all(x, 'sample', 0, 0, tiled=False)  45.4 us
    all_to_all x3, starting transfers between devices, exchange(): return lax.all_to_all(x, 'sample', 0, 0, tiled=False)  20.4 us
    ppermute x3, waiting for transfers between devices, from_far(): return lax.ppermute(x, both, far_route)  5.53 us
    ppermute x2, starting transfers between devices, from_partner(): return lax.ppermute(x, 'sample', partner_route)  3.84 us
    pallas_call x1, Pallas kernels, tiles(): pl.pallas_call(tiles_kernel, out_shape=jax.ShapeDtypeStruct((parts, 2 * t...  3.16 us
    pallas_call x1, Pallas kernels, factored(): pl.pallas_call(functools.partial(factor_kernel, count + 1), out_shape=(ja...  2.76 us
    pallas_call x1, Pallas kernels, local_sums(): pl.pallas_call(sums_kernel, out_shape=jax.ShapeDtypeStruct((parts, padded...  2.09 us
  transfers between devices with their start and end apart: 10, of which 4 were waited for; matrix products, arithmetic and copies ran while one was open for 1% of the time, Pallas kernels for 6%

profile of v8, /device:TPU:6, one launch (start us, length us, event | category | flops | bytes accessed | tf_op | source)
XLA Modules:
  0.0 89.9 jit_solution(13370843269770329469)
XLA Ops:
  0.0 0.0 copy-start.1
  0.0 1.9 %collective-permute-start.1 = (bf16[512,512]{1,0:T(8,128)(2,1)}, bf16[512,512]{1,0:T(8,128)(2,1)S(1)}, u32[]{:S(2)}, u32[]{:S(2)}) collective-permute-start(bf16[512,512]{1,0:T(8,128)(2,1)} %own0.1), channel_id=1, source_target_pairs={{0,16},{16,0},{32,48},{48,32},{64,80},{80,64},{96,112},{112,96},{1... | collective-permute-start | bytes 1572872 | tf_op jit(solution)/shard_map/ppermute | solution.py:292
  1.9 0.8 collective-permute-start
  2.7 2.1 %local_sums.1 = f32[16,2,1024]{2,1,0:T(2,128)} custom-call(bf16[512,512]{1,0:T(8,128)(2,1)} %own0.1, f32[30,512]{1,0:T(8,128)} %cov0.1), custom_call_target="tpu_custom_call" | custom-call | tf_op jit(solution)/shard_map/local_sums/pallas_call | solution.py:57
  4.8 10.3 %all-to-all-start = ((f32[16,2,1024]{2,1,0:T(2,128)}), f32[16,2,1024]{2,1,0:T(2,128)S(1)}, u32[]{:S(2)}, u32[]{:S(2)}) async-start(f32[16,2,1024]{2,1,0:T(2,128)} %local_sums.1), calls=%async_computation | async-start | bytes 262144 | tf_op jit(solution)/shard_map/all_to_all | solution.py:266
  15.1 1.9 %collective-permute-start.2 = (f32[30,512]{1,0:T(8,128)}, f32[30,512]{1,0:T(8,128)S(1)}, u32[]{:S(2)}, u32[]{:S(2)}) collective-permute-start(f32[30,512]{1,0:T(8,128)} %cov0.1), channel_id=1, source_target_pairs={{0,16},{16,0},{32,48},{48,32},{64,80},{80,64},{96,112},{112,96},{1... | collective-permute-start | bytes 184328 | tf_op jit(solution)/shard_map/ppermute | solution.py:292
  17.1 8.4 %all-to-all-done.sums_ref = f32[16,2,1024]{2,1,0:T(2,128)S(1)} async-done(((f32[16,2,1024]{2,1,0:T(2,128)}), f32[16,2,1024]{2,1,0:T(2,128)S(1)}, u32[]{:S(2)}, u32[]{:S(2)}) %all-to-all-start) | async-done | bytes 131104 | tf_op jit(solution)/shard_map/all_to_all | solution.py:266
  25.5 0.0 collective-permute-done.2.cov1
  25.5 0.0 collective-permute-done.1.own1
  25.5 0.0 collective-permute-done.far0
  25.5 0.6 broadcast_in_dim.2
  26.2 0.7 collective-permute-start.3
  26.9 6.4 %all-to-all-start.1 = ((f32[16,2,512]{2,1,0:T(2,128)}), f32[16,2,512]{2,1,0:T(2,128)S(1)}, u32[]{:S(2)}, u32[]{:S(2)}) async-start(f32[16,2,512]{2,1,0:T(2,128)} %broadcast_in_dim.2), calls=%async_computation.1 | async-start | bytes 131072 | tf_op jit(solution)/shard_map/all_to_all | solution.py:266
  33.3 0.0 copy-done.1
  33.3 0.0 copy-start
  33.3 2.8 %factored.1 = (f32[32,32]{1,0:T(8,128)S(1)}, bf16[192,1024]{1,0:T(8,128)(2,1)S(1)}) custom-call(f32[16,2,1024]{2,1,0:T(2,128)S(1)} %all-to-all-done.sums_ref, f32[30,512]{1,0:T(8,128)S(1)} %copy-done.1, f32[30,512]{1,0:T(8,128)S(1)} %collective-permute-done.2.cov1), custom_call_target="tpu_custom_call" | custom-call | flops 3000000000 | bytes 10000000 | tf_op jit(solution)/shard_map/factored/pallas_call | solution.py:171
  36.1 7.2 %all-to-all-done.1 = f32[16,2,512]{2,1,0:T(2,128)S(1)} async-done(((f32[16,2,512]{2,1,0:T(2,128)}), f32[16,2,512]{2,1,0:T(2,128)S(1)}, u32[]{:S(2)}, u32[]{:S(2)}) %all-to-all-start.1) | async-done | bytes 65568 | tf_op jit(solution)/shard_map/all_to_all | solution.py:266
  43.4 0.0 copy-done
  43.4 0.7 own_residual.1
  44.1 0.0 collective-permute-done.3.far1
  44.1 0.2 maximum_select_fusion
  44.3 0.1 collective-permute-start.4
  44.4 0.1 collective-permute-start.5
  44.5 1.0 %collective-permute-start.6 = (f32[32,512]{1,0:T(8,128)S(1)}, f32[32,512]{1,0:T(8,128)S(1)}, u32[]{:S(2)}, u32[]{:S(2)}) collective-permute-start(f32[32,512]{1,0:T(8,128)S(1)} %reshape.11.cross), channel_id=1, source_target_pairs={{1,0},{2,1},{3,2},{4,3},{5,4},{6,5},{7,6},{8,7},{9,8},{10,9},{11,1... | collective-permute-start | bytes 196616 | tf_op jit(solution)/shard_map/ppermute | solution.py:321
  45.5 5.5 %collective-permute-done.5.cross_far = f32[32,512]{1,0:T(8,128)S(1)} collective-permute-done((f32[32,512]{1,0:T(8,128)S(1)}, f32[32,512]{1,0:T(8,128)S(1)}, u32[]{:S(2)}, u32[]{:S(2)}) %collective-permute-start.5) | collective-permute-done | bytes 65568 | tf_op jit(solution)/shard_map/ppermute | solution.py:295
  51.0 0.0 collective-permute-done.6.cross_near
  51.0 0.0 collective-permute-done.4.near
  51.0 3.2 %tiles.1 = bf16[16,272,128]{2,1,0:T(8,128)(2,1)} custom-call(bf16[512,512]{1,0:T(8,128)(2,1)S(1)} %collective-permute-done.far0, bf16[512,512]{1,0:T(8,128)(2,1)S(1)} %collective-permute-done.3.far1, bf16[2,512,512]{2,1,0:T(8,128)(2,1)S(1)} %collective-permute-done.4.near, f32[32,512]{1,0:T(8,128)S(1)} %collective-permute-done.5.cross_far, ...), custom_call_target="tpu_custom_call" | custom-call | flops 2000000000 | bytes 6000000 | tf_op jit(solution)/shard_map/tiles/pallas_call | solution.py:203
  54.2 0.0 copy-start.2
  54.2 3.7 %all-to-all-start.2 = ((bf16[16,272,128]{2,1,0:T(8,128)(2,1)}), bf16[16,272,128]{2,1,0:T(8,128)(2,1)S(1)}, u32[]{:S(2)}, u32[]{:S(2)}) async-start(bf16[16,272,128]{2,1,0:T(8,128)(2,1)} %tiles.1), calls=%async_computation.2 | async-start | bytes 2228224 | tf_op jit(solution)/shard_map/all_to_all | solution.py:266
  57.9 0.0 copy-done.2
  57.9 0.6 dynamic_slice.3
  58.5 0.6 stack.22.marks_ref
  59.2 29.8 %all-to-all-done.2.arrived_ref = bf16[16,272,128]{2,1,0:T(8,128)(2,1)S(1)} async-done(((bf16[16,272,128]{2,1,0:T(8,128)(2,1)}), bf16[16,272,128]{2,1,0:T(8,128)(2,1)S(1)}, u32[]{:S(2)}, u32[]{:S(2)}) %all-to-all-start.2) | async-done | bytes 1114144 | tf_op jit(solution)/shard_map/all_to_all | solution.py:266
  89.0 0.9 bands.1
  (3 shorter events, 0.1 us)
Async XLA Ops:
  0.0 33.3 %copy-start.1 = (f32[30,512]{1,0:T(8,128)S(1)}, f32[30,512]{1,0:T(8,128)}, u32[]{:S(2)}) copy-start(f32[30,512]{1,0:T(8,128)} %cov0.1) | copy-start | bytes 184324
  0.0 25.5 %collective-permute-start.1 = (bf16[512,512]{1,0:T(8,128)(2,1)}, bf16[512,512]{1,0:T(8,128)(2,1)S(1)}, u32[]{:S(2)}, u32[]{:S(2)}) collective-permute-start(bf16[512,512]{1,0:T(8,128)(2,1)} %own0.1), channel_id=1, source_target_pairs={{0,16},{16,0},{32,48},{48,32},{64,80},{80,64},{96,112},{112,96},{1... | collective-permute-start | bytes 1572872 | tf_op jit(solution)/shard_map/ppermute | solution.py:292
  1.9 23.6 %collective-permute-start = (bf16[512,512]{1,0:T(8,128)(2,1)}, bf16[512,512]{1,0:T(8,128)(2,1)S(1)}, u32[]{:S(2)}, u32[]{:S(2)}) collective-permute-start(bf16[512,512]{1,0:T(8,128)(2,1)} %own0.1), channel_id=1, source_target_pairs={{2,0},{3,1},{4,2},{5,3},{6,4},{7,5},{8,6},{9,7},{10,8},{11,9},{12,... | collective-permute-start | bytes 1572872 | tf_op jit(solution)/shard_map/ppermute | solution.py:295
  4.8 20.6 %all-to-all-start = ((f32[16,2,1024]{2,1,0:T(2,128)}), f32[16,2,1024]{2,1,0:T(2,128)S(1)}, u32[]{:S(2)}, u32[]{:S(2)}) async-start(f32[16,2,1024]{2,1,0:T(2,128)} %local_sums.1), calls=%async_computation | async-start | bytes 262144 | tf_op jit(solution)/shard_map/all_to_all | solution.py:266
  15.1 10.3 %collective-permute-start.2 = (f32[30,512]{1,0:T(8,128)}, f32[30,512]{1,0:T(8,128)S(1)}, u32[]{:S(2)}, u32[]{:S(2)}) collective-permute-start(f32[30,512]{1,0:T(8,128)} %cov0.1), channel_id=1, source_target_pairs={{0,16},{16,0},{32,48},{48,32},{64,80},{80,64},{96,112},{112,96},{1... | collective-permute-start | bytes 184328 | tf_op jit(solution)/shard_map/ppermute | solution.py:292
  26.2 17.9 %collective-permute-start.3 = (bf16[512,512]{1,0:T(8,128)(2,1)S(1)}, bf16[512,512]{1,0:T(8,128)(2,1)S(1)}, u32[]{:S(2)}, u32[]{:S(2)}) collective-permute-start(bf16[512,512]{1,0:T(8,128)(2,1)S(1)} %collective-permute-done.1.own1), channel_id=1, source_target_pairs={{2,0},{3,1},{4,2},{5,3},{6,4},{7,5},{8,6},{9,7},{10,8},{11,9},{12,... | collective-permute-start | bytes 1572872 | tf_op jit(solution)/shard_map/ppermute | solution.py:295
  26.9 16.4 %all-to-all-start.1 = ((f32[16,2,512]{2,1,0:T(2,128)}), f32[16,2,512]{2,1,0:T(2,128)S(1)}, u32[]{:S(2)}, u32[]{:S(2)}) async-start(f32[16,2,512]{2,1,0:T(2,128)} %broadcast_in_dim.2), calls=%async_computation.1 | async-start | bytes 131072 | tf_op jit(solution)/shard_map/all_to_all | solution.py:266
  33.3 10.1 %copy-start = (bf16[512,512]{1,0:T(8,128)(2,1)S(1)}, bf16[512,512]{1,0:T(8,128)(2,1)}, u32[]{:S(2)}) copy-start(bf16[512,512]{1,0:T(8,128)(2,1)} %own0.1) | copy-start | bytes 1572868
  44.3 6.7 %collective-permute-start.4 = (bf16[2,512,512]{2,1,0:T(8,128)(2,1)S(1)}, bf16[2,512,512]{2,1,0:T(8,128)(2,1)S(1)}, u32[]{:S(2)}, u32[]{:S(2)}) collective-permute-start(bf16[2,512,512]{2,1,0:T(8,128)(2,1)S(1)} %maximum_select_fusion), channel_id=1, source_target_pairs={{0,1},{1,0},{2,3},{3,2},{4,5},{5,4},{6,7},{7,6},{8,9},{9,8},{10,11... | collective-permute-start | bytes 3145736 | tf_op jit(solution)/shard_map/ppermute | solution.py:301
  44.4 6.6 %collective-permute-start.5 = (f32[32,512]{1,0:T(8,128)S(1)}, f32[32,512]{1,0:T(8,128)S(1)}, u32[]{:S(2)}, u32[]{:S(2)}) collective-permute-start(f32[32,512]{1,0:T(8,128)S(1)} %reshape.11.cross), channel_id=1, source_target_pairs={{2,0},{3,1},{4,2},{5,3},{6,4},{7,5},{8,6},{9,7},{10,8},{11,9},{12,... | collective-permute-start | bytes 196616 | tf_op jit(solution)/shard_map/ppermute | solution.py:295
  44.5 6.5 %collective-permute-start.6 = (f32[32,512]{1,0:T(8,128)S(1)}, f32[32,512]{1,0:T(8,128)S(1)}, u32[]{:S(2)}, u32[]{:S(2)}) collective-permute-start(f32[32,512]{1,0:T(8,128)S(1)} %reshape.11.cross), channel_id=1, source_target_pairs={{1,0},{2,1},{3,2},{4,3},{5,4},{6,5},{7,6},{8,7},{9,8},{10,9},{11,1... | collective-permute-start | bytes 196616 | tf_op jit(solution)/shard_map/ppermute | solution.py:321
  54.2 3.7 %copy-start.2 = (s32[16]{0:T(128)S(1)}, s32[16]{0:T(128)}, u32[]{:S(2)}) copy-start(s32[16]{0:T(128)} %param.5) | copy-start | bytes 196
  54.2 34.8 %all-to-all-start.2 = ((bf16[16,272,128]{2,1,0:T(8,128)(2,1)}), bf16[16,272,128]{2,1,0:T(8,128)(2,1)S(1)}, u32[]{:S(2)}, u32[]{:S(2)}) async-start(bf16[16,272,128]{2,1,0:T(8,128)(2,1)} %tiles.1), calls=%async_computation.2 | async-start | bytes 2228224 | tf_op jit(solution)/shard_map/all_to_all | solution.py:266
